TPU v7x, 32 devices: a whole 2x2x4 slice. The times are simulated.
32 devices in a mesh: dp: 16 (over z, x, core), tensor: 2 (over y).
Axes of the slice: x: 2, y: 2, z: 4, core: 2. Of those that a mesh axis runs over, the one named last changes fastest.
Arguments:
- hidden_in: bfloat16 [12288, 2048], P(('dp', 'tensor')), may hold values from -6 to 6
- per_layer_input: bfloat16 [12288, 256], P(('dp', 'tensor')), may hold values from -6 to 6
- out_grad: bfloat16 [12288, 2048], P(('dp', 'tensor')), may hold values from -6 to 6
- adapter_ids: int32 [16], P('dp'), may hold values from 0 to 7
- weight_qkv: bfloat16 [2048, 2, 1536], P('dp', 'tensor'), may hold values from -0.125 to 0.125
- weight_attn_out: bfloat16 [2048, 2048], P('tensor', 'dp'), may hold values from -0.125 to 0.125
- weight_gate_up: bfloat16 [2048, 2, 8192], P('dp', None, 'tensor'), may hold values from -0.125 to 0.125
- weight_down: bfloat16 [8192, 2048], P('tensor', 'dp'), may hold values from -0.0625 to 0.0625
- laurel_left: bfloat16 [2048, 64], P('dp'), may hold values from -0.125 to 0.125
- laurel_right: bfloat16 [64, 2048], P(None, 'dp'), may hold values from -0.75 to 0.75
- per_layer_gate: bfloat16 [2048, 256], P('dp'), may hold values from -0.125 to 0.125
- per_layer_proj: bfloat16 [256, 2048], P(None, 'dp'), may hold values from -0.375 to 0.375
- norm_gains: float32 [6, 2048], replicated, may hold values from 0.1 to 1.9
- head_gains: float32 [2, 256], replicated, may hold values from 0.1 to 1.9
- adapter_qkv_in: bfloat16 [8, 2048, 48], replicated, may hold values from -0.125 to 0.125
- adapter_qkv_out: bfloat16 [8, 16, 2, 1536], P(None, None, 'tensor'), may hold values from -0.75 to 0.75
- adapter_attn_in: bfloat16 [8, 2048, 16], P(None, 'tensor'), may hold values from -0.125 to 0.125
- adapter_attn_out: bfloat16 [8, 16, 2048], replicated, may hold values from -0.75 to 0.75
- adapter_ffn_in: bfloat16 [8, 2048, 32], replicated, may hold values from -0.125 to 0.125
- adapter_ffn_out: bfloat16 [8, 16, 2, 8192], P(None, None, None, 'tensor'), may hold values from -0.75 to 0.75
- adapter_down_in: bfloat16 [8, 8192, 16], P(None, 'tensor'), may hold values from -0.0625 to 0.0625
- adapter_down_out: bfloat16 [8, 16, 2048], replicated, may hold values from -0.75 to 0.75
Outputs:
- layer_out: bfloat16 [12288, 2048], P(('dp', 'tensor'))
- input_grad: float32 [12288, 2048], P(('dp', 'tensor'))
- grad_qkv_in: float32 [8, 2048, 48], P(None, ('dp', 'tensor'))
- grad_qkv_out: float32 [8, 16, 2, 1536], P(None, None, 'tensor')
- grad_attn_in: float32 [8, 2048, 16], P(None, 'tensor')
- grad_attn_out: float32 [8, 16, 2048], P(None, None, ('dp', 'tensor'))
- grad_ffn_in: float32 [8, 2048, 32], P(None, ('dp', 'tensor'))
- grad_ffn_out: float32 [8, 16, 2, 8192], P(None, None, None, 'tensor')
- grad_down_in: float32 [8, 8192, 16], P(None, 'tensor')
- grad_down_out: float32 [8, 16, 2048], P(None, None, ('dp', 'tensor'))
Inputs may be any that keep to these rules, and one draw needn't show every extreme that they name: `adapter_ids`: the adapter that each sequence uses.
All inputs are finite; a program needn't handle non-finite values.
Results may differ from a plain program's by a relative error of at most 0.018.
Values may be sent and summed in bfloat16 or wider, within the bound.
A program may use at most 320 MiB of HBM per device.

v0:
```python
import jax
import jax.numpy as jnp
from jax import lax
from jax.sharding import PartitionSpec as P

HEADS = 8
KV = 2
HD = 256
WIN = 512
BLK = 256
ADAPTER_RANK = 16


NORM_EPSILON = 1e-06
ADAPTER_SCALE = 2.0
RSQRT_TWO = 0.7071067811865476
ROPE_BASE = 10000.0
NEG_BIG = -1e30


def normed(values, gains):
    return (
        values * lax.rsqrt(jnp.mean(values * values, axis=-1, keepdims=True) + NORM_EPSILON) * gains
    )


def norm_back(values, gains, cotangent):
    _, pullback = jax.vjp(lambda inner_value: normed(inner_value, gains), values)
    return pullback(cotangent)[0]


def matrix_multiply(left_side, right_side):
    return jnp.dot(left_side, right_side, preferred_element_type=jnp.float32)


def exact_product(left_side, right_side):
    return jnp.dot(
        left_side.astype(jnp.float32),
        right_side.astype(jnp.float32),
        precision=lax.Precision.HIGHEST,
        preferred_element_type=jnp.float32,
    )


def rotary(values, positions):
    half_dim = values.shape[-1] // 2
    inverse = ROPE_BASE ** (-jnp.arange(half_dim, dtype=jnp.float32) / half_dim)
    angles = positions[:, None] * inverse[None, :]
    angles = angles.reshape((positions.shape[0],) + (1,) * (values.ndim - 2) + (half_dim,))
    cosines = jnp.cos(angles)
    sinusoid = jnp.sin(angles)
    leading = values[..., :half_dim]
    trailing = values[..., half_dim:]
    return jnp.concatenate(
        [leading * cosines - trailing * sinusoid, trailing * cosines + leading * sinusoid], axis=-1
    )


def window_mask(length):
    blocks = jnp.arange(length) // BLK
    distance = blocks[:, None] - blocks[None, :]
    return (distance >= 0) & (distance < WIN // BLK)


def gelu_tanh(values):
    return jax.nn.gelu(values, approximate=True)


def on_device(
    hidden_in,
    per_layer_input,
    out_grad,
    adapter_ids,
    weight_qkv,
    weight_attn_out,
    weight_gate_up,
    weight_down,
    laurel_left,
    laurel_right,
    per_layer_gate,
    per_layer_proj,
    norm_gains,
    head_gains,
    adapter_qkv_in,
    adapter_qkv_out,
    adapter_attn_in,
    adapter_attn_out,
    adapter_ffn_in,
    adapter_ffn_out,
    adapter_down_in,
    adapter_down_out,
):
    rows_here = hidden_in.shape[0]
    model_width = hidden_in.shape[1]
    length = rows_here * lax.axis_size("tensor")
    per_group = HEADS // KV
    q_width = per_group * HD
    score_scale = HD ** (-0.5)
    selected_adapter = adapter_ids[0]
    positions = jnp.arange(length, dtype=jnp.float32)
    allowed = window_mask(length)[None]
    ple_float = per_layer_input.astype(jnp.float32)
    bounds = ((0, q_width), (q_width, q_width + HD), (q_width + HD, q_width + 2 * HD))
    x_float = hidden_in.astype(jnp.float32)
    x_norm = normed(x_float, norm_gains[0])
    h_local = x_norm.astype(jnp.bfloat16)
    query_key_value_combined, attention_combined, left_full, right_full = (
        lax.all_gather(weight_qkv, "dp", axis=0, tiled=True),
        lax.all_gather(weight_attn_out, "dp", axis=1, tiled=True),
        lax.all_gather(laurel_left, "dp", axis=0, tiled=True),
        lax.all_gather(laurel_right, "dp", axis=1, tiled=True),
    )
    query_key_value_combined = query_key_value_combined.reshape(model_width, -1)
    hidden_everything = lax.all_gather(h_local, "tensor", axis=0, tiled=True)
    qkv_in = adapter_qkv_in[selected_adapter]
    qkv_out = adapter_qkv_out[selected_adapter].reshape(ADAPTER_RANK, -1).astype(jnp.float32)
    u_qkv = matrix_multiply(hidden_everything, qkv_in)
    adapter_apply = jnp.concatenate(
        [
            exact_product(
                u_qkv[:, member * ADAPTER_RANK : (member + 1) * ADAPTER_RANK],
                qkv_out[:, column_from:column_to],
            )
            for member, (column_from, column_to) in enumerate(bounds)
        ],
        axis=1,
    )
    query_key_value_unrotated = (
        matrix_multiply(hidden_everything, query_key_value_combined) + ADAPTER_SCALE * adapter_apply
    )
    q_raw = query_key_value_unrotated[:, :q_width].reshape(length, per_group, HD)
    k_raw = query_key_value_unrotated[:, q_width : q_width + HD]

    def rotate_both(query_in, key_in):
        return (
            rotary(normed(query_in, head_gains[0]), positions),
            rotary(normed(key_in, head_gains[1]), positions),
        )

    q_rot, k_rot = rotate_both(q_raw, k_raw)
    queries = q_rot.astype(jnp.bfloat16)
    keys_low = k_rot.astype(jnp.bfloat16)
    values_low = query_key_value_unrotated[:, q_width + HD :].astype(jnp.bfloat16)
    scores = (
        jnp.einsum("lqd,md->qlm", queries, keys_low, preferred_element_type=jnp.float32)
        * score_scale
    )
    scores = jnp.where(allowed, scores, NEG_BIG)
    row_max = jnp.max(scores, axis=-1, keepdims=True)
    shifted = jnp.exp(scores - row_max)
    row_sum = jnp.sum(shifted, axis=-1, keepdims=True)
    attn_probs = shifted / row_sum
    log_total = row_max + jnp.log(row_sum)
    probs_low = attn_probs.astype(jnp.bfloat16)
    context_rows = (
        jnp.einsum("qlm,md->lqd", probs_low, values_low, preferred_element_type=jnp.float32)
        .reshape(length, q_width)
        .astype(jnp.bfloat16)
    )
    attn_in = adapter_attn_in[selected_adapter]
    attention_output_float = adapter_attn_out[selected_adapter].astype(jnp.float32)
    attention_update = matrix_multiply(context_rows, attn_in)
    attention_portion = matrix_multiply(
        context_rows, attention_combined
    ) + ADAPTER_SCALE * exact_product(attention_update, attention_output_float)
    attention_projected = lax.psum_scatter(
        attention_portion, "tensor", scatter_dimension=0, tiled=True
    )
    laurel_low = matrix_multiply(h_local, left_full).astype(jnp.bfloat16)
    laurel_wide = matrix_multiply(laurel_low, right_full)
    laurel_out = x_norm + normed(laurel_wide, norm_gains[2])
    combined = (x_float + normed(attention_projected, norm_gains[1]) + laurel_out) * RSQRT_TWO
    h2_local = normed(combined, norm_gains[3]).astype(jnp.bfloat16)
    gate_full, down_combined, pgate_full, pproj_full = (
        lax.all_gather(weight_gate_up, "dp", axis=0, tiled=True),
        lax.all_gather(weight_down, "dp", axis=1, tiled=True),
        lax.all_gather(per_layer_gate, "dp", axis=0, tiled=True),
        lax.all_gather(per_layer_proj, "dp", axis=1, tiled=True),
    )
    gate_full = gate_full.reshape(model_width, -1)
    hidden_unit_count = down_combined.shape[0]
    h2_all = lax.all_gather(h2_local, "tensor", axis=0, tiled=True)
    ffn_in = adapter_ffn_in[selected_adapter]
    feed_output = adapter_ffn_out[selected_adapter].astype(jnp.float32)
    feed_update = matrix_multiply(h2_all, ffn_in)
    gate_up_output = matrix_multiply(h2_all, gate_full)
    gate_preactivation = gate_up_output[:, :hidden_unit_count] + ADAPTER_SCALE * exact_product(
        feed_update[:, :ADAPTER_RANK], feed_output[:, 0]
    )
    up_preactivation = gate_up_output[:, hidden_unit_count:] + ADAPTER_SCALE * exact_product(
        feed_update[:, ADAPTER_RANK:], feed_output[:, 1]
    )
    hidden_state = (gelu_tanh(gate_preactivation) * up_preactivation).astype(jnp.bfloat16)
    down_in = adapter_down_in[selected_adapter]
    down_output = adapter_down_out[selected_adapter].astype(jnp.float32)
    down_update = matrix_multiply(hidden_state, down_in)
    feed_portion = matrix_multiply(hidden_state, down_combined) + ADAPTER_SCALE * exact_product(
        down_update, down_output
    )
    feed_projected = lax.psum_scatter(feed_portion, "tensor", scatter_dimension=0, tiled=True)
    y_first = combined + normed(feed_projected, norm_gains[4])
    ple_pre = matrix_multiply(y_first.astype(jnp.bfloat16), pgate_full)
    ple_hidden = (gelu_tanh(ple_pre) * ple_float).astype(jnp.bfloat16)
    ple_wide = matrix_multiply(ple_hidden, pproj_full)
    layer_out = (y_first + normed(ple_wide, norm_gains[5])).astype(jnp.bfloat16)
    gate_full, down_combined, pgate_full, pproj_full = (
        lax.all_gather(weight_gate_up, "dp", axis=0, tiled=True),
        lax.all_gather(weight_down, "dp", axis=1, tiled=True),
        lax.all_gather(per_layer_gate, "dp", axis=0, tiled=True),
        lax.all_gather(per_layer_proj, "dp", axis=1, tiled=True),
    )
    gate_full = gate_full.reshape(model_width, -1)
    cotangent = out_grad.astype(jnp.float32)
    d_wide = norm_back(ple_wide, norm_gains[5], cotangent).astype(jnp.bfloat16)
    d_ple_hidden = matrix_multiply(d_wide, pproj_full.T)
    _, pullback = jax.vjp(lambda pre_value: gelu_tanh(pre_value) * ple_float, ple_pre)
    d_pre = pullback(d_ple_hidden)[0].astype(jnp.bfloat16)
    d_first = cotangent + matrix_multiply(d_pre, pgate_full.T)
    d_ffn = norm_back(feed_projected, norm_gains[4], d_first).astype(jnp.bfloat16)
    feed_gradient_total = lax.all_gather(d_ffn, "tensor", axis=0, tiled=True)
    down_update_gradient = ADAPTER_SCALE * exact_product(feed_gradient_total, down_output.T)
    d_hidden = matrix_multiply(feed_gradient_total, down_combined.T) + exact_product(
        down_update_gradient, down_in.T
    )
    down_output_gradient_local = ADAPTER_SCALE * exact_product(down_update.T, feed_gradient_total)
    grad_down_in_here = exact_product(hidden_state.T, down_update_gradient)
    _, pullback = jax.vjp(
        lambda gate_value, up_value: gelu_tanh(gate_value) * up_value,
        gate_preactivation,
        up_preactivation,
    )
    d_gate, d_up = pullback(d_hidden)
    d_gate = d_gate.astype(jnp.bfloat16)
    d_up = d_up.astype(jnp.bfloat16)
    feed_update_gradient = ADAPTER_SCALE * jnp.concatenate(
        [exact_product(d_gate, feed_output[:, 0].T), exact_product(d_up, feed_output[:, 1].T)],
        axis=1,
    )
    d_h2_part = matrix_multiply(
        jnp.concatenate([d_gate, d_up], axis=1), gate_full.T
    ) + exact_product(feed_update_gradient, ffn_in.T)
    feed_output_gradient_local = ADAPTER_SCALE * jnp.stack(
        [
            exact_product(feed_update[:, :ADAPTER_RANK].T, d_gate),
            exact_product(feed_update[:, ADAPTER_RANK:].T, d_up),
        ],
        axis=1,
    )
    grad_ffn_in_here = exact_product(h2_all.T, feed_update_gradient)
    d_h2 = lax.psum_scatter(
        d_h2_part.astype(jnp.bfloat16), "tensor", scatter_dimension=0, tiled=True
    ).astype(jnp.float32)
    d_combined = d_first + norm_back(combined, norm_gains[3], d_h2)
    d_branch = d_combined * RSQRT_TWO
    query_key_value_combined, attention_combined, left_full, right_full = (
        lax.all_gather(weight_qkv, "dp", axis=0, tiled=True),
        lax.all_gather(weight_attn_out, "dp", axis=1, tiled=True),
        lax.all_gather(laurel_left, "dp", axis=0, tiled=True),
        lax.all_gather(laurel_right, "dp", axis=1, tiled=True),
    )
    query_key_value_combined = query_key_value_combined.reshape(model_width, -1)
    d_laurel_wide = norm_back(laurel_wide, norm_gains[2], d_branch).astype(jnp.bfloat16)
    d_laurel_low = matrix_multiply(d_laurel_wide, right_full.T).astype(jnp.bfloat16)
    d_norm = d_branch + matrix_multiply(d_laurel_low, left_full.T)
    d_attn = norm_back(attention_projected, norm_gains[1], d_branch).astype(jnp.bfloat16)
    attention_gradient_total = lax.all_gather(d_attn, "tensor", axis=0, tiled=True)
    attention_update_gradient = ADAPTER_SCALE * exact_product(
        attention_gradient_total, attention_output_float.T
    )
    d_context = (
        matrix_multiply(attention_gradient_total, attention_combined.T)
        + exact_product(attention_update_gradient, attn_in.T)
    ).astype(jnp.bfloat16)
    attention_output_gradient_local = ADAPTER_SCALE * exact_product(
        attention_update.T, attention_gradient_total
    )
    grad_attn_in_here = exact_product(context_rows.T, attention_update_gradient)
    d_context = d_context.reshape(length, per_group, HD)
    scores = (
        jnp.einsum("lqd,md->qlm", queries, keys_low, preferred_element_type=jnp.float32)
        * score_scale
    )
    scores = jnp.where(allowed, scores, NEG_BIG)
    attn_probs = jnp.exp(scores - log_total)
    d_probs = jnp.einsum("lqd,md->qlm", d_context, values_low, preferred_element_type=jnp.float32)
    row_dot = jnp.sum(attn_probs * d_probs, axis=-1, keepdims=True)
    d_scores = (attn_probs * (d_probs - row_dot)).astype(jnp.bfloat16)
    d_queries = (
        jnp.einsum("qlm,md->lqd", d_scores, keys_low, preferred_element_type=jnp.float32)
        * score_scale
    )
    d_keys = (
        jnp.einsum("qlm,lqd->md", d_scores, queries, preferred_element_type=jnp.float32)
        * score_scale
    )
    d_values = jnp.einsum(
        "qlm,lqd->md",
        attn_probs.astype(jnp.bfloat16),
        d_context,
        preferred_element_type=jnp.float32,
    )
    _, pullback = jax.vjp(rotate_both, q_raw, k_raw)
    d_q_raw, d_k_raw = pullback((d_queries, d_keys))
    d_raw = jnp.concatenate([d_q_raw.reshape(length, q_width), d_k_raw, d_values], axis=1).astype(
        jnp.bfloat16
    )
    query_key_value_update_gradient = ADAPTER_SCALE * jnp.concatenate(
        [
            exact_product(d_raw[:, column_from:column_to], qkv_out[:, column_from:column_to].T)
            for column_from, column_to in bounds
        ],
        axis=1,
    )
    query_key_value_output_gradient_local = ADAPTER_SCALE * jnp.concatenate(
        [
            exact_product(
                u_qkv[:, member * ADAPTER_RANK : (member + 1) * ADAPTER_RANK].T,
                d_raw[:, column_from:column_to],
            )
            for member, (column_from, column_to) in enumerate(bounds)
        ],
        axis=1,
    )
    query_key_value_output_gradient_local = query_key_value_output_gradient_local.reshape(
        ADAPTER_RANK, 1, -1
    )
    grad_qkv_in_here = exact_product(hidden_everything.T, query_key_value_update_gradient)
    d_h_part = matrix_multiply(d_raw, query_key_value_combined.T) + exact_product(
        query_key_value_update_gradient, qkv_in.T
    )
    d_h = lax.psum_scatter(
        d_h_part.astype(jnp.bfloat16), "tensor", scatter_dimension=0, tiled=True
    ).astype(jnp.float32)
    d_norm = d_norm + d_h
    input_grad = d_branch + norm_back(x_float, norm_gains[0], d_norm)
    onehot = (jnp.arange(adapter_qkv_in.shape[0]) == selected_adapter).astype(jnp.float32)

    def spread(grad_here):
        return onehot.reshape((-1,) + (1,) * grad_here.ndim) * grad_here[None]

    shared = (
        lax.psum_scatter(
            spread(grad_qkv_in_here), ("dp", "tensor"), scatter_dimension=1, tiled=True
        ),
        lax.psum_scatter(
            spread(grad_ffn_in_here), ("dp", "tensor"), scatter_dimension=1, tiled=True
        ),
        lax.psum_scatter(
            spread(attention_output_gradient_local),
            ("dp", "tensor"),
            scatter_dimension=2,
            tiled=True,
        ),
        lax.psum_scatter(
            spread(down_output_gradient_local), ("dp", "tensor"), scatter_dimension=2, tiled=True
        ),
    )
    dp_only = lax.psum(
        (
            spread(query_key_value_output_gradient_local),
            spread(feed_output_gradient_local),
            spread(grad_attn_in_here),
            spread(grad_down_in_here),
        ),
        "dp",
    )
    return (
        layer_out,
        input_grad,
        shared[0],
        dp_only[0],
        dp_only[2],
        shared[2],
        shared[1],
        dp_only[1],
        dp_only[3],
        shared[3],
    )


def solution(mesh):
    in_specs = (
        P(("dp", "tensor"), None),
        P(("dp", "tensor"), None),
        P(("dp", "tensor"), None),
        P("dp"),
        P("dp", "tensor", None),
        P("tensor", "dp"),
        P("dp", None, "tensor"),
        P("tensor", "dp"),
        P("dp", None),
        P(None, "dp"),
        P("dp", None),
        P(None, "dp"),
        P(),
        P(),
        P(),
        P(None, None, "tensor", None),
        P(None, "tensor", None),
        P(),
        P(),
        P(None, None, None, "tensor"),
        P(None, "tensor", None),
        P(),
    )
    out_specs = (
        P(("dp", "tensor"), None),
        P(("dp", "tensor"), None),
        P(None, ("dp", "tensor"), None),
        P(None, None, "tensor", None),
        P(None, "tensor", None),
        P(None, None, ("dp", "tensor")),
        P(None, ("dp", "tensor"), None),
        P(None, None, None, "tensor"),
        P(None, "tensor", None),
        P(None, None, ("dp", "tensor")),
    )
    return jax.shard_map(
        on_device, mesh=mesh, in_specs=in_specs, out_specs=out_specs, check_vma=False
    )
```

profile of v0, /device:TPU:0, one launch (start us, length us, event | category | flops | bytes accessed | tf_op | source)
XLA Modules:
  0.0 1792.9 jit_solution(14510706811313298158)
XLA Ops:
  19.3 43.1 %all-gather.11.cloned.1.call-done = bf16[768,2048]{1,0:T(8,128)(2,1)} async-done(((bf16[384,2048]{1,0:T(8,128)(2,1)}), bf16[768,2048]{1,0:T(8,128)(2,1)}) %all-gather.11.cloned.1.call-update) | async-done | bytes 3145744 | tf_op jit(solution)/shard_map/all_gather | solution.py:114
  70.3 56.2 %all-gather.13.cloned.1.call-done = bf16[2048,1,1536]{2,0,1:T(8,128)(2,1)} async-done(((bf16[128,1,1536]{2,0,1:T(8,128)(2,1)}), bf16[2048,1,1536]{2,0,1:T(8,128)(2,1)}) %all-gather.13.cloned.1.call-update) | async-done | bytes 6291472 | tf_op jit(solution)/shard_map/all_gather | solution.py:108
  193.1 19.3 %all_gather.47 = bf16[2048,64]{0,1:T(8,128)(2,1)S(1)} all-gather(bf16[128,64]{0,1:T(8,128)(2,1)S(1)} %copy-done.109), channel_id=1, replica_groups=mesh['dp'=16,'tensor'=2] {'dp'}, dimensions={0}, use_global_device_ids=true | all-gather | bytes 278528 | tf_op jit(solution)/shard_map/all_gather | solution.py:110
  235.2 32.5 %reduce-scatter.17.cloned.1.call-done = f32[384,2048]{1,0:T(8,128)} async-done(((f32[768,2048]{1,0:T(8,128)}), f32[384,2048]{1,0:T(8,128)}) %reduce-scatter.17.cloned.1.call-update) | async-done | bytes 3145744 | tf_op jit(solution)/shard_map/reduce_scatter | solution.py:166
  279.7 43.3 %all-gather.17.cloned.1.call-done = bf16[768,2048]{1,0:T(8,128)(2,1)} async-done(((bf16[384,2048]{1,0:T(8,128)(2,1)}), bf16[768,2048]{1,0:T(8,128)(2,1)}) %all-gather.17.cloned.1.call-update) | async-done | bytes 3145744 | tf_op jit(solution)/shard_map/all_gather | solution.py:182
  325.9 166.8 %all-gather.19.cloned.1.call-done = bf16[2048,2,4096]{2,1,0:T(2,128)(2,1)} async-done(((bf16[128,2,4096]{2,1,0:T(2,128)(2,1)}), bf16[2048,2,4096]{2,1,0:T(2,128)(2,1)}) %all-gather.19.cloned.1.call-update) | async-done | bytes 33554448 | tf_op jit(solution)/shard_map/all_gather | solution.py:175
  492.7 30.1 %copy.161 = bf16[256,8,2,4096]{3,1,2,0:T(8,128)(2,1)} copy(bf16[256,8,2,4096]{3,2,1,0:T(2,128)(2,1)} %bitcast.199) | data formatting | bytes 67108864
  522.8 32.6 %fusion.228 = f32[768,8192]{1,0:T(8,128)} fusion(bf16[768,2048]{1,0:T(8,128)(2,1)S(1)} %copy-done.16, bf16[2048,8192]{1,0:T(8,128)(2,1)} %bitcast.197), kind=kOutput, calls=%fused_computation.326 | convolution fusion | flops 25769803776 | bytes 61865984 | tf_op jit(solution)/shard_map/dot_general | solution.py:33
  566.7 18.8 %multiply_convert_fusion.1 = (bf16[768,4096]{1,0:T(8,128)(2,1)S(1)}, f32[768,4096]{1,0:T(8,128)}) fusion(f32[768,4096]{1,0:T(8,128)} %slice_add_fusion.1, bf16[16,2,4096]{2,0,1:T(8,128)(2,1)S(1)} %bitcast.210, f32[768,32]{0,1:T(8,128)S(1)} %fusion.115, f32[768,8192]{1,0:T(8,128)} %fusion.228), kind=kOutput, calls=%fused_computation.16 | convolution fusion | flops 641728512 | bytes 44220416 | tf_op jit(solution)/shard_map/dot_general | solution.py:37
  594.2 32.1 %all-gather.21.cloned.1.call-done = bf16[4096,2048]{1,0:T(8,128)(2,1)} async-done(((bf16[4096,128]{1,0:T(8,128)(2,1)}), bf16[4096,2048]{1,0:T(8,128)(2,1)}) %all-gather.21.cloned.1.call-update) | async-done | bytes 16777232 | tf_op jit(solution)/shard_map/all_gather | solution.py:176
  626.4 21.2 %multiply_add_fusion = f32[768,2048]{1,0:T(8,128)} fusion(f32[768,2048]{1,0:T(8,128)} %fusion.131, bf16[768,4096]{1,0:T(8,128)(2,1)} %copy-done.11, bf16[4096,2048]{1,0:T(8,128)(2,1)} %all-gather.21.cloned.1.call-done), kind=kOutput, calls=%fused_computation.36 | convolution fusion | flops 12888047616 | bytes 35651584 | tf_op jit(solution)/shard_map/dot_general | solution.py:33
  649.4 72.7 %reduce-scatter.19.cloned.1.call-done = f32[384,2048]{1,0:T(8,128)} async-done(((f32[768,2048]{1,0:T(8,128)}), f32[384,2048]{1,0:T(8,128)}) %reduce-scatter.19.cloned.1.call-update) | async-done | bytes 3145744 | tf_op jit(solution)/shard_map/reduce_scatter | solution.py:200
  724.2 38.0 %all-gather.23.cloned.1.call-done = bf16[2048,256]{1,0:T(8,128)(2,1)} async-done(((bf16[128,256]{1,0:T(8,128)(2,1)}), bf16[2048,256]{1,0:T(8,128)(2,1)}) %all-gather.23.cloned.1.call-update) | async-done | bytes 1048592 | tf_op jit(solution)/shard_map/all_gather | solution.py:177
  765.8 34.2 %all-gather.25.cloned.1.call-done = bf16[256,2048]{1,0:T(8,128)(2,1)} async-done(((bf16[256,128]{1,0:T(8,128)(2,1)}), bf16[256,2048]{1,0:T(8,128)(2,1)}) %all-gather.25.cloned.1.call-update) | async-done | bytes 1048592 | tf_op jit(solution)/shard_map/all_gather | solution.py:178
  818.4 44.5 %all-gather.27.cloned.1.call-done = bf16[768,2048]{1,0:T(8,128)(2,1)} async-done(((bf16[384,2048]{1,0:T(8,128)(2,1)}), bf16[768,2048]{1,0:T(8,128)(2,1)}) %all-gather.27.cloned.1.call-update) | async-done | bytes 3145744 | tf_op jit(solution)/shard_map/all_gather | solution.py:220
  874.9 32.2 %fusion.6 = (bf16[768,4096]{1,0:T(8,128)(2,1)}, bf16[768,4096]{1,0:T(8,128)(2,1)}) fusion(f32[768,4096]{1,0:T(8,128)} %slice_add_fusion.1, f32[768,4096]{1,0:T(8,128)} %get-tuple-element.54, f32[768,4096]{1,0:T(8,128)} %fusion.110, bf16[768,2048]{1,0:T(8,128)(2,1)S(1)} %copy-done.12, bf16[4096,2048]{1,0:T(8,128)(2,1)} %all-gather.21.cloned.1.call-done), kind=kOutput, calls=%fused_computation.8 | convolution fusion | flops 12963545088 | bytes 70254592 | tf_op jit(solution)/shard_map/dot_general | solution.py:33
  911.7 33.9 %fusion.7 = f32[768,2048]{1,0:T(8,128)} fusion(bf16[2048,8192]{1,0:T(8,128)(2,1)} %bitcast.198, bf16[768,4096]{1,0:T(8,128)(2,1)} %get-tuple-element.22, bf16[768,4096]{1,0:T(8,128)(2,1)} %get-tuple-element.21), kind=kOutput, calls=%fused_computation.11 | convolution fusion | flops 25794969600 | bytes 52428800 | tf_op jit(solution)/shard_map/dot_general | solution.py:33
  956.0 42.8 %reduce-scatter.21.cloned.1.call-done = bf16[384,2048]{1,0:T(8,128)(2,1)} async-done(((bf16[768,2048]{1,0:T(8,128)(2,1)}), bf16[384,2048]{1,0:T(8,128)(2,1)}) %reduce-scatter.21.cloned.1.call-update) | async-done | bytes 1572880 | tf_op jit(solution)/shard_map/reduce_scatter | solution.py:250
  1028.5 28.9 %all-gather.29.cloned.1.call-done = bf16[768,2048]{1,0:T(8,128)(2,1)} async-done(((bf16[384,2048]{1,0:T(8,128)(2,1)}), bf16[768,2048]{1,0:T(8,128)(2,1)}) %all-gather.29.cloned.1.call-update) | async-done | bytes 3145744 | tf_op jit(solution)/shard_map/all_gather | solution.py:266
  1207.4 122.5 %reduce-scatter.31.cloned.1.call-done = f32[64,128]{1,0:T(8,128)} async-done(((f32[2048,128]{1,0:T(8,128)}), f32[64,128]{1,0:T(8,128)}) %reduce-scatter.31.cloned.1.call-update) | async-done | bytes 32784
  1333.2 129.7 %reduce-scatter.27.cloned.1.call-done = f32[64,128]{1,0:T(8,128)} async-done(((f32[2048,128]{1,0:T(8,128)}), f32[64,128]{1,0:T(8,128)}) %reduce-scatter.27.cloned.1.call-update) | async-done | bytes 32784
  1466.1 99.5 %reduce-scatter.25.cloned.1.call-done = f32[64,384]{1,0:T(8,128)} async-done(((f32[2048,384]{1,0:T(8,128)}), f32[64,384]{1,0:T(8,128)}) %reduce-scatter.25.cloned.1.call-update) | async-done | bytes 98320
  1569.1 40.9 %reduce-scatter.23.cloned.1.call-done = bf16[384,2048]{1,0:T(8,128)(2,1)} async-done(((bf16[768,2048]{1,0:T(8,128)(2,1)}), bf16[384,2048]{1,0:T(8,128)(2,1)}) %reduce-scatter.23.cloned.1.call-update) | async-done | bytes 1572880 | tf_op jit(solution)/shard_map/reduce_scatter | solution.py:331
  1623.3 152.6 %all-reduce.7.cloned.1.call-done = (f32[8,16,1,1536]{3,2,1,0:T(1,128)}, f32[8,1024,16]{1,2,0:T(8,128)}, f32[8,16,2,4096]{3,2,1,0:T(2,128)}, f32[8,4096,16]{1,2,0:T(8,128)}) async-done(((f32[8,16,1,1536]{3,2,1,0:T(1,128)}, f32[8,1024,16]{1,2,0:T(8,128)}, f32[8,16,2,4096]{3,2,1,0:T(2,128)}, f32[8,4096,16]{1,2,0:T(8,128)}), (f32[8,16,1,1536]{3,2,1,0:T(1,128)}, f32[8,1024,16]{1,2,0:T(8,128)}, ...) | async-done | bytes 7602192 | tf_op jit(solution)/shard_map/psum | solution.py:358
  (418 shorter events, 408.2 us)
Async XLA Ops:
  7.2 55.1 %all-gather.11.cloned.1.call-start = ((), (), s32[]{:S(2)}) async-start(), calls=%async_computation.8 | async-start | bytes 4718592 | tf_op jit(solution)/shard_map/all_gather | solution.py:114
  14.5 111.9 %all-gather.13.cloned.1.call-start = ((), (), s32[]{:S(2)}) async-start(), calls=%async_computation.9 | async-start | bytes 6684672 | tf_op jit(solution)/shard_map/all_gather | solution.py:108
  15.3 165.2 %all-gather.15.cloned.1.call-start = ((), (), s32[]{:S(2)}) async-start(), calls=%async_computation.10 | async-start | bytes 4456448 | tf_op jit(solution)/shard_map/all_gather | solution.py:109
  16.0 251.7 %reduce-scatter.17.cloned.1.call-start = ((), (), s32[]{:S(2)}) async-start(), calls=%async_computation.11 | async-start | bytes 9437184 | tf_op jit(solution)/shard_map/reduce_scatter | solution.py:166
  192.4 130.6 %all-gather.17.cloned.1.call-start = ((), (), s32[]{:S(2)}) async-start(), calls=%async_computation.12 | async-start | bytes 4718592 | tf_op jit(solution)/shard_map/all_gather | solution.py:182
  277.9 214.8 %all-gather.19.cloned.1.call-start = ((), (), s32[]{:S(2)}) async-start(), calls=%async_computation.13 | async-start | bytes 35651584 | tf_op jit(solution)/shard_map/all_gather | solution.py:175
  278.5 347.9 %all-gather.21.cloned.1.call-start = ((), (), s32[]{:S(2)}) async-start(), calls=%async_computation.14 | async-start | bytes 17825792 | tf_op jit(solution)/shard_map/all_gather | solution.py:176
  279.2 442.8 %reduce-scatter.19.cloned.1.call-start = ((), (), s32[]{:S(2)}) async-start(), calls=%async_computation.15 | async-start | bytes 9437184 | tf_op jit(solution)/shard_map/reduce_scatter | solution.py:200
  647.6 114.6 %all-gather.23.cloned.1.call-start = ((), (), s32[]{:S(2)}) async-start(), calls=%async_computation.16 | async-start | bytes 1114112 | tf_op jit(solution)/shard_map/all_gather | solution.py:177
  648.3 151.6 %all-gather.25.cloned.1.call-start = ((), (), s32[]{:S(2)}) async-start(), calls=%async_computation.17 | async-start | bytes 1114112 | tf_op jit(solution)/shard_map/all_gather | solution.py:178
  648.9 214.0 %all-gather.27.cloned.1.call-start = ((), (), s32[]{:S(2)}) async-start(), calls=%async_computation.18 | async-start | bytes 4718592 | tf_op jit(solution)/shard_map/all_gather | solution.py:220
  818.4 180.5 %reduce-scatter.21.cloned.1.call-start = ((), (), s32[]{:S(2)}) async-start(), calls=%async_computation.19 | async-start | bytes 4718592 | tf_op jit(solution)/shard_map/reduce_scatter | solution.py:250
  955.4 102.0 %all-gather.29.cloned.1.call-start = ((), (), s32[]{:S(2)}) async-start(), calls=%async_computation.20 | async-start | bytes 4718592 | tf_op jit(solution)/shard_map/all_gather | solution.py:266
  1012.3 191.5 %reduce-scatter.29.cloned.1.call-start = ((), (), s32[]{:S(2)}) async-start(), calls=%async_computation.24 | async-start | bytes 2162688
  1027.1 302.8 %reduce-scatter.31.cloned.1.call-start = ((), (), s32[]{:S(2)}) async-start(), calls=%async_computation.25 | async-start | bytes 1081344
  1110.2 352.7 %reduce-scatter.27.cloned.1.call-start = ((), (), s32[]{:S(2)}) async-start(), calls=%async_computation.23 | async-start | bytes 1081344
  1139.0 426.7 %reduce-scatter.25.cloned.1.call-start = ((), (), s32[]{:S(2)}) async-start(), calls=%async_computation.22 | async-start | bytes 3244032
  1164.5 445.6 %reduce-scatter.23.cloned.1.call-start = ((), (), s32[]{:S(2)}) async-start(), calls=%async_computation.21 | async-start | bytes 4718592 | tf_op jit(solution)/shard_map/reduce_scatter | solution.py:331
  1178.7 597.2 %all-reduce.7.cloned.1.call-start = ((), (), s32[]{:S(2)}) async-start(), calls=%async_computation.26 | async-start | bytes 15204352 | tf_op jit(solution)/shard_map/psum | solution.py:358
  1203.7 406.4 %copy-start.9 = (f32[384,2048]{1,0:T(8,128)S(1)}, f32[384,2048]{1,0:T(8,128)}, u32[]{:S(2)}) copy-start(f32[384,2048]{1,0:T(8,128)} %get-tuple-element.50) | copy-start | bytes 9437188
  1203.7 406.4 %copy-start.35 = (bf16[2048,64]{0,1:T(8,128)(2,1)S(1)}, bf16[2048,64]{0,1:T(8,128)(2,1)}, u32[]{:S(2)}) copy-start(bf16[2048,64]{0,1:T(8,128)(2,1)} %copy-done.34) | copy-start | bytes 786436
  1203.7 406.4 %copy-start.67 = (f32[1,2048]{1,0:T(1,128)S(1)}, f32[1,2048]{1,0:T(1,128)}, u32[]{:S(2)}) copy-start(f32[1,2048]{1,0:T(1,128)} %copy-done.66) | copy-start | bytes 24580
  1203.7 406.4 %copy-start.74 = (f32[2048]{0:T(1024)S(1)}, f32[2048]{0:T(1024)}, u32[]{:S(2)}) copy-start(f32[2048]{0:T(1024)} %copy-done.73) | copy-start | bytes 24580
  1203.8 406.4 %copy-start.98 = (f32[384]{0:T(512)S(1)}, f32[384]{0:T(512)}, u32[]{:S(2)}) copy-start(f32[384]{0:T(512)} %copy-done.97) | copy-start | bytes 4612
  (115 other events, 2864.4 us)
Sparse Core Ops, SparseCore 0:
  14.7 47.6 all-gather.10
  64.6 61.8 all-gather.12
  128.7 51.8 all-gather.14
  192.5 75.2 reduce-scatter.16
  278.0 44.9 all-gather.16
  324.5 168.1 all-gather.18
  495.1 131.2 all-gather.20
  647.7 74.3 reduce-scatter.18
  724.2 37.9 all-gather.22
  764.2 35.7 all-gather.24
  818.5 44.4 all-gather.26
  955.5 43.3 reduce-scatter.20
  1012.4 44.9 all-gather.28
  1059.6 136.7 reduce-scatter.28
  1198.5 131.3 reduce-scatter.30
  1332.1 130.7 reduce-scatter.26
  1468.1 97.4 reduce-scatter.24
  1567.7 42.2 reduce-scatter.22
  1616.0 159.8 all-reduce.6
where the time goes:
time: 1800 us; the launch traced here: 1790 us
  waiting for transfers between devices  1200 us (67%)
  matrix products  319 us (18%)
  local copies, waits for them, and re-layouts  132 us (7%)
  other arithmetic  85.4 us (5%)
  blocking collectives  37.6 us (2%)
    unnamed x23, waiting for transfers between devices  356 us
    dot_general x17, matrix products, matrix_multiply(): return jnp.dot(left_side, right_side, preferred_element_type=jnp.float32)  186 us
    all_gather x1, waiting for transfers between devices, on_device(): lax.all_gather(weight_gate_up, 'dp', axis=0, tiled=True)  167 us
    psum x1, waiting for transfers between devices, on_device(): lax.psum((spread(query_key_value_output_gradient_local), spread(feed_outp...  153 us
    unnamed x261, local copies, waits for them, and re-layouts  115 us
    dot_general x29, matrix products, exact_product(): jnp.dot(left_side.astype(jnp.float32), right_side.astype(jnp.float32), pr...  110 us
    reduce_scatter x1, waiting for transfers between devices, on_device(): lax.psum_scatter(feed_portion, 'tensor', scatter_dimension=0, tiled=True)  72.7 us
    all_gather x1, waiting for transfers between devices, on_device(): lax.all_gather(weight_qkv, 'dp', axis=0, tiled=True)  56.2 us
  transfers between devices with their start and end apart: 19, of which 18 were waited for; matrix products, arithmetic and copies ran while one was open for 19% of the time, Pallas kernels for 0%

commit v1 on v0

v1 whole, which is shorter than its diff:
```python
import functools

import jax
import jax.numpy as jnp
from jax import lax
from jax.experimental import pallas as pl
from jax.experimental.pallas import tpu as pltpu
from jax.sharding import PartitionSpec as P

HEADS = 8
KV = 2
HD = 256
WIN = 512
BLK = 256
RANK = 16
UB = 512
FB = 3 * UB

NORM_EPSILON = 1e-06
RSQRT_TWO = 0.7071067811865476
ROPE_BASE = 10000.0
NEG_BIG = -1e30
GELU_A = 0.7978845608028654
GELU_B = 0.044715

F32 = jnp.float32
BF16 = jnp.bfloat16
VMEM_LIMIT = 58 * 1024 * 1024


def dot(a, b):
    return lax.dot_general(a, b, (((1,), (0,)), ((), ())), preferred_element_type=F32)


def dot_nt(a, b):
    return lax.dot_general(a, b, (((1,), (1,)), ((), ())), preferred_element_type=F32)


def dot_tn(a, b):
    return lax.dot_general(a, b, (((0,), (0,)), ((), ())), preferred_element_type=F32)


def inv_rms(v):
    return lax.rsqrt(jnp.mean(v * v, axis=-1, keepdims=True) + NORM_EPSILON)


def normed(v, gains):
    return v * inv_rms(v) * gains


def norm_back(v, gains, cotangent):
    r = inv_rms(v)
    gc = gains * cotangent
    return r * gc - v * (r * r * r * jnp.mean(v * gc, axis=-1, keepdims=True))


def gelu_tanh(v):
    return 0.5 * v * (1.0 + jnp.tanh(GELU_A * (v + GELU_B * v * v * v)))


def gelu_both(v):
    v2 = v * v
    th = jnp.tanh(GELU_A * v * (1.0 + GELU_B * v2))
    half = 0.5 * (1.0 + th)
    slope = half + 0.5 * v * (1.0 - th * th) * (GELU_A * (1.0 + 3.0 * GELU_B * v2))
    return v * half, slope


def const_spec(shape):
    return pl.BlockSpec(shape, lambda *_: (0,) * len(shape), pipeline_mode=pl.Buffered(1))


def any_spec():
    return pl.BlockSpec(memory_space=pl.ANY)


def params():
    return pltpu.CompilerParams(vmem_limit_bytes=VMEM_LIMIT)


def pack_blocks(gate_up, down, first, count, rest, cols, name):
    rows = gate_up.shape[0]
    widths = [n for _, n in rest]

    def body(gu_ref, down_ref, *refs):
        out = refs[-1]
        for b in range(count):
            cs = slice(b * UB, (b + 1) * UB)
            out[:, b * FB : b * FB + UB] = gu_ref[:, 0, cs]
            out[:, b * FB + UB : b * FB + 2 * UB] = gu_ref[:, 1, cs]
            out[:, b * FB + 2 * UB : (b + 1) * FB] = down_ref[cs, :].T
        at = count * FB
        for ref, (value, n) in zip(refs[:-1], rest):
            if value.ndim == 3:
                out[:, at : at + n] = ref[:, 0, :]
            elif value.shape[0] == rows and value.shape[1] == n:
                out[:, at : at + n] = ref[...]
            else:
                out[:, at : at + n] = ref[...].T
            at += n

    lo = first * UB
    return pl.pallas_call(
        body,
        grid=(1,),
        in_specs=[
            pl.BlockSpec((pl.Element(rows), pl.Element(2), pl.Element(count * UB)), lambda i: (0, 0, lo)),
            pl.BlockSpec((pl.Element(count * UB), pl.Element(rows)), lambda i: (lo, 0)),
        ]
        + [const_spec(v.shape) for v, _ in rest],
        out_specs=const_spec((rows, count * FB + sum(widths))),
        out_shape=jax.ShapeDtypeStruct((rows, count * FB + sum(widths)), BF16),
        compiler_params=params(),
        name=name,
    )(gate_up, down, *[v for v, _ in rest])


def ffn_fwd(h2, packed, blocks, first, u_low, bgu, ad_t, bd, prev, last):
    rows, width = h2.shape
    units = ad_t.shape[1]
    stream = last is not None
    r = rows // 2 if stream else rows
    rb = last if stream else 0
    half = r // 2
    tile = rows // 2
    sub = 256

    def body(*refs):
        h_ref, w_ref, ul_ref, bgu_ref, ad_ref, bd_ref = refs[:6]
        at = 6
        if prev is not None:
            acc_in, ud_in = refs[6:8]
            at = 10
        outs = refs[at:]
        if stream:
            g_out, u_out, own_out, peer_out, ud_out, acc, ud, hs = outs
        else:
            g_out, u_out, acc_out, ud_out, acc, ud, hs = outs
        j = pl.program_id(0)

        @pl.when(j == 0)
        def _():
            if prev is None:
                acc[...] = jnp.zeros_like(acc)
                ud[...] = jnp.zeros_like(ud)
            else:
                acc[...] = acc_in[...]
                ud[...] = ud_in[...]

        for k in range(r // tile):
            at_rows = slice(k * tile, (k + 1) * tile)
            h = h_ref[at_rows, :]
            ul = ul_ref[at_rows, :]
            for n in range(UB // sub):
                cs = slice(n * sub, (n + 1) * sub)
                us = slice(UB + n * sub, UB + (n + 1) * sub)
                g = dot(h, w_ref[:, cs]) + dot(ul, bgu_ref[:, cs])
                u = dot(h, w_ref[:, us]) + dot(ul, bgu_ref[:, us])
                g_out[at_rows, cs] = g.astype(BF16)
                u_out[at_rows, cs] = u.astype(BF16)
                hs[at_rows, cs] = (gelu_tanh(g) * u).astype(BF16)
            hidden = hs[at_rows, :]
            for c in range(width // 512):
                cc = slice(c * 512, (c + 1) * 512)
                acc[at_rows, cc] += dot_nt(hidden, w_ref[cc, 2 * UB : 3 * UB])
            ud[at_rows, :] += dot_nt(hidden, ad_ref[...])

        @pl.when(j == blocks - 1)
        def _():
            ud_out[...] = ud[...]
            if stream:
                total = acc[...] + dot(ud[...].astype(BF16), bd_ref[...])
                own_out[...] = total[:half]
                peer_out[...] = total[half:].astype(BF16)
            else:
                acc_out[...] = acc[...]

    row_const = lambda n: pl.BlockSpec((r, n), lambda j: (rb, 0), pipeline_mode=pl.Buffered(1))
    in_specs = [
        row_const(width),
        pl.BlockSpec((width, FB), lambda j: (0, j)),
        row_const(2 * RANK),
        pl.BlockSpec((2 * RANK, 2 * UB), lambda j: (0, first + j)),
        pl.BlockSpec((RANK, UB), lambda j: (0, first + j)),
        const_spec((RANK, width)),
    ]
    args = [h2, packed, u_low, bgu, ad_t, bd]
    aliases = {}
    if prev is not None:
        acc_prev, ud_prev, g_prev, u_prev = prev
        in_specs += [row_const(width), row_const(RANK), any_spec(), any_spec()]
        args += [acc_prev, ud_prev, g_prev, u_prev]
        aliases = {8: 0, 9: 1}
    pre_spec = pl.BlockSpec((r, UB), lambda j: (rb, first + j))
    out_specs = [pre_spec, pre_spec]
    shape = jax.ShapeDtypeStruct
    out_shape = [shape((rows, units), BF16)] * 2
    if stream:
        out_specs += [const_spec((half, width)), const_spec((half, width)), const_spec((r, RANK))]
        out_shape += [
            shape((half, width), F32),
            shape((half, width), BF16),
            shape((r, RANK), F32),
        ]
    else:
        out_specs += [const_spec((r, width)), const_spec((r, RANK))]
        out_shape += [shape((r, width), F32), shape((r, RANK), F32)]
    return pl.pallas_call(
        body,
        grid=(blocks,),
        in_specs=in_specs,
        out_specs=out_specs,
        out_shape=out_shape,
        scratch_shapes=[
            pltpu.VMEM((r, width), F32),
            pltpu.VMEM((r, RANK), F32),
            pltpu.VMEM((r, UB), BF16),
        ],
        input_output_aliases=aliases,
        compiler_params=params(),
        cost_estimate=pl.CostEstimate(
            flops=6 * r * width * UB * blocks,
            bytes_accessed=2 * width * FB * blocks + 8 * r * width,
            transcendentals=r * UB * blocks,
        ),
        name="ffn_fwd",
    )(*args)


def ffn_bwd(own, peer, packs, counts, g_pre, u_pre, bgu, ad_t, bd, u_t, a_in_t, rb):
    half, width = own.shape
    r = 2 * half
    units = ad_t.shape[1]
    blocks = units // UB

    def body(
        own_ref, peer_ref, p0, p1, p2, g_ref, u_ref, bgu_ref, ad_ref, bd_ref, ut_ref,
        ain_ref, own_out, peer_out, dbg_out, dbu_out, gad_out, du_out,
        df, acc, wbuf, dd, du, dgu, hs, sem,
    ):
        j = pl.program_id(0)
        slot = lax.rem(j, 2)

        def fetch(step, where):
            base = 0
            for ref, count in zip((p0, p1, p2), counts):
                low = base

                @pl.when((step >= low) & (step < low + count))
                def _(ref=ref, low=low):
                    column = pl.multiple_of((step - low) * FB, FB)
                    pltpu.make_async_copy(
                        ref.at[:, pl.ds(column, FB)], wbuf.at[where], sem.at[where]
                    ).start()

                base += count

        @pl.when(j == 0)
        def _():
            fetch(j, 0)
            df[0:half, :] = own_ref[...]
            df[half:r, :] = peer_ref[...]
            acc[...] = jnp.zeros_like(acc)
            du[...] = jnp.zeros_like(du)
            dd[...] = dot_nt(df[...], bd_ref[...]).astype(BF16)

        @pl.when(j + 1 < blocks)
        def _():
            fetch(j + 1, 1 - slot)

        pltpu.make_async_copy(p0.at[:, pl.ds(0, FB)], wbuf.at[slot], sem.at[slot]).wait()

        sub = 256
        for n in range(UB // sub):
            cs = slice(n * sub, (n + 1) * sub)
            dh = dot(df[...], wbuf[slot, :, 2 * UB + n * sub : 2 * UB + (n + 1) * sub])
            dh += dot(dd[...], ad_ref[:, cs])
            g = g_ref[:, cs].astype(F32)
            u = u_ref[:, cs].astype(F32)
            act, slope = gelu_both(g)
            dgu[:, cs] = (dh * u * slope).astype(BF16)
            dgu[:, UB + n * sub : UB + (n + 1) * sub] = (dh * act).astype(BF16)
            hs[:, cs] = (act * u).astype(BF16)
        d_both = dgu[...]
        for c in range(width // 512):
            cc = slice(c * 512, (c + 1) * 512)
            acc[:, cc] += dot_nt(d_both, wbuf[slot, cc, 0 : 2 * UB])
        du[...] += dot_nt(d_both, bgu_ref[...])
        both = dot(ut_ref[...], d_both)
        dbg_out[...] = both[:RANK, :UB]
        dbu_out[...] = both[RANK:, UB:]
        gad_out[...] = dot_tn(dd[...], hs[...])

        @pl.when(j == blocks - 1)
        def _():
            total = acc[...] + dot(du[...].astype(BF16), ain_ref[...])
            own_out[...] = total[:half]
            peer_out[...] = total[half:].astype(BF16)
            du_out[...] = du[...]

    rows_block = lambda: pl.BlockSpec((r, UB), lambda j: (rb, j))
    unit_block = lambda: pl.BlockSpec((RANK, UB), lambda j: (0, j))
    row_const = lambda n: pl.BlockSpec((r, n), lambda j: (rb, 0), pipeline_mode=pl.Buffered(1))
    shape = jax.ShapeDtypeStruct
    return pl.pallas_call(
        body,
        grid=(blocks,),
        in_specs=[
            const_spec((half, width)),
            const_spec((half, width)),
            any_spec(),
            any_spec(),
            any_spec(),
            rows_block(),
            rows_block(),
            pl.BlockSpec((2 * RANK, 2 * UB), lambda j: (0, j)),
            unit_block(),
            const_spec((RANK, width)),
            pl.BlockSpec((2 * RANK, r), lambda j: (0, rb), pipeline_mode=pl.Buffered(1)),
            const_spec((2 * RANK, width)),
        ],
        out_specs=[
            const_spec((half, width)),
            const_spec((half, width)),
            unit_block(),
            unit_block(),
            unit_block(),
            const_spec((r, 2 * RANK)),
        ],
        out_shape=[
            shape((half, width), F32),
            shape((half, width), BF16),
            shape((RANK, units), F32),
            shape((RANK, units), F32),
            shape((RANK, units), F32),
            shape((r, 2 * RANK), F32),
        ],
        scratch_shapes=[
            pltpu.VMEM((r, width), BF16),
            pltpu.VMEM((r, width), F32),
            pltpu.VMEM((2, width, FB), BF16),
            pltpu.VMEM((r, RANK), BF16),
            pltpu.VMEM((r, 2 * RANK), F32),
            pltpu.VMEM((r, 2 * UB), BF16),
            pltpu.VMEM((r, UB), BF16),
            pltpu.SemaphoreType.DMA((2,)),
        ],
        compiler_params=params(),
        cost_estimate=pl.CostEstimate(
            flops=6 * r * width * units,
            bytes_accessed=6 * width * units,
            transcendentals=r * units,
        ),
        name="ffn_bwd",
    )(own, peer, *packs, g_pre, u_pre, bgu, ad_t, bd, u_t, a_in_t)


def ple_both(combined, ffn_own, ffn_recv, out_grad, ple_in, packed, column, gains, prev, rb):
    half, width = ffn_own.shape
    rows = combined.shape[0]
    pd = ple_in.shape[1]
    tile = half // 2

    def body(c_ref, fo_ref, fr_ref, og_ref, pi_ref, w_ref, gain_ref, *refs):
        out_ref, dffn_ref, dfirst_ref = refs[-3:]
        ffn = fo_ref[...] + fr_ref[...].astype(F32)
        y = c_ref[...] + normed(ffn, gain_ref[4:5, :])
        pre = dot(y.astype(BF16), w_ref[:, 0:pd])
        side = pi_ref[...].astype(F32)
        act, slope = gelu_both(pre)
        wide = dot_nt((act * side).astype(BF16), w_ref[:, pd : 2 * pd])
        out_ref[...] = (y + normed(wide, gain_ref[5:6, :])).astype(BF16)
        cot = og_ref[...].astype(F32)
        d_wide = norm_back(wide, gain_ref[5:6, :], cot).astype(BF16)
        d_pre = (dot(d_wide, w_ref[:, pd : 2 * pd]) * side * slope).astype(BF16)
        d_first = cot + dot_nt(d_pre, w_ref[:, 0:pd])
        dfirst_ref[...] = d_first
        dffn_ref[...] = norm_back(ffn, gain_ref[4:5, :], d_first).astype(BF16)

    n = half // tile
    here = lambda w: pl.BlockSpec((tile, w), lambda i: (i, 0))
    there = lambda w: pl.BlockSpec((tile, w), lambda i: (rb * n + i, 0))
    shape = jax.ShapeDtypeStruct
    return pl.pallas_call(
        body,
        grid=(n,),
        in_specs=[
            there(width),
            here(width),
            here(width),
            there(width),
            there(pd),
            pl.BlockSpec((width, 2 * pd), lambda i: (0, column), pipeline_mode=pl.Buffered(1)),
            const_spec(gains.shape),
        ]
        + [any_spec() for _ in prev],
        out_specs=[there(width), here(width), here(width)],
        out_shape=[
            shape((rows, width), BF16),
            shape((half, width), BF16),
            shape((half, width), F32),
        ],
        input_output_aliases={7: 0} if prev else {},
        compiler_params=params(),
        cost_estimate=pl.CostEstimate(
            flops=8 * half * width * pd, bytes_accessed=20 * half * width, transcendentals=0
        ),
        name="ple_both",
    )(combined, ffn_own, ffn_recv, out_grad, ple_in, packed, gains, *prev)


def between_bwd(d_first, combined, dh_own, dh_recv, attn_proj, low, packed, column, gains, prev, rb):
    half, width = d_first.shape
    rows = combined.shape[0]
    lr = low.shape[1]
    tile = half // 2

    def body(df_ref, c_ref, ho_ref, hr_ref, ap_ref, low_ref, w_ref, gain_ref, *refs):
        da_ref, db_ref, dn_ref = refs[-3:]
        d_h2 = ho_ref[...] + hr_ref[...].astype(F32)
        d_comb = df_ref[...] + norm_back(c_ref[...], gain_ref[3:4, :], d_h2)
        d_branch = d_comb * RSQRT_TWO
        db_ref[...] = d_branch
        da_ref[...] = norm_back(ap_ref[...], gain_ref[1:2, :], d_branch).astype(BF16)
        wide = dot_nt(low_ref[...], w_ref[:, lr : 2 * lr])
        d_wide = norm_back(wide, gain_ref[2:3, :], d_branch).astype(BF16)
        d_low = dot(d_wide, w_ref[:, lr : 2 * lr]).astype(BF16)
        dn_ref[...] = d_branch + dot_nt(d_low, w_ref[:, 0:lr])

    n = half // tile
    here = lambda w: pl.BlockSpec((tile, w), lambda i: (i, 0))
    there = lambda w: pl.BlockSpec((tile, w), lambda i: (rb * n + i, 0))
    shape = jax.ShapeDtypeStruct
    return pl.pallas_call(
        body,
        grid=(n,),
        in_specs=[
            here(width),
            there(width),
            here(width),
            here(width),
            there(width),
            there(lr),
            pl.BlockSpec((width, 2 * lr), lambda i: (0, column), pipeline_mode=pl.Buffered(1)),
            const_spec(gains.shape),
        ]
        + [any_spec() for _ in prev],
        out_specs=[here(width), there(width), there(width)],
        out_shape=[
            shape((half, width), BF16),
            shape((rows, width), F32),
            shape((rows, width), F32),
        ],
        input_output_aliases={8: 1, 9: 2} if prev else {},
        compiler_params=params(),
        cost_estimate=pl.CostEstimate(
            flops=6 * half * width * lr, bytes_accessed=26 * half * width, transcendentals=0
        ),
        name="between_bwd",
    )(d_first, combined, dh_own, dh_recv, attn_proj, low, packed, gains, *prev)


def attention_bwd(pieces, turn, packed, wo_column, bo, ao_t, q, k, v, probs, raw, gains, cos, sin):
    length, q_width = q.shape
    width = packed.shape[0]
    heads = q_width // HD
    half_hd = HD // 2
    scale = HD ** (-0.5)
    n_blocks = length // BLK
    span = WIN // BLK
    quarter = pieces[0].shape[0]
    count = len(pieces)

    def unrotate(d, cos_v, sin_v):
        d1, d2 = d[:, :half_hd], d[:, half_hd:]
        return jnp.concatenate([d1 * cos_v + d2 * sin_v, d2 * cos_v - d1 * sin_v], axis=1)

    def body(turn_ref, *refs):
        piece_refs = refs[:count]
        (wo_ref, bo_ref, ao_ref, q_ref, k_ref, v_ref, p_ref, rq_ref, rk_ref, gain_ref, cos_ref,
         sin_ref, out_ref, du_ref, da, du, dk, dv) = refs[count:]
        hh = pl.program_id(0)

        @pl.when(hh == 0)
        def _():
            shift = turn_ref[0] * (length // 2)
            for i, ref in enumerate(piece_refs):
                place = lax.rem(shift + i * quarter, length)
                da[pl.ds(pl.multiple_of(place, quarter), quarter), :] = ref[...]
            got = dot_nt(da[...], bo_ref[...])
            du_ref[...] = got
            du[...] = got.astype(BF16)
            dk[...] = jnp.zeros_like(dk)
            dv[...] = jnp.zeros_like(dv)

        dctx = (dot(da[...], wo_ref[...]) + dot(du[...], ao_ref[...])).astype(BF16)
        cos_v, sin_v = cos_ref[...], sin_ref[...]
        for i in range(n_blocks):
            low, high = max(0, i - span + 1) * BLK, (i + 1) * BLK
            rows = slice(i * BLK, (i + 1) * BLK)
            d_i = dctx[rows]
            p_i = p_ref[0, rows, low:high]
            p_f = p_i.astype(F32)
            dp = dot_nt(d_i, v_ref[low:high, :])
            ds = p_f * (dp - jnp.sum(p_f * dp, axis=-1, keepdims=True))
            ds = ds.astype(BF16)
            dq = dot(ds, k_ref[low:high, :]) * scale
            dk[low:high, :] += dot_tn(ds, q_ref[rows, :])
            dv[low:high, :] += dot_tn(p_i, d_i)
            back = norm_back(rq_ref[rows, :], gain_ref[0:1, :], unrotate(dq, cos_v[rows], sin_v[rows]))
            out_ref[rows, pl.ds(pl.multiple_of(hh * HD, HD), HD)] = back.astype(BF16)

        @pl.when(hh == heads - 1)
        def _():
            back = norm_back(rk_ref[...], gain_ref[1:2, :], unrotate(dk[...] * scale, cos_v, sin_v))
            out_ref[:, q_width : q_width + HD] = back.astype(BF16)
            out_ref[:, q_width + HD : q_width + 2 * HD] = dv[...].astype(BF16)

    shape = jax.ShapeDtypeStruct
    head_block = pl.BlockSpec((length, HD), lambda h: (0, h))
    total = q_width + 2 * HD
    return pl.pallas_call(
        body,
        grid=(heads,),
        in_specs=[pl.BlockSpec(memory_space=pltpu.SMEM)]
        + [const_spec(piece.shape) for piece in pieces]
        + [
            pl.BlockSpec((width, HD), lambda h: (0, wo_column + h)),
            const_spec(bo.shape),
            pl.BlockSpec((RANK, HD), lambda h: (0, h)),
            head_block,
            const_spec(k.shape),
            const_spec(v.shape),
            pl.BlockSpec((1, length, length), lambda h: (h, 0, 0)),
            head_block,
            pl.BlockSpec((length, HD), lambda h: (0, heads), pipeline_mode=pl.Buffered(1)),
            const_spec(gains.shape),
            const_spec(cos.shape),
            const_spec(sin.shape),
        ],
        out_specs=[const_spec((length, total)), const_spec((length, RANK))],
        out_shape=[shape((length, total), BF16), shape((length, RANK), F32)],
        scratch_shapes=[
            pltpu.VMEM((length, width), BF16),
            pltpu.VMEM((length, RANK), BF16),
            pltpu.VMEM((length, HD), F32),
            pltpu.VMEM((length, HD), F32),
        ],
        compiler_params=params(),
        cost_estimate=pl.CostEstimate(
            flops=2 * length * width * q_width + 8 * heads * length * WIN * HD,
            bytes_accessed=24 * 1024 * 1024,
            transcendentals=0,
        ),
        name="attention_bwd",
    )(turn, *pieces, packed, bo, ao_t, q, k, v, probs, raw, raw, gains, cos, sin)


def final_bwd(x, d_norm, d_branch, dh_own, dh_recv, gains):
    rows, width = x.shape
    tile = rows // 4

    def body(x_ref, dn_ref, db_ref, ho_ref, hr_ref, gain_ref, out_ref):
        total = dn_ref[...] + ho_ref[...] + hr_ref[...].astype(F32)
        out_ref[...] = db_ref[...] + norm_back(x_ref[...].astype(F32), gain_ref[0:1, :], total)

    block = pl.BlockSpec((tile, width), lambda i: (i, 0))
    return pl.pallas_call(
        body,
        grid=(rows // tile,),
        in_specs=[block] * 5 + [const_spec(gains.shape)],
        out_specs=block,
        out_shape=jax.ShapeDtypeStruct((rows, width), F32),
        compiler_params=params(),
        cost_estimate=pl.CostEstimate(
            flops=20 * rows * width, bytes_accessed=20 * rows * width, transcendentals=0
        ),
        name="final_bwd",
    )(x, d_norm, d_branch, dh_own, dh_recv, gains)


def rope_tables(length):
    half_dim = HD // 2
    inverse = ROPE_BASE ** (-jnp.arange(half_dim, dtype=F32) / half_dim)
    angles = jnp.arange(length, dtype=F32)[:, None] * inverse[None, :]
    return jnp.cos(angles), jnp.sin(angles)


def rotate(values, cos, sin):
    half_dim = HD // 2
    a, b = values[..., :half_dim], values[..., half_dim:]
    return jnp.concatenate([a * cos - b * sin, b * cos + a * sin], axis=-1)


def on_device(
    hidden_in,
    per_layer_input,
    out_grad,
    adapter_ids,
    weight_qkv,
    weight_attn_out,
    weight_gate_up,
    weight_down,
    laurel_left,
    laurel_right,
    per_layer_gate,
    per_layer_proj,
    norm_gains,
    head_gains,
    adapter_qkv_in,
    adapter_qkv_out,
    adapter_attn_in,
    adapter_attn_out,
    adapter_ffn_in,
    adapter_ffn_out,
    adapter_down_in,
    adapter_down_out,
):
    rows_here, width = hidden_in.shape
    dp = lax.axis_size("dp")
    length = rows_here * 2
    half = rows_here // 2
    per_group = HEADS // KV
    q_width = per_group * HD
    qkv_width = q_width + 2 * HD
    units = weight_down.shape[0]
    blocks = units // UB
    adapters = adapter_qkv_in.shape[0]
    a = adapter_ids[0]
    t = lax.axis_index("tensor")

    def swap(v):
        return lax.ppermute(v, "tensor", [(0, 1), (1, 0)])

    def in_order(own, other):
        first = jnp.where(t == 0, own, other)
        second = jnp.where(t == 0, other, own)
        return jnp.concatenate([first, second], axis=0)

    def mine(v):
        return lax.dynamic_slice_in_dim(v, t * rows_here, rows_here, axis=0)

    def theirs(v):
        return lax.dynamic_slice_in_dim(v, (1 - t) * rows_here, rows_here, axis=0)

    counts = (1, blocks // 2, blocks - 1 - blocks // 2)
    lr = laurel_left.shape[1]
    pd = per_layer_gate.shape[1]
    pack_1 = pack_blocks(
        weight_gate_up, weight_down, 0, counts[0],
        [(weight_qkv, qkv_width), (weight_attn_out, q_width), (laurel_left, lr), (laurel_right, lr)],
        width, "pack_1",
    )
    gather = lambda v: lax.all_gather(v, "dp", axis=0, tiled=True)
    full_1 = gather(pack_1)
    x_peer = swap(hidden_in)
    pack_2 = pack_blocks(
        weight_gate_up, weight_down, counts[0], counts[1],
        [(per_layer_gate, pd), (per_layer_proj, pd)], width, "pack_2",
    )
    pack_3 = pack_blocks(
        weight_gate_up, weight_down, counts[0] + counts[1], counts[2], [], width, "pack_3"
    )
    pack_2, _ = lax.optimization_barrier((pack_2, full_1))
    full_2 = gather(pack_2)
    w_qkv = full_1[:, FB : FB + qkv_width]
    wo_at = FB + qkv_width
    w_o_t = full_1[:, wo_at : wo_at + q_width]
    lau_at = wo_at + q_width
    left = full_1[:, lau_at : lau_at + lr]
    right_t = full_1[:, lau_at + lr : lau_at + 2 * lr]
    ple_column = counts[1] * FB // (2 * pd)

    two = jnp.asarray(2.0, BF16)
    qkv_in = adapter_qkv_in[a]
    raw_out = adapter_qkv_out[a].reshape(RANK, qkv_width) * two
    column = jnp.arange(qkv_width)
    member = (column >= q_width).astype(jnp.int32) + (column >= q_width + HD).astype(jnp.int32)
    pick = (jnp.arange(3)[:, None] == member[None, :]).astype(BF16)
    b_qkv = (pick[:, None, :] * raw_out[None]).reshape(3 * RANK, qkv_width)
    a_o = adapter_attn_in[a]
    b_o = adapter_attn_out[a] * two
    a_ffn = adapter_ffn_in[a]
    b_ffn = adapter_ffn_out[a] * two
    b_unit = jnp.swapaxes(b_ffn.reshape(RANK, 2, blocks, UB), 1, 2)
    side = (jnp.arange(2)[:, None] == jnp.arange(2)[None, :]).astype(BF16)
    bgu = (side[:, None, None, :, None] * b_unit[None]).reshape(2 * RANK, 2 * units)
    ad_t = adapter_down_in[a].T
    b_d = adapter_down_out[a] * two

    cos, sin = rope_tables(length)
    x_float = hidden_in.astype(F32)
    x_norm = normed(x_float, norm_gains[0])
    h_own = x_norm.astype(BF16)
    x_all = in_order(hidden_in, x_peer)
    h_all = normed(x_all.astype(F32), norm_gains[0]).astype(BF16)
    u_qkv = dot(h_all, qkv_in).astype(BF16)
    raw = dot(h_all, w_qkv) + dot(u_qkv, b_qkv)
    q_raw = raw[:, :q_width].reshape(length, per_group, HD)
    k_raw = raw[:, q_width : q_width + HD]
    queries = rotate(normed(q_raw, head_gains[0]), cos[:, None], sin[:, None]).astype(BF16)
    keys = rotate(normed(k_raw, head_gains[1]), cos, sin).astype(BF16)
    values = raw[:, q_width + HD :].astype(BF16)
    index = jnp.arange(length) // BLK
    distance = index[:, None] - index[None, :]
    allowed = ((distance >= 0) & (distance < WIN // BLK))[None]
    scores = jnp.einsum("lqd,md->qlm", queries, keys, preferred_element_type=F32) * HD ** (-0.5)
    scores = jnp.where(allowed, scores, NEG_BIG)
    shifted = jnp.exp(scores - jnp.max(scores, axis=-1, keepdims=True))
    probs = (shifted / jnp.sum(shifted, axis=-1, keepdims=True)).astype(BF16)
    context = (
        jnp.einsum("qlm,md->lqd", probs, values, preferred_element_type=F32)
        .reshape(length, q_width)
        .astype(BF16)
    )
    queries = queries.reshape(length, q_width)
    u_attn_f = dot(context, a_o)
    u_attn = u_attn_f.astype(BF16)
    attn_part = dot_nt(context, w_o_t) + dot(u_attn, b_o)
    attn_recv = swap(theirs(attn_part).astype(BF16))
    attn_proj = mine(attn_part) + attn_recv.astype(F32)
    laurel_low = dot(h_own, left).astype(BF16)
    laurel_wide = dot_nt(laurel_low, right_t)
    combined = (
        x_float + normed(attn_proj, norm_gains[1]) + x_norm + normed(laurel_wide, norm_gains[2])
    ) * RSQRT_TWO
    h2_own = normed(combined, norm_gains[3]).astype(BF16)

    h2_peer = swap(h2_own)
    h2 = jnp.concatenate([h2_own[:half], h2_peer[:half], h2_own[half:], h2_peer[half:]], axis=0)
    u_ffn = dot(h2, a_ffn).astype(BF16)
    pack_3, _, _ = lax.optimization_barrier((pack_3, full_2, h2_own))
    full_3 = gather(pack_3)
    g_pre, u_pre, acc, ud = ffn_fwd(
        h2, full_1, counts[0], 0, u_ffn, bgu, ad_t, b_d, None, None
    )
    g_pre, u_pre, acc, ud = ffn_fwd(
        h2, full_2, counts[1], counts[0], u_ffn, bgu, ad_t, b_d, (acc, ud, g_pre, u_pre), None
    )
    at = counts[0] + counts[1]
    fwd_parts, ud_parts, ple_parts, bwd_parts = [], [], [], []
    d_ffn_parts, d_attn_own, d_attn_peer = [], [], []
    for s in range(2):
        g_pre, u_pre, own, peer, ud_s = ffn_fwd(
            h2, full_3, counts[2], at, u_ffn, bgu, ad_t, b_d, (acc, ud, g_pre, u_pre), s
        )
        fwd_parts.append((own, swap(peer)))
        ud_parts.append(ud_s)
    layer_out = []
    for s in range(2):
        own, recv = fwd_parts[s]
        whole, d_ffn_s, d_first_s = ple_both(
            combined, own, recv, out_grad, per_layer_input, full_2, ple_column, norm_gains,
            layer_out, s,
        )
        layer_out = [whole]
        ple_parts.append((d_ffn_s, swap(d_ffn_s), d_first_s))
    packs = (full_1, full_2, full_3)
    branch = []
    for s in range(2):
        d_ffn_s, d_ffn_recv, d_first_s = ple_parts[s]
        got = ffn_bwd(
            d_ffn_s, d_ffn_recv, packs, counts, g_pre, u_pre, bgu, ad_t, b_d, u_ffn.T, a_ffn.T, s
        )
        bwd_parts.append(got[2:])
        d_ffn_parts += [d_ffn_s, d_ffn_recv]
        d_h2_recv = swap(got[1])
        d_attn_s, *branch = between_bwd(
            d_first_s, combined, got[0], d_h2_recv, attn_proj, laurel_low, full_1,
            lau_at // (2 * lr), norm_gains, branch, s,
        )
        d_attn_own.append(d_attn_s)
        d_attn_peer.append(swap(d_attn_s))
    d_branch, d_norm = branch

    tag = jnp.full((1, 128), a, BF16)

    def onehot_of(ids):
        return (ids[None, :] == jnp.arange(adapters, dtype=F32)[:, None]).astype(BF16)

    def over_sequences(grad):
        n, m = grad.shape
        send = jnp.concatenate([grad.astype(BF16), jnp.broadcast_to(tag, (n, 128))], axis=1)
        return send

    def summed(send):
        got = lax.all_gather(send, "dp", axis=0, tiled=False)
        onehot = onehot_of(got[:, 0, send.shape[1] - 1].astype(F32))
        got = got[:, :, : send.shape[1] - 128]
        return jnp.einsum("as,snm->anm", onehot, got, preferred_element_type=F32)

    send_ffn = over_sequences(
        jnp.concatenate(
            [
                2.0 * (bwd_parts[0][0] + bwd_parts[1][0]),
                2.0 * (bwd_parts[0][1] + bwd_parts[1][1]),
                bwd_parts[0][2] + bwd_parts[1][2],
            ],
            axis=0,
        )
    )

    pieces = d_attn_own + d_attn_peer
    pieces, send_ffn = lax.optimization_barrier((pieces, send_ffn))
    sum_ffn = summed(send_ffn)
    d_raw, du_attn = attention_bwd(
        pieces, t.astype(jnp.int32).reshape(1), full_1, wo_at // HD, b_o, a_o.T, queries, keys,
        values, probs, raw, head_gains, cos, sin,
    )
    d_u = dot_nt(d_raw, b_qkv).astype(BF16)
    d_h_peer = (dot_nt(theirs(d_raw), w_qkv) + dot_nt(theirs(d_u), qkv_in)).astype(BF16)
    d_h_recv = swap(d_h_peer)
    d_raw, d_u, _ = lax.optimization_barrier((d_raw, d_u, d_h_peer))
    grad_b = 2.0 * dot_tn(u_qkv, d_raw)
    grad_qkv_out = jnp.concatenate(
        [
            grad_b[:RANK, :q_width],
            grad_b[RANK : 2 * RANK, q_width : q_width + HD],
            grad_b[2 * RANK :, q_width + HD :],
        ],
        axis=1,
    )
    sum_qkv_out = summed(over_sequences(grad_qkv_out))
    sum_attn_in = summed(over_sequences(dot_tn(du_attn.astype(BF16), context)))

    d_attn_all = in_order(
        jnp.concatenate(d_attn_own, axis=0), jnp.concatenate(d_attn_peer, axis=0)
    )
    d_ffn_all = jnp.concatenate(d_ffn_parts, axis=0)
    du_ffn = jnp.concatenate([bwd_parts[0][3], bwd_parts[1][3]], axis=0).astype(BF16)
    ud_low = jnp.concatenate(ud_parts, axis=0).astype(BF16)
    send = jnp.concatenate(
        [
            dot_tn(h2, du_ffn).astype(BF16),
            (2.0 * dot_tn(d_ffn_all, ud_low)).astype(BF16),
            (2.0 * dot_tn(d_attn_all, u_attn)).astype(BF16),
            dot_tn(h_all, d_u).astype(BF16),
            jnp.broadcast_to(tag[:, :1], (width, 1)),
        ],
        axis=1,
    )
    got = lax.all_to_all(send, ("dp", "tensor"), 0, 0, tiled=True).reshape(2 * dp, -1, send.shape[1])
    onehot = onehot_of(got[:, 0, send.shape[1] - 1].astype(F32))
    shared = jnp.einsum("as,snm->anm", onehot, got, preferred_element_type=F32)
    d_h_own = dot_nt(mine(d_raw), w_qkv) + dot_nt(mine(d_u), qkv_in)
    input_grad = final_bwd(hidden_in, d_norm, d_branch, d_h_own, d_h_recv, norm_gains)
    return (
        layer_out[0],
        input_grad,
        shared[:, :, 4 * RANK : 7 * RANK],
        sum_qkv_out.reshape(adapters, RANK, 1, qkv_width),
        jnp.swapaxes(sum_attn_in, 1, 2),
        jnp.swapaxes(shared[:, :, 3 * RANK : 4 * RANK], 1, 2),
        shared[:, :, : 2 * RANK],
        jnp.stack([sum_ffn[:, :RANK], sum_ffn[:, RANK : 2 * RANK]], axis=2),
        jnp.swapaxes(sum_ffn[:, 2 * RANK :], 1, 2),
        jnp.swapaxes(shared[:, :, 2 * RANK : 3 * RANK], 1, 2),
    )


def solution(mesh):
    in_specs = (
        P(("dp", "tensor"), None),
        P(("dp", "tensor"), None),
        P(("dp", "tensor"), None),
        P("dp"),
        P("dp", "tensor", None),
        P("tensor", "dp"),
        P("dp", None, "tensor"),
        P("tensor", "dp"),
        P("dp", None),
        P(None, "dp"),
        P("dp", None),
        P(None, "dp"),
        P(),
        P(),
        P(),
        P(None, None, "tensor", None),
        P(None, "tensor", None),
        P(),
        P(),
        P(None, None, None, "tensor"),
        P(None, "tensor", None),
        P(),
    )
    out_specs = (
        P(("dp", "tensor"), None),
        P(("dp", "tensor"), None),
        P(None, ("dp", "tensor"), None),
        P(None, None, "tensor", None),
        P(None, "tensor", None),
        P(None, None, ("dp", "tensor")),
        P(None, ("dp", "tensor"), None),
        P(None, None, None, "tensor"),
        P(None, "tensor", None),
        P(None, None, ("dp", "tensor")),
    )
    return jax.shard_map(
        on_device, mesh=mesh, in_specs=in_specs, out_specs=out_specs, check_vma=False
    )
```

time: 1800 us -> 735 us (0.41)
  waiting for transfers between devices: 1200 us -> 248 us
  matrix products: 319 us -> 67.4 us
  Pallas kernels: 0 us -> 219 us
  local copies, waits for them, and re-layouts: 132 us -> 69.9 us
  other arithmetic: 85.4 us -> 49.1 us
    all_gather x10 -> x4, waiting for transfers between devices: 504 us -> 101 us  [the longest x3 101 us: on_device(): gather = lambda v: lax.all_gather(v, 'dp', axis=0, tiled=True)]
    unnamed x23 -> x4, waiting for transfers between devices: 356 us -> 0.07 us
    dot_general x52 -> x26, matrix products: 319 us -> 67.4 us  [the longest x7 24.7 us: dot_nt(): lax.dot_general(a, b, (((1,), (1,)), ((), ())), preferred_element_type=F32)]
    pallas_call x0 -> x15, Pallas kernels: none -> 219 us  [the longest x4 76.9 us: ffn_fwd(): pl.pallas_call(body, grid=(blocks,), in_specs=in_specs, out_specs=out_spe...]
    reduce_scatter x4 -> x0, waiting for transfers between devices: 189 us -> none  [the longest x1 72.7 us: on_device(): lax.psum_scatter(feed_portion, 'tensor', scatter_dimension=0, tiled=True)]
    psum x1 -> x0, waiting for transfers between devices: 153 us -> none  [on_device(): lax.psum((spread(query_key_value_output_gradient_local), spread(feed_outp...]
    ppermute x0 -> x12, waiting for transfers between devices: none -> 142 us  [swap(): return lax.ppermute(v, 'tensor', [(0, 1), (1, 0)])]
    unnamed x261 -> x143, local copies, waits for them, and re-layouts: 115 us -> 34.2 us
  transfers between devices with their start and end apart: 19 -> 17, of which waited for: 18 -> 12; matrix products, arithmetic and copies ran while one was open for 19% -> 19% of each run, Pallas kernels for 0% -> 26%
where the time goes in v1:
time: 735 us; the launch traced here: 729 us
  waiting for transfers between devices  248 us (34%)
  Pallas kernels  219 us (30%)
  local copies, waits for them, and re-layouts  69.9 us (10%)
  matrix products  67.4 us (9%)
  other arithmetic  49.1 us (7%)
  blocking collectives  44.2 us (6%)
  starting transfers between devices  16.5 us (2%)
  between operations  15.7 us (2%)
    ppermute x12, waiting for transfers between devices, swap(): return lax.ppermute(v, 'tensor', [(0, 1), (1, 0)])  142 us
    all_gather x3, waiting for transfers between devices, on_device(): gather = lambda v: lax.all_gather(v, 'dp', axis=0, tiled=True)  101 us
    pallas_call x4, Pallas kernels, ffn_fwd(): pl.pallas_call(body, grid=(blocks,), in_specs=in_specs, out_specs=out_spe...  76.9 us
    pallas_call x2, Pallas kernels, ffn_bwd(): pl.pallas_call(body, grid=(blocks,), in_specs=[const_spec((half, width)),...  70.2 us
    all_gather x2, blocking collectives, summed(): got = lax.all_gather(send, 'dp', axis=0, tiled=False)  44.2 us
    unnamed x143, local copies, waits for them, and re-layouts  34.2 us
    dot_general x7, matrix products, dot_nt(): lax.dot_general(a, b, (((1,), (1,)), ((), ())), preferred_element_type=F32)  24.7 us
    pallas_call x1, Pallas kernels, attention_bwd(): pl.pallas_call(body, grid=(heads,), in_specs=[pl.BlockSpec(memory_space=p...  21.3 us
  transfers between devices with their start and end apart: 17, of which 12 were waited for; matrix products, arithmetic and copies ran while one was open for 19% of the time, Pallas kernels for 26%

profile of v1, /device:TPU:0, one launch (start us, length us, event | category | flops | bytes accessed | tf_op | source)
XLA Modules:
  0.0 728.7 jit_solution(17608465343566351369)
XLA Ops:
  20.6 89.1 %all-gather.8.cloned.1.call-done.refs_1_.p0.w_ref.refs_4_ = bf16[2048,4224]{1,0:T(8,128)(2,1)} async-done(((bf16[128,4224]{1,0:T(8,128)(2,1)}), bf16[2048,4224]{1,0:T(8,128)(2,1)}) %all-gather.8.cloned.1.call-update) | async-done | bytes 17301520 | tf_op jit(solution)/shard_map/all_gather | solution.py:654
  117.6 29.0 %collective-permute-done = bf16[384,2048]{1,0:T(8,128)(2,1)} collective-permute-done((bf16[384,2048]{1,0:T(8,128)(2,1)S(1)}, bf16[384,2048]{1,0:T(8,128)(2,1)}, u32[]{:S(2)}, u32[]{:S(2)}) %collective-permute-start) | collective-permute-done | bytes 1572896 | tf_op jit(solution)/shard_map/ppermute | solution.py:633
  151.0 7.9 %fusion.18.refs_11_.refs_12_ = f32[768,1536]{1,0:T(8,128)S(1)} fusion(f32[768,1536]{1,0:T(8,128)S(1)} %fusion.153, bf16[2048,4224]{1,0:T(8,128)(2,1)} %all-gather.8.cloned.1.call-done.refs_1_.p0.w_ref.refs_4_, f32[2048]{0:T(1024)S(1)} %bitcast.149, f32[768]{0:T(1024)S(1)} %add_rsqrt_fusion.2, bf16[384,2048]{1,0:T(8,128)(2,1)S(1)} %get-tuple-element.170, ...), kind=kOutput, calls=%fused_computation.28 | convolution fusion | flops 4844027904 | bytes 18885632 | tf_op jit(solution)/shard_map/dot_general | solution.py:32
  184.2 14.6 %fusion.151 = (f32[4,768]{1,0:T(4,128)S(1)}, f32[4,768,768]{2,1,0:T(8,128)}) fusion(f32[768,768,4]{0,1,2:T(8,128)} %fusion.82, pred[768,768]{1,0:T(8,128)(4,1)S(1)} %copy-done.41), kind=kOutput, calls=%fused_computation.225 | output fusion | flops 14156543 | bytes 19476480 | tf_op jit(solution)/shard_map/sub | solution.py:709
  228.5 26.2 %collective-permute-done.1 = bf16[384,2048]{1,0:T(8,128)(2,1)} collective-permute-done((bf16[384,2048]{1,0:T(8,128)(2,1)}, bf16[384,2048]{1,0:T(8,128)(2,1)}, u32[]{:S(2)}, u32[]{:S(2)}) %collective-permute-start.1) | collective-permute-done | bytes 1572896 | tf_op jit(solution)/shard_map/ppermute | solution.py:633
  272.0 23.5 %collective-permute-done.2 = bf16[384,2048]{1,0:T(8,128)(2,1)} collective-permute-done((bf16[384,2048]{1,0:T(8,128)(2,1)S(1)}, bf16[384,2048]{1,0:T(8,128)(2,1)}, u32[]{:S(2)}, u32[]{:S(2)}) %collective-permute-start.2) | collective-permute-done | bytes 1572896 | tf_op jit(solution)/shard_map/ppermute | solution.py:633
  302.0 12.3 %ffn_fwd.4 = (bf16[768,4096]{1,0:T(8,128)(2,1)}, bf16[768,4096]{1,0:T(8,128)(2,1)}, f32[768,2048]{1,0:T(8,128)}, f32[768,16]{1,0:T(8,128)}) custom-call(bf16[768,2048]{1,0:T(8,128)(2,1)} %copy-done.1, bf16[2048,4224]{1,0:T(8,128)(2,1)} %all-gather.8.cloned.1.call-done.refs_1_.p0.w_ref.refs_4_, bf16[768,32]{1,0:T(8,128)(2,1)} %copy.136.refs_2_, ...), custom_call_target="tpu_custom_call" | custom-call | flops 4831838208 | bytes 18874368 | tf_op jit(solution)/shard_map/ffn_fwd/pallas_call | solution.py:208
  314.4 33.0 %ffn_fwd.5 = (bf16[768,4096]{1,0:T(8,128)(2,1)}, bf16[768,4096]{1,0:T(8,128)(2,1)}, f32[768,2048]{1,0:T(8,128)}, f32[768,16]{1,0:T(8,128)}) custom-call(bf16[768,2048]{1,0:T(8,128)(2,1)} %copy-done.1, bf16[2048,6656]{1,0:T(8,128)(2,1)} %all-gather.10.cloned.1.call-done.refs_1_.w_ref.p1, ...), custom_call_target="tpu_custom_call", output_to_operand_aliasing={{0}: (8, {}), {1}: (9, {})} | custom-call | flops 19327352832 | bytes 37748736 | tf_op jit(solution)/shard_map/ffn_fwd/pallas_call | solution.py:208
  347.4 12.1 %all-gather.12.cloned.1.call-done.refs_1_.p2 = bf16[2048,4608]{1,0:T(8,128)(2,1)} async-done(((bf16[128,4608]{1,0:T(8,128)(2,1)}), bf16[2048,4608]{1,0:T(8,128)(2,1)}) %all-gather.12.cloned.1.call-update) | async-done | bytes 18874384 | tf_op jit(solution)/shard_map/all_gather | solution.py:654
  359.4 15.9 %ffn_fwd.6 = (bf16[768,4096]{1,0:T(8,128)(2,1)}, bf16[768,4096]{1,0:T(8,128)(2,1)}, f32[192,2048]{1,0:T(8,128)}, bf16[192,2048]{1,0:T(8,128)(2,1)}, f32[384,16]{1,0:T(8,128)}) custom-call(bf16[768,2048]{1,0:T(8,128)(2,1)} %copy-done.1, bf16[2048,4608]{1,0:T(8,128)(2,1)} %all-gather.12.cloned.1.call-done.refs_1_.p2, ...), custom_call_target="tpu_custom_call", output_to_operand_aliasing={{0}: (8, {}), {1}: (9, {})} | custom-call | flops 7247757312 | bytes 25165824 | tf_op jit(solution)/shard_map/ffn_fwd/pallas_call | solution.py:208
  376.8 15.7 %ffn_fwd.7 = (bf16[768,4096]{1,0:T(8,128)(2,1)}, bf16[768,4096]{1,0:T(8,128)(2,1)}, f32[192,2048]{1,0:T(8,128)}, bf16[192,2048]{1,0:T(8,128)(2,1)}, f32[384,16]{1,0:T(8,128)}) custom-call(bf16[768,2048]{1,0:T(8,128)(2,1)} %copy-done.1, bf16[2048,4608]{1,0:T(8,128)(2,1)} %all-gather.12.cloned.1.call-done.refs_1_.p2, ...), custom_call_target="tpu_custom_call", output_to_operand_aliasing={{0}: (8, {}), {1}: (9, {})} | custom-call | flops 7247757312 | bytes 25165824 | tf_op jit(solution)/shard_map/ffn_fwd/pallas_call | solution.py:208
  396.2 8.2 %ple_both.2 = (bf16[384,2048]{1,0:T(8,128)(2,1)}, bf16[192,2048]{1,0:T(8,128)(2,1)}, f32[192,2048]{1,0:T(8,128)}) custom-call(f32[384,2048]{1,0:T(8,128)} %get-tuple-element.168.c_ref, f32[192,2048]{1,0:T(8,128)} %get-tuple-element.77.fo_ref, bf16[192,2048]{1,0:T(8,128)(2,1)} %copy-done.37, bf16[384,2048]{1,0:T(8,128)(2,1)} %og_ref.3, ...), custom_call_target="tpu_custom_call" | custom-call | flops 805306368 | bytes 7864320 | tf_op jit(solution)/shard_map/ple_both/pallas_call | solution.py:384
  404.4 7.9 %collective-permute-done.3.fr_ref = bf16[192,2048]{1,0:T(8,128)(2,1)S(1)} collective-permute-done((bf16[192,2048]{1,0:T(8,128)(2,1)}, bf16[192,2048]{1,0:T(8,128)(2,1)S(1)}, u32[]{:S(2)}, u32[]{:S(2)}) %collective-permute-start.3) | collective-permute-done | bytes 786464 | tf_op jit(solution)/shard_map/ppermute | solution.py:633
  413.1 8.3 %ple_both.3 = (bf16[384,2048]{1,0:T(8,128)(2,1)}, bf16[192,2048]{1,0:T(8,128)(2,1)}, f32[192,2048]{1,0:T(8,128)}) custom-call(f32[384,2048]{1,0:T(8,128)} %get-tuple-element.168.c_ref, f32[192,2048]{1,0:T(8,128)} %get-tuple-element.75.fo_ref, bf16[192,2048]{1,0:T(8,128)(2,1)} %copy-done.38, ...), custom_call_target="tpu_custom_call", output_to_operand_aliasing={{0}: (7, {})} | custom-call | flops 805306368 | bytes 7864320 | tf_op jit(solution)/shard_map/ple_both/pallas_call | solution.py:384
  425.0 17.1 %collective-permute-done.5.peer_ref = bf16[192,2048]{1,0:T(8,128)(2,1)S(1)} collective-permute-done((bf16[192,2048]{1,0:T(8,128)(2,1)}, bf16[192,2048]{1,0:T(8,128)(2,1)S(1)}, u32[]{:S(2)}, u32[]{:S(2)}) %collective-permute-start.5) | collective-permute-done | bytes 786464 | tf_op jit(solution)/shard_map/ppermute | solution.py:633
  443.0 35.3 %ffn_bwd.2 = (f32[192,2048]{1,0:T(8,128)}, bf16[192,2048]{1,0:T(8,128)(2,1)}, f32[16,4096]{1,0:T(8,128)}, f32[16,4096]{1,0:T(8,128)}, f32[16,4096]{1,0:T(8,128)}, /*index=5*/f32[384,32]{1,0:T(8,128)}) custom-call(bf16[192,2048]{1,0:T(8,128)(2,1)} %get-tuple-element.82.own_ref, bf16[192,2048]{1,0:T(8,128)(2,1)} %copy-done.34, ...), custom_call_target="tpu_custom_call" | custom-call | flops 19327352832 | bytes 50331648 | tf_op jit(solution)/shard_map/ffn_bwd/pallas_call | solution.py:305
  480.7 34.9 %ffn_bwd.3 = (f32[192,2048]{1,0:T(8,128)}, bf16[192,2048]{1,0:T(8,128)(2,1)}, f32[16,4096]{1,0:T(8,128)}, f32[16,4096]{1,0:T(8,128)}, f32[16,4096]{1,0:T(8,128)}, /*index=5*/f32[384,32]{1,0:T(8,128)}) custom-call(bf16[192,2048]{1,0:T(8,128)(2,1)} %get-tuple-element.88.own_ref, bf16[192,2048]{1,0:T(8,128)(2,1)} %copy-done.35, ...), custom_call_target="tpu_custom_call" | custom-call | flops 19327352832 | bytes 50331648 | tf_op jit(solution)/shard_map/ffn_bwd/pallas_call | solution.py:305
  517.4 14.6 %collective-permute-done.8.hr_ref = bf16[192,2048]{1,0:T(8,128)(2,1)S(1)} collective-permute-done((bf16[192,2048]{1,0:T(8,128)(2,1)}, bf16[192,2048]{1,0:T(8,128)(2,1)S(1)}, u32[]{:S(2)}, u32[]{:S(2)}) %collective-permute-start.8) | collective-permute-done | bytes 786464 | tf_op jit(solution)/shard_map/ppermute | solution.py:633
  549.2 10.6 %collective-permute-done.9.refs_2_ = bf16[192,2048]{1,0:T(8,128)(2,1)} collective-permute-done((bf16[192,2048]{1,0:T(8,128)(2,1)}, bf16[192,2048]{1,0:T(8,128)(2,1)}, u32[]{:S(2)}, u32[]{:S(2)}) %collective-permute-start.9) | collective-permute-done | bytes 786464 | tf_op jit(solution)/shard_map/ppermute | solution.py:633
  559.9 11.5 %collective-permute-done.10.refs_3_ = bf16[192,2048]{1,0:T(8,128)(2,1)} collective-permute-done((bf16[192,2048]{1,0:T(8,128)(2,1)}, bf16[192,2048]{1,0:T(8,128)(2,1)}, u32[]{:S(2)}, u32[]{:S(2)}) %collective-permute-start.10) | collective-permute-done | bytes 786464 | tf_op jit(solution)/shard_map/ppermute | solution.py:633
  582.9 21.3 %attention_bwd.1 = (bf16[768,1536]{1,0:T(8,128)(2,1)}, f32[768,16]{1,0:T(8,128)}) custom-call(s32[1]{0:T(128)} %bitcast.27.turn_ref, bf16[192,2048]{1,0:T(8,128)(2,1)} %get-tuple-element.103.refs_0_, bf16[192,2048]{1,0:T(8,128)(2,1)} %get-tuple-element.104.refs_1_, bf16[192,2048]{1,0:T(8,128)(2,1)} %collective-permute-done.9.refs_2_, ...), custom_call_target="tpu_custom_call" | custom-call | flops 6442450944 | bytes 25165824 | tf_op jit(solution)/shard_map/attention_bwd/pallas_call | solution.py:522
  614.5 24.6 %all-gather = bf16[256,1664]{1,0:T(8,128)(2,1)S(1)} all-gather(bf16[16,1664]{1,0:T(8,128)(2,1)S(1)} %fusion.101), channel_id=2, replica_groups=mesh['dp'=16,'tensor'=2] {'dp'}, dimensions={0}, use_global_device_ids=true | all-gather | bytes 905216 | tf_op jit(solution)/shard_map/all_gather | solution.py:787
  639.8 19.5 %all-gather.1 = bf16[256,1152]{1,0:T(8,128)(2,1)S(1)} all-gather(bf16[16,1152]{1,0:T(8,128)(2,1)S(1)} %concatenate.68), channel_id=3, replica_groups=mesh['dp'=16,'tensor'=2] {'dp'}, dimensions={0}, use_global_device_ids=true | all-gather | bytes 626688 | tf_op jit(solution)/shard_map/all_gather | solution.py:787
  703.6 9.6 %fusion.5 = f32[8,48,4096]{2,0,1:T(8,128)S(1)} fusion(bf16[16,48,4096]{2,1,0:T(8,128)(2,1)} %slice.185, f32[16]{0:T(128)S(1)} %bitcast_convert_fusion), kind=kOutput, calls=%fused_computation.10 | convolution fusion | flops 50331776 | bytes 12582976 | tf_op jit(solution)/shard_map/as,snm->anm/dot_general | solution.py:790
  (287 shorter events, 210.3 us)
Async XLA Ops:
  7.2 141.9 %copy-start = (bf16[8,2048,48]{1,2,0:T(8,128)(2,1)S(1)}, bf16[8,2048,48]{1,2,0:T(8,128)(2,1)}, u32[]{:S(2)}) copy-start(bf16[8,2048,48]{1,2,0:T(8,128)(2,1)} %param.36) | copy-start | bytes 4718596
  7.2 102.5 %all-gather.8.cloned.1.call-start = ((), (), s32[]{:S(2)}) async-start(), calls=%async_computation.1 | async-start | bytes 18382848 | tf_op jit(solution)/shard_map/all_gather | solution.py:654
  15.3 94.7 %copy-start.5 = (bf16[384,2048]{1,0:T(8,128)(2,1)S(1)}, bf16[384,2048]{1,0:T(8,128)(2,1)}, u32[]{:S(2)}) copy-start(bf16[384,2048]{1,0:T(8,128)(2,1)} %x_ref.1) | copy-start | bytes 4718596
  15.3 101.1 %copy-start.61 = (f32[2,256]{1,0:T(2,128)S(1)}, f32[2,256]{1,0:T(2,128)}, u32[]{:S(2)}) copy-start(f32[2,256]{1,0:T(2,128)} %refs_13_.1) | copy-start | bytes 6148
  15.3 101.6 %copy-start.24 = (f32[6,2048]{1,0:T(8,128)S(1)}, f32[6,2048]{1,0:T(8,128)}, u32[]{:S(2)}) copy-start(f32[6,2048]{1,0:T(8,128)} %gain_ref.9) | copy-start | bytes 147460
  15.3 245.0 %all-gather.10.cloned.1.call-start = ((), (), s32[]{:S(2)}) async-start(), calls=%async_computation.2 | async-start | bytes 28966912 | tf_op jit(solution)/shard_map/all_gather | solution.py:654
  109.7 249.7 %all-gather.12.cloned.1.call-start = ((), (), s32[]{:S(2)}) async-start(), calls=%async_computation.3 | async-start | bytes 20054016 | tf_op jit(solution)/shard_map/all_gather | solution.py:654
  110.0 36.7 %collective-permute-start = (bf16[384,2048]{1,0:T(8,128)(2,1)S(1)}, bf16[384,2048]{1,0:T(8,128)(2,1)}, u32[]{:S(2)}, u32[]{:S(2)}) collective-permute-start(bf16[384,2048]{1,0:T(8,128)(2,1)S(1)} %copy-done.5), channel_id=1, source_target_pairs={{0,1},{1,0},{2,3},{3,2},{4,5},{5,4},{6,7},{7,6},{8,9},{9,8},{10,11... | collective-permute-start | bytes 4718600 | tf_op jit(solution)/shard_map/ppermute | solution.py:633
  117.6 33.4 %copy-start.56 = (f32[1,2048]{1,0:T(1,128)}, f32[1,2048]{1,0:T(1,128)S(1)}, u32[]{:S(2)}) copy-start(f32[1,2048]{1,0:T(1,128)S(1)} %get-tuple-element.184) | copy-start | bytes 24580
  218.5 36.2 %collective-permute-start.1 = (bf16[384,2048]{1,0:T(8,128)(2,1)}, bf16[384,2048]{1,0:T(8,128)(2,1)}, u32[]{:S(2)}, u32[]{:S(2)}) collective-permute-start(bf16[384,2048]{1,0:T(8,128)(2,1)} %dynamic-slice_convert_fusion), channel_id=1, source_target_pairs={{0,1},{1,0},{2,3},{3,2},{4,5},{5,4},{6,7},{7,6},{8,9},{9,8},{10,11... | collective-permute-start | bytes 4718600 | tf_op jit(solution)/shard_map/ppermute | solution.py:633
  260.3 436.1 %all-gather.14.cloned.1.call-start = ((), (), s32[]{:S(2)}) async-start(), calls=%async_computation.4 | async-start | bytes 6893568 | tf_op jit(solution)/shard_map/all_gather | solution.py:787
  260.4 35.1 %collective-permute-start.2 = (bf16[384,2048]{1,0:T(8,128)(2,1)S(1)}, bf16[384,2048]{1,0:T(8,128)(2,1)}, u32[]{:S(2)}, u32[]{:S(2)}) collective-permute-start(bf16[384,2048]{1,0:T(8,128)(2,1)S(1)} %get-tuple-element.167), channel_id=1, source_target_pairs={{0,1},{1,0},{2,3},{3,2},{4,5},{5,4},{6,7},{7,6},{8,9},{9,8},{10,11... | collective-permute-start | bytes 4718600 | tf_op jit(solution)/shard_map/ppermute | solution.py:633
  375.3 20.0 %collective-permute-start.4 = (bf16[192,2048]{1,0:T(8,128)(2,1)}, bf16[192,2048]{1,0:T(8,128)(2,1)S(1)}, u32[]{:S(2)}, u32[]{:S(2)}) collective-permute-start(bf16[192,2048]{1,0:T(8,128)(2,1)} %get-tuple-element.78), channel_id=1, source_target_pairs={{0,1},{1,0},{2,3},{3,2},{4,5},{5,4},{6,7},{7,6},{8,9},{9,8},{10,11... | collective-permute-start | bytes 2359304 | tf_op jit(solution)/shard_map/ppermute | solution.py:633
  392.6 19.7 %collective-permute-start.3 = (bf16[192,2048]{1,0:T(8,128)(2,1)}, bf16[192,2048]{1,0:T(8,128)(2,1)S(1)}, u32[]{:S(2)}, u32[]{:S(2)}) collective-permute-start(bf16[192,2048]{1,0:T(8,128)(2,1)} %get-tuple-element.76), channel_id=1, source_target_pairs={{0,1},{1,0},{2,3},{3,2},{4,5},{5,4},{6,7},{7,6},{8,9},{9,8},{10,11... | collective-permute-start | bytes 2359304 | tf_op jit(solution)/shard_map/ppermute | solution.py:633
  421.4 20.7 %collective-permute-start.5 = (bf16[192,2048]{1,0:T(8,128)(2,1)}, bf16[192,2048]{1,0:T(8,128)(2,1)S(1)}, u32[]{:S(2)}, u32[]{:S(2)}) collective-permute-start(bf16[192,2048]{1,0:T(8,128)(2,1)} %get-tuple-element.82.own_ref), channel_id=1, source_target_pairs={{0,1},{1,0},{2,3},{3,2},{4,5},{5,4},{6,7},{7,6},{8,9},{9,8},{10,11... | collective-permute-start | bytes 2359304 | tf_op jit(solution)/shard_map/ppermute | solution.py:633
  424.3 55.4 %collective-permute-start.7 = (bf16[192,2048]{1,0:T(8,128)(2,1)S(1)}, bf16[192,2048]{1,0:T(8,128)(2,1)S(1)}, u32[]{:S(2)}, u32[]{:S(2)}) collective-permute-start(bf16[192,2048]{1,0:T(8,128)(2,1)S(1)} %copy-done.33), channel_id=1, source_target_pairs={{0,1},{1,0},{2,3},{3,2},{4,5},{5,4},{6,7},{7,6},{8,9},{9,8},{10,11... | collective-permute-start | bytes 2359304 | tf_op jit(solution)/shard_map/ppermute | solution.py:633
  478.3 38.0 %copy-start.45 = (f32[16,4096]{1,0:T(8,128)S(1)}, f32[16,4096]{1,0:T(8,128)}, u32[]{:S(2)}) copy-start(f32[16,4096]{1,0:T(8,128)} %get-tuple-element.100) | copy-start | bytes 786436
  478.3 38.0 %copy-start.46 = (f32[16,4096]{1,0:T(8,128)S(1)}, f32[16,4096]{1,0:T(8,128)}, u32[]{:S(2)}) copy-start(f32[16,4096]{1,0:T(8,128)} %get-tuple-element.102) | copy-start | bytes 786436
  478.3 61.1 %collective-permute-start.6 = (bf16[192,2048]{1,0:T(8,128)(2,1)}, bf16[192,2048]{1,0:T(8,128)(2,1)S(1)}, u32[]{:S(2)}, u32[]{:S(2)}) collective-permute-start(bf16[192,2048]{1,0:T(8,128)(2,1)} %get-tuple-element.86), channel_id=1, source_target_pairs={{0,1},{1,0},{2,3},{3,2},{4,5},{5,4},{6,7},{7,6},{8,9},{9,8},{10,11... | collective-permute-start | bytes 2359304 | tf_op jit(solution)/shard_map/ppermute | solution.py:633
  515.6 16.4 %collective-permute-start.8 = (bf16[192,2048]{1,0:T(8,128)(2,1)}, bf16[192,2048]{1,0:T(8,128)(2,1)S(1)}, u32[]{:S(2)}, u32[]{:S(2)}) collective-permute-start(bf16[192,2048]{1,0:T(8,128)(2,1)} %get-tuple-element.90), channel_id=1, source_target_pairs={{0,1},{1,0},{2,3},{3,2},{4,5},{5,4},{6,7},{7,6},{8,9},{9,8},{10,11... | collective-permute-start | bytes 2359304 | tf_op jit(solution)/shard_map/ppermute | solution.py:633
  539.1 20.8 %collective-permute-start.9 = (bf16[192,2048]{1,0:T(8,128)(2,1)}, bf16[192,2048]{1,0:T(8,128)(2,1)}, u32[]{:S(2)}, u32[]{:S(2)}) collective-permute-start(bf16[192,2048]{1,0:T(8,128)(2,1)} %get-tuple-element.103.refs_0_), channel_id=1, source_target_pairs={{0,1},{1,0},{2,3},{3,2},{4,5},{5,4},{6,7},{7,6},{8,9},{9,8},{10,11... | collective-permute-start | bytes 2359304 | tf_op jit(solution)/shard_map/ppermute | solution.py:633
  546.6 24.8 %collective-permute-start.10 = (bf16[192,2048]{1,0:T(8,128)(2,1)}, bf16[192,2048]{1,0:T(8,128)(2,1)}, u32[]{:S(2)}, u32[]{:S(2)}) collective-permute-start(bf16[192,2048]{1,0:T(8,128)(2,1)} %get-tuple-element.104.refs_1_), channel_id=1, source_target_pairs={{0,1},{1,0},{2,3},{3,2},{4,5},{5,4},{6,7},{7,6},{8,9},{9,8},{10,11... | collective-permute-start | bytes 2359304 | tf_op jit(solution)/shard_map/ppermute | solution.py:633
  613.6 75.0 %collective-permute-start.11 = (bf16[384,2048]{1,0:T(8,128)(2,1)}, bf16[384,2048]{1,0:T(8,128)(2,1)}, u32[]{:S(2)}, u32[]{:S(2)}) collective-permute-start(bf16[384,2048]{1,0:T(8,128)(2,1)} %add_convert_fusion), channel_id=1, source_target_pairs={{0,1},{1,0},{2,3},{3,2},{4,5},{5,4},{6,7},{7,6},{8,9},{9,8},{10,11... | collective-permute-start | bytes 4718600 | tf_op jit(solution)/shard_map/ppermute | solution.py:633
  666.3 17.9 %all-to-all-start = ((bf16[32,64,113]{2,1,0:T(8,128)(2,1)}), bf16[32,64,113]{2,1,0:T(8,128)(2,1)S(1)}, u32[]{:S(2)}, u32[]{:S(2)}) async-start(bf16[32,64,113]{2,1,0:T(8,128)(2,1)} %bitcast.141), calls=%async_computation | async-start | bytes 1048576 | tf_op jit(solution)/shard_map/all_to_all | solution.py:842
  (57 other events, 424.4 us)
Sparse Core Ops, SparseCore 0:
  15.4 94.2 all-gather.7
  111.9 138.4 all-gather.9
  260.4 98.9 all-gather.11
  571.5 66.4 all-gather.13

commit v2 on v1

--- a/solution.py
+++ b/solution.py
@@ -91,9 +91,7 @@
             out[:, b * FB + 2 * UB : (b + 1) * FB] = down_ref[cs, :].T
         at = count * FB
         for ref, (value, n) in zip(refs[:-1], rest):
-            if value.ndim == 3:
-                out[:, at : at + n] = ref[:, 0, :]
-            elif value.shape[0] == rows and value.shape[1] == n:
+            if value.shape == (rows, n):
                 out[:, at : at + n] = ref[...]
             else:
                 out[:, at : at + n] = ref[...].T
@@ -227,23 +225,33 @@
     )(*args)
 
 
-def ffn_bwd(own, peer, packs, counts, g_pre, u_pre, bgu, ad_t, bd, u_t, a_in_t, rb):
+def ffn_bwd(own, peer, packs, counts, first, g_pre, u_pre, bgu, ad_t, bd, u_t, a_in_t, rb, prev, last):
     half, width = own.shape
     r = 2 * half
     units = ad_t.shape[1]
-    blocks = units // UB
-
-    def body(
-        own_ref, peer_ref, p0, p1, p2, g_ref, u_ref, bgu_ref, ad_ref, bd_ref, ut_ref,
-        ain_ref, own_out, peer_out, dbg_out, dbu_out, gad_out, du_out,
-        df, acc, wbuf, dd, du, dgu, hs, sem,
-    ):
+    blocks = sum(counts)
+    sub = 256
+
+    def body(*refs):
+        own_ref, peer_ref, g_ref, u_ref, bgu_ref, ad_ref, bd_ref, ut_ref, ain_ref = refs[:9]
+        pack_refs = refs[9 : 9 + len(packs)]
+        at = 9 + len(packs)
+        if prev is not None:
+            acc_in, du_in = refs[at : at + 2]
+            at += 5
+        if last:
+            dbg_out, dbu_out, gad_out, du_out, own_out, peer_out = refs[at : at + 6]
+            at += 6
+        else:
+            dbg_out, dbu_out, gad_out, du_out, acc_out = refs[at : at + 5]
+            at += 5
+        df, acc, wbuf, dd, du, dgu, hs, sem = refs[at:]
         j = pl.program_id(0)
         slot = lax.rem(j, 2)
 
         def fetch(step, where):
             base = 0
-            for ref, count in zip((p0, p1, p2), counts):
+            for ref, count in zip(pack_refs, counts):
                 low = base
 
                 @pl.when((step >= low) & (step < low + count))
@@ -260,17 +268,22 @@
             fetch(j, 0)
             df[0:half, :] = own_ref[...]
             df[half:r, :] = peer_ref[...]
-            acc[...] = jnp.zeros_like(acc)
-            du[...] = jnp.zeros_like(du)
+            if prev is None:
+                acc[...] = jnp.zeros_like(acc)
+                du[...] = jnp.zeros_like(du)
+            else:
+                acc[...] = acc_in[...]
+                du[...] = du_in[...]
             dd[...] = dot_nt(df[...], bd_ref[...]).astype(BF16)
 
         @pl.when(j + 1 < blocks)
         def _():
             fetch(j + 1, 1 - slot)
 
-        pltpu.make_async_copy(p0.at[:, pl.ds(0, FB)], wbuf.at[slot], sem.at[slot]).wait()
-
-        sub = 256
+        pltpu.make_async_copy(
+            pack_refs[0].at[:, pl.ds(0, FB)], wbuf.at[slot], sem.at[slot]
+        ).wait()
+
         for n in range(UB // sub):
             cs = slice(n * sub, (n + 1) * sub)
             dh = dot(df[...], wbuf[slot, :, 2 * UB + n * sub : 2 * UB + (n + 1) * sub])
@@ -293,48 +306,49 @@
 
         @pl.when(j == blocks - 1)
         def _():
-            total = acc[...] + dot(du[...].astype(BF16), ain_ref[...])
-            own_out[...] = total[:half]
-            peer_out[...] = total[half:].astype(BF16)
             du_out[...] = du[...]
-
-    rows_block = lambda: pl.BlockSpec((r, UB), lambda j: (rb, j))
-    unit_block = lambda: pl.BlockSpec((RANK, UB), lambda j: (0, j))
-    row_const = lambda n: pl.BlockSpec((r, n), lambda j: (rb, 0), pipeline_mode=pl.Buffered(1))
+            if last:
+                total = acc[...] + dot(du[...].astype(BF16), ain_ref[...])
+                own_out[...] = total[:half]
+                peer_out[...] = total[half:].astype(BF16)
+            else:
+                acc_out[...] = acc[...]
+
+    rows_block = lambda: pl.BlockSpec((r, UB), lambda j: (rb, first + j))
+    unit_block = lambda: pl.BlockSpec((RANK, UB), lambda j: (0, first + j))
     shape = jax.ShapeDtypeStruct
+    in_specs = [
+        const_spec((half, width)),
+        const_spec((half, width)),
+        rows_block(),
+        rows_block(),
+        pl.BlockSpec((2 * RANK, 2 * UB), lambda j: (0, first + j)),
+        unit_block(),
+        const_spec((RANK, width)),
+        pl.BlockSpec((2 * RANK, r), lambda j: (0, rb), pipeline_mode=pl.Buffered(1)),
+        const_spec((2 * RANK, width)),
+    ] + [any_spec() for _ in packs]
+    args = [own, peer, g_pre, u_pre, bgu, ad_t, bd, u_t, a_in_t, *packs]
+    aliases = {}
+    if prev is not None:
+        at = len(args)
+        in_specs += [const_spec((r, width)), const_spec((r, 2 * RANK))] + [any_spec()] * 3
+        args += list(prev)
+        aliases = {at + 2: 0, at + 3: 1, at + 4: 2}
+    out_specs = [unit_block(), unit_block(), unit_block(), const_spec((r, 2 * RANK))]
+    out_shape = [shape((RANK, units), F32)] * 3 + [shape((r, 2 * RANK), F32)]
+    if last:
+        out_specs += [const_spec((half, width)), const_spec((half, width))]
+        out_shape += [shape((half, width), F32), shape((half, width), BF16)]
+    else:
+        out_specs += [const_spec((r, width))]
+        out_shape += [shape((r, width), F32)]
     return pl.pallas_call(
         body,
         grid=(blocks,),
-        in_specs=[
-            const_spec((half, width)),
-            const_spec((half, width)),
-            any_spec(),
-            any_spec(),
-            any_spec(),
-            rows_block(),
-            rows_block(),
-            pl.BlockSpec((2 * RANK, 2 * UB), lambda j: (0, j)),
-            unit_block(),
-            const_spec((RANK, width)),
-            pl.BlockSpec((2 * RANK, r), lambda j: (0, rb), pipeline_mode=pl.Buffered(1)),
-            const_spec((2 * RANK, width)),
-        ],
-        out_specs=[
-            const_spec((half, width)),
-            const_spec((half, width)),
-            unit_block(),
-            unit_block(),
-            unit_block(),
-            const_spec((r, 2 * RANK)),
-        ],
-        out_shape=[
-            shape((half, width), F32),
-            shape((half, width), BF16),
-            shape((RANK, units), F32),
-            shape((RANK, units), F32),
-            shape((RANK, units), F32),
-            shape((r, 2 * RANK), F32),
-        ],
+        in_specs=in_specs,
+        out_specs=out_specs,
+        out_shape=out_shape,
         scratch_shapes=[
             pltpu.VMEM((r, width), BF16),
             pltpu.VMEM((r, width), F32),
@@ -345,14 +359,15 @@
             pltpu.VMEM((r, UB), BF16),
             pltpu.SemaphoreType.DMA((2,)),
         ],
+        input_output_aliases=aliases,
         compiler_params=params(),
         cost_estimate=pl.CostEstimate(
-            flops=6 * r * width * units,
-            bytes_accessed=6 * width * units,
-            transcendentals=r * units,
+            flops=6 * r * width * UB * blocks,
+            bytes_accessed=6 * width * UB * blocks,
+            transcendentals=r * UB * blocks,
         ),
         name="ffn_bwd",
-    )(own, peer, *packs, g_pre, u_pre, bgu, ad_t, bd, u_t, a_in_t)
+    )(*args)
 
 
 def ple_both(combined, ffn_own, ffn_recv, out_grad, ple_in, packed, column, gains, prev, rb):
@@ -548,8 +563,8 @@
         ],
         compiler_params=params(),
         cost_estimate=pl.CostEstimate(
-            flops=2 * length * width * q_width + 8 * heads * length * WIN * HD,
-            bytes_accessed=24 * 1024 * 1024,
+            flops=1024 * 1024,
+            bytes_accessed=1024 * 1024,
             transcendentals=0,
         ),
         name="attention_bwd",
@@ -577,6 +592,45 @@
         ),
         name="final_bwd",
     )(x, d_norm, d_branch, dh_own, dh_recv, gains)
+
+
+def ffn_adapter_sums(got, onehot, units):
+    seqs = got.shape[0]
+    adapters = onehot.shape[0]
+    tile = 512
+
+    def body(hot_ref, got_ref, out_ref, down_ref):
+        for a in range(adapters):
+            total = hot_ref[a, 0] * got_ref[0].astype(F32)
+            for s in range(1, seqs):
+                total += hot_ref[a, s] * got_ref[s].astype(F32)
+            out_ref[a, :, 0, :] = total[:RANK]
+            out_ref[a, :, 1, :] = total[RANK : 2 * RANK]
+            down_ref[a] = total[2 * RANK :]
+
+    return pl.pallas_call(
+        body,
+        grid=(units // tile,),
+        in_specs=[
+            pl.BlockSpec(memory_space=pltpu.SMEM),
+            pl.BlockSpec((seqs, 3 * RANK, tile), lambda i: (0, 0, i)),
+        ],
+        out_specs=[
+            pl.BlockSpec((adapters, RANK, 2, tile), lambda i: (0, 0, 0, i)),
+            pl.BlockSpec((adapters, RANK, tile), lambda i: (0, 0, i)),
+        ],
+        out_shape=[
+            jax.ShapeDtypeStruct((adapters, RANK, 2, units), F32),
+            jax.ShapeDtypeStruct((adapters, RANK, units), F32),
+        ],
+        compiler_params=params(),
+        cost_estimate=pl.CostEstimate(
+            flops=6 * adapters * seqs * RANK * units,
+            bytes_accessed=6 * seqs * RANK * units,
+            transcendentals=0,
+        ),
+        name="adapter_sums",
+    )(onehot, got)
 
 
 def rope_tables(length):
@@ -648,7 +702,7 @@
     pd = per_layer_gate.shape[1]
     pack_1 = pack_blocks(
         weight_gate_up, weight_down, 0, counts[0],
-        [(weight_qkv, qkv_width), (weight_attn_out, q_width), (laurel_left, lr), (laurel_right, lr)],
+        [(weight_qkv[:, 0, :], qkv_width), (weight_attn_out, q_width), (laurel_left.T, lr), (laurel_right, lr)],
         width, "pack_1",
     )
     gather = lambda v: lax.all_gather(v, "dp", axis=0, tiled=True)
@@ -661,8 +715,6 @@
     pack_3 = pack_blocks(
         weight_gate_up, weight_down, counts[0] + counts[1], counts[2], [], width, "pack_3"
     )
-    pack_2, _ = lax.optimization_barrier((pack_2, full_1))
-    full_2 = gather(pack_2)
     w_qkv = full_1[:, FB : FB + qkv_width]
     wo_at = FB + qkv_width
     w_o_t = full_1[:, wo_at : wo_at + q_width]
@@ -695,6 +747,8 @@
     x_all = in_order(hidden_in, x_peer)
     h_all = normed(x_all.astype(F32), norm_gains[0]).astype(BF16)
     u_qkv = dot(h_all, qkv_in).astype(BF16)
+    pack_2, _, h_all, u_qkv, bgu = lax.optimization_barrier((pack_2, full_1, h_all, u_qkv, bgu))
+    full_2 = gather(pack_2)
     raw = dot(h_all, w_qkv) + dot(u_qkv, b_qkv)
     q_raw = raw[:, :q_width].reshape(length, per_group, HD)
     k_raw = raw[:, q_width : q_width + HD]
@@ -738,8 +792,7 @@
         h2, full_2, counts[1], counts[0], u_ffn, bgu, ad_t, b_d, (acc, ud, g_pre, u_pre), None
     )
     at = counts[0] + counts[1]
-    fwd_parts, ud_parts, ple_parts, bwd_parts = [], [], [], []
-    d_ffn_parts, d_attn_own, d_attn_peer = [], [], []
+    fwd_parts, ud_parts, ple_parts = [], [], []
     for s in range(2):
         g_pre, u_pre, own, peer, ud_s = ffn_fwd(
             h2, full_3, counts[2], at, u_ffn, bgu, ad_t, b_d, (acc, ud, g_pre, u_pre), s
@@ -755,23 +808,37 @@
         )
         layer_out = [whole]
         ple_parts.append((d_ffn_s, swap(d_ffn_s), d_first_s))
-    packs = (full_1, full_2, full_3)
-    branch = []
-    for s in range(2):
-        d_ffn_s, d_ffn_recv, d_first_s = ple_parts[s]
-        got = ffn_bwd(
-            d_ffn_s, d_ffn_recv, packs, counts, g_pre, u_pre, bgu, ad_t, b_d, u_ffn.T, a_ffn.T, s
-        )
-        bwd_parts.append(got[2:])
-        d_ffn_parts += [d_ffn_s, d_ffn_recv]
-        d_h2_recv = swap(got[1])
-        d_attn_s, *branch = between_bwd(
-            d_first_s, combined, got[0], d_h2_recv, attn_proj, laurel_low, full_1,
-            lau_at // (2 * lr), norm_gains, branch, s,
-        )
-        d_attn_own.append(d_attn_s)
-        d_attn_peer.append(swap(d_attn_s))
+    common = (g_pre, u_pre, bgu, ad_t, b_d, u_ffn.T, a_ffn.T)
+    lau_column = lau_at // (2 * lr)
+    (own_0, recv_0, first_0), (own_1, recv_1, first_1) = ple_parts
+    d_ffn_parts = [own_0, recv_0, own_1, recv_1]
+    *grads_0, d_h2_own_0, d_h2_peer_0 = ffn_bwd(
+        own_0, recv_0, (full_1, full_2, full_3), counts, 0, *common, 0, None, True
+    )
+    d_h2_recv_0 = swap(d_h2_peer_0)
+    own_1, _ = lax.optimization_barrier((own_1, d_h2_peer_0))
+    dbg_1, dbu_1, gad_1, du_1, acc_1 = ffn_bwd(
+        own_1, recv_1, (full_1, full_2), counts[:2], 0, *common, 1, None, False
+    )
+    d_h2_recv_0, acc_1 = lax.optimization_barrier((d_h2_recv_0, acc_1))
+    d_attn_0, *branch = between_bwd(
+        first_0, combined, d_h2_own_0, d_h2_recv_0, attn_proj, laurel_low, full_1, lau_column,
+        norm_gains, [], 0,
+    )
+    d_attn_recv_0 = swap(d_attn_0)
+    acc_1, _ = lax.optimization_barrier((acc_1, d_attn_0))
+    *grads_1, d_h2_own_1, d_h2_peer_1 = ffn_bwd(
+        own_1, recv_1, (full_3,), counts[2:], at, *common, 1, (acc_1, du_1, dbg_1, dbu_1, gad_1),
+        True,
+    )
+    d_attn_1, *branch = between_bwd(
+        first_1, combined, d_h2_own_1, swap(d_h2_peer_1), attn_proj, laurel_low, full_1,
+        lau_column, norm_gains, branch, 1,
+    )
     d_branch, d_norm = branch
+    bwd_parts = [grads_0, grads_1]
+    d_attn_own = [d_attn_0, d_attn_1]
+    d_attn_peer = [d_attn_recv_0, swap(d_attn_1)]
 
     tag = jnp.full((1, 128), a, BF16)
 
@@ -779,15 +846,17 @@
         return (ids[None, :] == jnp.arange(adapters, dtype=F32)[:, None]).astype(BF16)
 
     def over_sequences(grad):
-        n, m = grad.shape
-        send = jnp.concatenate([grad.astype(BF16), jnp.broadcast_to(tag, (n, 128))], axis=1)
-        return send
-
-    def summed(send):
+        return jnp.concatenate(
+            [grad.astype(BF16), jnp.broadcast_to(tag, (grad.shape[0], 128))], axis=1
+        )
+
+    def gathered(send):
         got = lax.all_gather(send, "dp", axis=0, tiled=False)
-        onehot = onehot_of(got[:, 0, send.shape[1] - 1].astype(F32))
-        got = got[:, :, : send.shape[1] - 128]
-        return jnp.einsum("as,snm->anm", onehot, got, preferred_element_type=F32)
+        return got, onehot_of(got[:, 0, send.shape[1] - 1].astype(F32))
+
+    def summed(send, m):
+        got, onehot = gathered(send)
+        return jnp.einsum("as,snm->anm", onehot, got[:, :, :m], preferred_element_type=F32)
 
     send_ffn = over_sequences(
         jnp.concatenate(
@@ -799,10 +868,17 @@
             axis=0,
         )
     )
-
+    send_ffn, d_attn_peer[0] = lax.optimization_barrier((send_ffn, d_attn_peer[0]))
+    got_ffn, hot_ffn = gathered(send_ffn)
+
+    d_ffn_all = jnp.concatenate(d_ffn_parts, axis=0)
+    du_ffn = jnp.concatenate([bwd_parts[0][3], bwd_parts[1][3]], axis=0).astype(BF16)
+    ud_low = jnp.concatenate(ud_parts, axis=0).astype(BF16)
+    shared_ffn = jnp.concatenate(
+        [dot_tn(h2, du_ffn).astype(BF16), (2.0 * dot_tn(d_ffn_all, ud_low)).astype(BF16)], axis=1
+    )
     pieces = d_attn_own + d_attn_peer
-    pieces, send_ffn = lax.optimization_barrier((pieces, send_ffn))
-    sum_ffn = summed(send_ffn)
+    pieces, _, shared_ffn = lax.optimization_barrier((pieces, send_ffn, shared_ffn))
     d_raw, du_attn = attention_bwd(
         pieces, t.astype(jnp.int32).reshape(1), full_1, wo_at // HD, b_o, a_o.T, queries, keys,
         values, probs, raw, head_gains, cos, sin,
@@ -810,50 +886,48 @@
     d_u = dot_nt(d_raw, b_qkv).astype(BF16)
     d_h_peer = (dot_nt(theirs(d_raw), w_qkv) + dot_nt(theirs(d_u), qkv_in)).astype(BF16)
     d_h_recv = swap(d_h_peer)
-    d_raw, d_u, _ = lax.optimization_barrier((d_raw, d_u, d_h_peer))
+    d_raw, d_u, _, got_ffn = lax.optimization_barrier((d_raw, d_u, d_h_peer, got_ffn))
+
+    d_attn_all = in_order(
+        jnp.concatenate(d_attn_own, axis=0), jnp.concatenate(d_attn_peer, axis=0)
+    )
+    send = jnp.concatenate(
+        [
+            shared_ffn,
+            (2.0 * dot_tn(d_attn_all, u_attn)).astype(BF16),
+            dot_tn(h_all, d_u).astype(BF16),
+            jnp.broadcast_to(tag[:, :1], (width, 1)),
+        ],
+        axis=1,
+    )
+    got = lax.all_to_all(send, ("dp", "tensor"), 0, 0, tiled=True).reshape(2 * dp, -1, send.shape[1])
     grad_b = 2.0 * dot_tn(u_qkv, d_raw)
-    grad_qkv_out = jnp.concatenate(
+    grad_heads = jnp.concatenate(
         [
             grad_b[:RANK, :q_width],
             grad_b[RANK : 2 * RANK, q_width : q_width + HD],
             grad_b[2 * RANK :, q_width + HD :],
+            dot_tn(du_attn.astype(BF16), context),
         ],
         axis=1,
     )
-    sum_qkv_out = summed(over_sequences(grad_qkv_out))
-    sum_attn_in = summed(over_sequences(dot_tn(du_attn.astype(BF16), context)))
-
-    d_attn_all = in_order(
-        jnp.concatenate(d_attn_own, axis=0), jnp.concatenate(d_attn_peer, axis=0)
-    )
-    d_ffn_all = jnp.concatenate(d_ffn_parts, axis=0)
-    du_ffn = jnp.concatenate([bwd_parts[0][3], bwd_parts[1][3]], axis=0).astype(BF16)
-    ud_low = jnp.concatenate(ud_parts, axis=0).astype(BF16)
-    send = jnp.concatenate(
-        [
-            dot_tn(h2, du_ffn).astype(BF16),
-            (2.0 * dot_tn(d_ffn_all, ud_low)).astype(BF16),
-            (2.0 * dot_tn(d_attn_all, u_attn)).astype(BF16),
-            dot_tn(h_all, d_u).astype(BF16),
-            jnp.broadcast_to(tag[:, :1], (width, 1)),
-        ],
-        axis=1,
-    )
-    got = lax.all_to_all(send, ("dp", "tensor"), 0, 0, tiled=True).reshape(2 * dp, -1, send.shape[1])
+    sum_heads = summed(over_sequences(grad_heads), qkv_width + q_width)
+    d_h_own = dot_nt(mine(d_raw), w_qkv) + dot_nt(mine(d_u), qkv_in)
+    out_ffn_out, out_down_in = ffn_adapter_sums(got_ffn, hot_ffn.astype(F32), units)
+    d_h_own, out_ffn_out, out_down_in = lax.optimization_barrier((d_h_own, out_ffn_out, out_down_in))
     onehot = onehot_of(got[:, 0, send.shape[1] - 1].astype(F32))
     shared = jnp.einsum("as,snm->anm", onehot, got, preferred_element_type=F32)
-    d_h_own = dot_nt(mine(d_raw), w_qkv) + dot_nt(mine(d_u), qkv_in)
     input_grad = final_bwd(hidden_in, d_norm, d_branch, d_h_own, d_h_recv, norm_gains)
     return (
         layer_out[0],
         input_grad,
         shared[:, :, 4 * RANK : 7 * RANK],
-        sum_qkv_out.reshape(adapters, RANK, 1, qkv_width),
-        jnp.swapaxes(sum_attn_in, 1, 2),
+        sum_heads[:, :, None, :qkv_width],
+        jnp.swapaxes(sum_heads[:, :, qkv_width:], 1, 2),
         jnp.swapaxes(shared[:, :, 3 * RANK : 4 * RANK], 1, 2),
         shared[:, :, : 2 * RANK],
-        jnp.stack([sum_ffn[:, :RANK], sum_ffn[:, RANK : 2 * RANK]], axis=2),
-        jnp.swapaxes(sum_ffn[:, 2 * RANK :], 1, 2),
+        out_ffn_out,
+        jnp.swapaxes(out_down_in, 1, 2),
         jnp.swapaxes(shared[:, :, 2 * RANK : 3 * RANK], 1, 2),
     )
 

time: 735 us -> 655 us (0.89)
  blocking collectives: 44.2 us -> 0 us
  waiting for transfers between devices: 248 us -> 204 us
  Pallas kernels: 219 us -> 238 us
  local copies, waits for them, and re-layouts: 69.9 us -> 52.8 us
    all_gather x2 -> x0, blocking collectives: 44.2 us -> none  [summed(): got = lax.all_gather(send, 'dp', axis=0, tiled=False)]
    ppermute x12, waiting for transfers between devices: 142 us -> 116 us  [swap(): return lax.ppermute(v, 'tensor', [(0, 1), (1, 0)])]
    pallas_call x2 -> x4, Pallas kernels: 70.2 us -> 90.7 us  [the longest x3 77.8 us: ffn_bwd(): pl.pallas_call(body, grid=(blocks,), in_specs=in_specs, out_specs=out_spe...]
    all_gather x3, waiting for transfers between devices: 101 us -> 87.5 us  [on_device(): gather = lambda v: lax.all_gather(v, 'dp', axis=0, tiled=True)]
    unnamed x143 -> x115, local copies, waits for them, and re-layouts: 34.2 us -> 22.4 us
    dot_general x3 -> x1, matrix products: 10.6 us -> 1.49 us  [summed(): jnp.einsum('as,snm->anm', onehot, got[:, :, :m], preferred_element_type=F32)]
  transfers between devices with their start and end apart: 17 -> 18, of which waited for: 12 -> 12; matrix products, arithmetic and copies ran while one was open for 19% -> 23% of each run, Pallas kernels for 26% -> 33%
where the time goes in v2:
time: 655 us; the launch traced here: 648 us
  Pallas kernels  238 us (36%)
  waiting for transfers between devices  204 us (31%)
  matrix products  60.1 us (9%)
  other arithmetic  54.9 us (8%)
  local copies, waits for them, and re-layouts  52.8 us (8%)
  starting transfers between devices  22.3 us (3%)
  between operations  15.8 us (2%)
    ppermute x12, waiting for transfers between devices, swap(): return lax.ppermute(v, 'tensor', [(0, 1), (1, 0)])  116 us
    all_gather x3, waiting for transfers between devices, on_device(): gather = lambda v: lax.all_gather(v, 'dp', axis=0, tiled=True)  87.5 us
    pallas_call x3, Pallas kernels, ffn_bwd(): pl.pallas_call(body, grid=(blocks,), in_specs=in_specs, out_specs=out_spe...  77.8 us
    pallas_call x4, Pallas kernels, ffn_fwd(): pl.pallas_call(body, grid=(blocks,), in_specs=in_specs, out_specs=out_spe...  77.2 us
    dot_general x7, matrix products, dot_nt(): lax.dot_general(a, b, (((1,), (1,)), ((), ())), preferred_element_type=F32)  23.9 us
    unnamed x115, local copies, waits for them, and re-layouts  22.4 us
    pallas_call x1, Pallas kernels, attention_bwd(): pl.pallas_call(body, grid=(heads,), in_specs=[pl.BlockSpec(memory_space=p...  21.1 us
    ppermute x12, starting transfers between devices, swap(): return lax.ppermute(v, 'tensor', [(0, 1), (1, 0)])  17.9 us
  transfers between devices with their start and end apart: 18, of which 12 were waited for; matrix products, arithmetic and copies ran while one was open for 23% of the time, Pallas kernels for 33%

profile of v2, /device:TPU:0, one launch (start us, length us, event | category | flops | bytes accessed | tf_op | source)
XLA Modules:
  0.0 647.7 jit_solution(8319024282016334416)
XLA Ops:
  26.7 21.4 %collective-permute-done = bf16[384,2048]{1,0:T(8,128)(2,1)} collective-permute-done((bf16[384,2048]{1,0:T(8,128)(2,1)S(1)}, bf16[384,2048]{1,0:T(8,128)(2,1)}, u32[]{:S(2)}, u32[]{:S(2)}) %collective-permute-start) | collective-permute-done | bytes 1572896 | tf_op jit(solution)/shard_map/ppermute | solution.py:687
  53.9 51.0 %all-gather.8.cloned.1.call-done.refs_1_.refs_9_.w_ref.refs_4_ = bf16[2048,4224]{1,0:T(8,128)(2,1)} async-done(((bf16[128,4224]{1,0:T(8,128)(2,1)}), bf16[2048,4224]{1,0:T(8,128)(2,1)}) %all-gather.8.cloned.1.call-update) | async-done | bytes 17301520 | tf_op jit(solution)/shard_map/all_gather | solution.py:708
  110.1 8.1 %fusion.9 = f32[768,1536]{1,0:T(8,128)S(1)} fusion(bf16[768,2048]{1,0:T(8,128)(2,1)} %copy-done.4, bf16[2048,4224]{1,0:T(8,128)(2,1)} %all-gather.8.cloned.1.call-done.refs_1_.refs_9_.w_ref.refs_4_), kind=kOutput, calls=%fused_computation.14 | convolution fusion | flops 4831838208 | bytes 14155776 | tf_op jit(solution)/shard_map/dot_general | solution.py:32
  145.7 14.5 %fusion.134 = (f32[4,768]{1,0:T(4,128)S(1)}, f32[4,768,768]{2,1,0:T(8,128)}) fusion(f32[768,768,4]{0,1,2:T(8,128)} %fusion.69, pred[768,768]{1,0:T(8,128)(4,1)S(1)} %copy-done.39), kind=kOutput, calls=%fused_computation.215 | output fusion | flops 14156543 | bytes 19476480 | tf_op jit(solution)/shard_map/sub | solution.py:763
  189.4 27.1 %collective-permute-done.1 = bf16[384,2048]{1,0:T(8,128)(2,1)} collective-permute-done((bf16[384,2048]{1,0:T(8,128)(2,1)}, bf16[384,2048]{1,0:T(8,128)(2,1)}, u32[]{:S(2)}, u32[]{:S(2)}) %collective-permute-start.1) | collective-permute-done | bytes 1572896 | tf_op jit(solution)/shard_map/ppermute | solution.py:687
  222.3 23.3 %all-gather.10.cloned.1.call-done.refs_1_.w_ref.refs_10_ = bf16[2048,6656]{1,0:T(8,128)(2,1)} async-done(((bf16[128,6656]{1,0:T(8,128)(2,1)}), bf16[2048,6656]{1,0:T(8,128)(2,1)}) %all-gather.10.cloned.1.call-update) | async-done | bytes 27262992 | tf_op jit(solution)/shard_map/all_gather | solution.py:708
  250.4 31.9 %collective-permute-done.2 = bf16[384,2048]{1,0:T(8,128)(2,1)S(1)} collective-permute-done((bf16[384,2048]{1,0:T(8,128)(2,1)S(1)}, bf16[384,2048]{1,0:T(8,128)(2,1)S(1)}, u32[]{:S(2)}, u32[]{:S(2)}) %collective-permute-start.2) | collective-permute-done | bytes 1572896 | tf_op jit(solution)/shard_map/ppermute | solution.py:687
  287.4 12.3 %ffn_fwd.4 = (bf16[768,4096]{1,0:T(8,128)(2,1)}, bf16[768,4096]{1,0:T(8,128)(2,1)}, f32[768,2048]{1,0:T(8,128)}, f32[768,16]{1,0:T(8,128)}) custom-call(bf16[768,2048]{1,0:T(8,128)(2,1)} %copy-done.1, bf16[2048,4224]{1,0:T(8,128)(2,1)} %all-gather.8.cloned.1.call-done.refs_1_.refs_9_.w_ref.refs_4_, bf16[768,32]{1,0:T(8,128)(2,1)} %copy.113.refs_2_, ...), custom_call_target="tpu_custom_call" | custom-call | flops 4831838208 | bytes 18874368 | tf_op jit(solution)/shard_map/ffn_fwd/pallas_call | solution.py:206
  299.7 33.1 %ffn_fwd.5 = (bf16[768,4096]{1,0:T(8,128)(2,1)}, bf16[768,4096]{1,0:T(8,128)(2,1)}, f32[768,2048]{1,0:T(8,128)}, f32[768,16]{1,0:T(8,128)}) custom-call(bf16[768,2048]{1,0:T(8,128)(2,1)} %copy-done.1, bf16[2048,6656]{1,0:T(8,128)(2,1)} %all-gather.10.cloned.1.call-done.refs_1_.w_ref.refs_10_, ...), custom_call_target="tpu_custom_call", output_to_operand_aliasing={{0}: (8, {}), {1}: (9, {})} | custom-call | flops 19327352832 | bytes 37748736 | tf_op jit(solution)/shard_map/ffn_fwd/pallas_call | solution.py:206
  332.9 13.3 %all-gather.12.cloned.1.call-done.refs_1_.refs_11_.refs_9_ = bf16[2048,4608]{1,0:T(8,128)(2,1)} async-done(((bf16[128,4608]{1,0:T(8,128)(2,1)}), bf16[2048,4608]{1,0:T(8,128)(2,1)}) %all-gather.12.cloned.1.call-update) | async-done | bytes 18874384 | tf_op jit(solution)/shard_map/all_gather | solution.py:708
  346.1 16.0 %ffn_fwd.6 = (bf16[768,4096]{1,0:T(8,128)(2,1)}, bf16[768,4096]{1,0:T(8,128)(2,1)}, f32[192,2048]{1,0:T(8,128)}, bf16[192,2048]{1,0:T(8,128)(2,1)}, f32[384,16]{1,0:T(8,128)}) custom-call(bf16[768,2048]{1,0:T(8,128)(2,1)} %copy-done.1, ...), custom_call_target="tpu_custom_call", output_to_operand_aliasing={{0}: (8, {}), {1}: (9, {})} | custom-call | flops 7247757312 | bytes 25165824 | tf_op jit(solution)/shard_map/ffn_fwd/pallas_call | solution.py:206
  363.7 15.7 %ffn_fwd.7 = (bf16[768,4096]{1,0:T(8,128)(2,1)}, bf16[768,4096]{1,0:T(8,128)(2,1)}, f32[192,2048]{1,0:T(8,128)}, bf16[192,2048]{1,0:T(8,128)(2,1)}, f32[384,16]{1,0:T(8,128)}) custom-call(bf16[768,2048]{1,0:T(8,128)(2,1)} %copy-done.1, ...), custom_call_target="tpu_custom_call", output_to_operand_aliasing={{0}: (8, {}), {1}: (9, {})} | custom-call | flops 7247757312 | bytes 25165824 | tf_op jit(solution)/shard_map/ffn_fwd/pallas_call | solution.py:206
  383.0 8.2 %ple_both.2 = (bf16[384,2048]{1,0:T(8,128)(2,1)}, bf16[192,2048]{1,0:T(8,128)(2,1)}, f32[192,2048]{1,0:T(8,128)}) custom-call(f32[384,2048]{1,0:T(8,128)} %get-tuple-element.205.c_ref, f32[192,2048]{1,0:T(8,128)} %get-tuple-element.100.fo_ref, bf16[192,2048]{1,0:T(8,128)(2,1)} %copy-done.36, bf16[384,2048]{1,0:T(8,128)(2,1)} %og_ref.3, ...), custom_call_target="tpu_custom_call" | custom-call | flops 805306368 | bytes 7864320 | tf_op jit(solution)/shard_map/ple_both/pallas_call | solution.py:399
  401.0 8.2 %ple_both.3 = (bf16[384,2048]{1,0:T(8,128)(2,1)}, bf16[192,2048]{1,0:T(8,128)(2,1)}, f32[192,2048]{1,0:T(8,128)}) custom-call(f32[384,2048]{1,0:T(8,128)} %get-tuple-element.205.c_ref, f32[192,2048]{1,0:T(8,128)} %get-tuple-element.98.fo_ref, bf16[192,2048]{1,0:T(8,128)(2,1)} %copy-done.35, ...), custom_call_target="tpu_custom_call", output_to_operand_aliasing={{0}: (7, {})} | custom-call | flops 805306368 | bytes 7864320 | tf_op jit(solution)/shard_map/ple_both/pallas_call | solution.py:399
  410.2 6.8 %collective-permute-done.5.refs_1_ = bf16[192,2048]{1,0:T(8,128)(2,1)S(1)} collective-permute-done((bf16[192,2048]{1,0:T(8,128)(2,1)}, bf16[192,2048]{1,0:T(8,128)(2,1)S(1)}, u32[]{:S(2)}, u32[]{:S(2)}) %collective-permute-start.5) | collective-permute-done | bytes 786464 | tf_op jit(solution)/shard_map/ppermute | solution.py:687
  417.9 35.1 %ffn_bwd.3 = (f32[16,4096]{1,0:T(8,128)}, f32[16,4096]{1,0:T(8,128)}, f32[16,4096]{1,0:T(8,128)}, f32[384,32]{1,0:T(8,128)}, f32[192,2048]{1,0:T(8,128)}, /*index=5*/bf16[192,2048]{1,0:T(8,128)(2,1)}) custom-call(bf16[192,2048]{1,0:T(8,128)(2,1)} %get-tuple-element.106.refs_0_, bf16[192,2048]{1,0:T(8,128)(2,1)} %copy-done.34, ...), custom_call_target="tpu_custom_call" | custom-call | flops 19327352832 | bytes 50331648 | tf_op jit(solution)/shard_map/ffn_bwd/pallas_call | solution.py:346
  455.0 24.4 %ffn_bwd.4 = (f32[16,4096]{1,0:T(8,128)}, f32[16,4096]{1,0:T(8,128)}, f32[16,4096]{1,0:T(8,128)}, f32[384,32]{1,0:T(8,128)}, f32[384,2048]{1,0:T(8,128)}) custom-call(bf16[192,2048]{1,0:T(8,128)(2,1)} %get-tuple-element.110.refs_0_, bf16[192,2048]{1,0:T(8,128)(2,1)} %copy-done.20, bf16[768,4096]{1,0:T(8,128)(2,1)} %get-tuple-element.107.refs_2_, ...), custom_call_target="tpu_custom_call" | custom-call | flops 12079595520 | bytes 31457280 | tf_op jit(solution)/shard_map/ffn_bwd/pallas_call | solution.py:346
  487.6 18.3 %ffn_bwd.5 = (f32[16,4096]{1,0:T(8,128)}, f32[16,4096]{1,0:T(8,128)}, f32[16,4096]{1,0:T(8,128)}, f32[384,32]{1,0:T(8,128)}, f32[192,2048]{1,0:T(8,128)}, /*index=5*/bf16[192,2048]{1,0:T(8,128)(2,1)}) custom-call(bf16[192,2048]{1,0:T(8,128)(2,1)} %get-tuple-element.110.refs_0_, ...), custom_call_target="tpu_custom_call", output_to_operand_aliasing={{0}: (12, {}), {1}: (13, {}), {2}: (14, {})} | custom-call | flops 7247757312 | bytes 18874368 | tf_op jit(solution)/shard_map/ffn_bwd/pallas_call | solution.py:346
  521.8 8.0 %collective-permute-done.8.hr_ref = bf16[192,2048]{1,0:T(8,128)(2,1)} collective-permute-done((bf16[192,2048]{1,0:T(8,128)(2,1)}, bf16[192,2048]{1,0:T(8,128)(2,1)}, u32[]{:S(2)}, u32[]{:S(2)}) %collective-permute-start.8) | collective-permute-done | bytes 786464 | tf_op jit(solution)/shard_map/ppermute | solution.py:687
  529.8 6.5 %between_bwd.3 = (bf16[192,2048]{1,0:T(8,128)(2,1)}, f32[384,2048]{1,0:T(8,128)}, f32[384,2048]{1,0:T(8,128)}) custom-call(f32[192,2048]{1,0:T(8,128)} %get-tuple-element.104.df_ref, f32[384,2048]{1,0:T(8,128)} %get-tuple-element.205.c_ref, f32[192,2048]{1,0:T(8,128)} %get-tuple-element.122.ho_ref, ...), custom_call_target="tpu_custom_call", output_to_operand_aliasing={{1}: (8, {}), {2}: (9, {})} | custom-call | flops 150994944 | bytes 10223616 | tf_op jit(solution)/shard_map/between_bwd/pallas_call | solution.py:449
  540.8 12.6 %collective-permute-done.10.refs_3_ = bf16[192,2048]{1,0:T(8,128)(2,1)} collective-permute-done((bf16[192,2048]{1,0:T(8,128)(2,1)}, bf16[192,2048]{1,0:T(8,128)(2,1)}, u32[]{:S(2)}, u32[]{:S(2)}) %collective-permute-start.10) | collective-permute-done | bytes 786464 | tf_op jit(solution)/shard_map/ppermute | solution.py:687
  553.3 21.1 %attention_bwd.1 = (bf16[768,1536]{1,0:T(8,128)(2,1)}, f32[768,16]{1,0:T(8,128)}) custom-call(s32[1]{0:T(128)} %bitcast.29.turn_ref, bf16[192,2048]{1,0:T(8,128)(2,1)} %get-tuple-element.141.refs_0_, bf16[192,2048]{1,0:T(8,128)(2,1)} %get-tuple-element.142.refs_1_, bf16[192,2048]{1,0:T(8,128)(2,1)} %collective-permute-done.9.refs_2_, ...), custom_call_target="tpu_custom_call" | custom-call | flops 1048576 | bytes 1048576 | tf_op jit(solution)/shard_map/attention_bwd/pallas_call | solution.py:537
  601.2 12.8 %adapter_sums.1 = (f32[8,16,2,4096]{3,2,1,0:T(2,128)}, f32[8,16,4096]{2,1,0:T(8,128)}) custom-call(f32[8,16]{1,0:T(8,128)} %fusion.119.hot_ref, bf16[16,48,4224]{2,1,0:T(8,128)(2,1)} %bitcast.120), custom_call_target="tpu_custom_call" | custom-call | flops 50331648 | bytes 6291456 | tf_op jit(solution)/shard_map/adapter_sums/pallas_call | solution.py:611
  622.0 7.6 %final_bwd.1 = f32[384,2048]{1,0:T(8,128)} custom-call(bf16[384,2048]{1,0:T(8,128)(2,1)} %x_ref.1, f32[384,2048]{1,0:T(8,128)} %get-tuple-element.126.dn_ref, f32[384,2048]{1,0:T(8,128)} %get-tuple-element.127.db_ref, f32[384,2048]{1,0:T(8,128)} %convolution_add_fusion.2.ho_ref, bf16[384,2048]{1,0:T(8,128)(2,1)} %collective-permute-done.11.hr_ref, ...), custom_call_target="tpu_custom_call" | custom-call | flops 15728640 | bytes 15728640 | tf_op jit(solution)/shard_map/final_bwd/pallas_call | solution.py:583
  (258 shorter events, 194.7 us)
Async XLA Ops:
  7.2 45.7 %copy-start = (bf16[8,2048,48]{1,2,0:T(8,128)(2,1)S(1)}, bf16[8,2048,48]{1,2,0:T(8,128)(2,1)}, u32[]{:S(2)}) copy-start(bf16[8,2048,48]{1,2,0:T(8,128)(2,1)} %param.36) | copy-start | bytes 4718596
  7.2 97.7 %all-gather.8.cloned.1.call-start = ((), (), s32[]{:S(2)}) async-start(), calls=%async_computation.1 | async-start | bytes 18382848 | tf_op jit(solution)/shard_map/all_gather | solution.py:708
  10.5 235.1 %all-gather.10.cloned.1.call-start = ((), (), s32[]{:S(2)}) async-start(), calls=%async_computation.2 | async-start | bytes 28966912 | tf_op jit(solution)/shard_map/all_gather | solution.py:708
  10.5 37.5 %collective-permute-start = (bf16[384,2048]{1,0:T(8,128)(2,1)S(1)}, bf16[384,2048]{1,0:T(8,128)(2,1)}, u32[]{:S(2)}, u32[]{:S(2)}) collective-permute-start(bf16[384,2048]{1,0:T(8,128)(2,1)S(1)} %copy-done.6), channel_id=1, source_target_pairs={{0,1},{1,0},{2,3},{3,2},{4,5},{5,4},{6,7},{7,6},{8,9},{9,8},{10,11... | collective-permute-start | bytes 4718600 | tf_op jit(solution)/shard_map/ppermute | solution.py:687
  52.8 53.0 %copy-start.51 = (f32[2,256]{1,0:T(2,128)S(1)}, f32[2,256]{1,0:T(2,128)}, u32[]{:S(2)}) copy-start(f32[2,256]{1,0:T(2,128)} %refs_13_.1) | copy-start | bytes 6148
  53.9 64.3 %copy-start.32 = (bf16[768,48]{0,1:T(8,128)(2,1)}, bf16[768,48]{0,1:T(8,128)(2,1)S(1)}, u32[]{:S(2)}) copy-start(bf16[768,48]{0,1:T(8,128)(2,1)S(1)} %convolution_convert_fusion.4) | copy-start | bytes 221188
  104.9 241.2 %all-gather.12.cloned.1.call-start = ((), (), s32[]{:S(2)}) async-start(), calls=%async_computation.3 | async-start | bytes 20054016 | tf_op jit(solution)/shard_map/all_gather | solution.py:708
  179.5 37.0 %collective-permute-start.1 = (bf16[384,2048]{1,0:T(8,128)(2,1)}, bf16[384,2048]{1,0:T(8,128)(2,1)}, u32[]{:S(2)}, u32[]{:S(2)}) collective-permute-start(bf16[384,2048]{1,0:T(8,128)(2,1)} %dynamic-slice_convert_fusion), channel_id=1, source_target_pairs={{0,1},{1,0},{2,3},{3,2},{4,5},{5,4},{6,7},{7,6},{8,9},{9,8},{10,11... | collective-permute-start | bytes 4718600 | tf_op jit(solution)/shard_map/ppermute | solution.py:687
  185.5 31.0 %copy-start.8 = (f32[768,2048]{1,0:T(8,128)S(1)}, f32[768,2048]{1,0:T(8,128)}, u32[]{:S(2)}) copy-start(f32[768,2048]{1,0:T(8,128)} %copy-done.7) | copy-start | bytes 18874372
  187.3 31.2 %copy-start.31 = (bf16[384,64]{1,0:T(8,128)(2,1)}, bf16[384,64]{1,0:T(8,128)(2,1)S(1)}, u32[]{:S(2)}) copy-start(bf16[384,64]{1,0:T(8,128)(2,1)S(1)} %fusion.56.low_ref) | copy-start | bytes 147460
  189.4 29.2 %copy-start.49 = (f32[1,2048]{1,0:T(1,128)S(1)}, f32[1,2048]{1,0:T(1,128)}, u32[]{:S(2)}) copy-start(f32[1,2048]{1,0:T(1,128)} %get-tuple-element.219) | copy-start | bytes 24580
  245.6 343.4 %all-gather.14.cloned.1.call-start = ((), (), s32[]{:S(2)}) async-start(), calls=%async_computation.4 | async-start | bytes 6893568 | tf_op jit(solution)/shard_map/all_gather | solution.py:854
  245.6 36.6 %collective-permute-start.2 = (bf16[384,2048]{1,0:T(8,128)(2,1)S(1)}, bf16[384,2048]{1,0:T(8,128)(2,1)S(1)}, u32[]{:S(2)}, u32[]{:S(2)}) collective-permute-start(bf16[384,2048]{1,0:T(8,128)(2,1)S(1)} %get-tuple-element.204), channel_id=1, source_target_pairs={{0,1},{1,0},{2,3},{3,2},{4,5},{5,4},{6,7},{7,6},{8,9},{9,8},{10,11... | collective-permute-start | bytes 4718600 | tf_op jit(solution)/shard_map/ppermute | solution.py:687
  362.1 20.0 %collective-permute-start.4 = (bf16[192,2048]{1,0:T(8,128)(2,1)}, bf16[192,2048]{1,0:T(8,128)(2,1)S(1)}, u32[]{:S(2)}, u32[]{:S(2)}) collective-permute-start(bf16[192,2048]{1,0:T(8,128)(2,1)} %get-tuple-element.101), channel_id=1, source_target_pairs={{0,1},{1,0},{2,3},{3,2},{4,5},{5,4},{6,7},{7,6},{8,9},{9,8},{10,11... | collective-permute-start | bytes 2359304 | tf_op jit(solution)/shard_map/ppermute | solution.py:687
  379.4 20.7 %collective-permute-start.3 = (bf16[192,2048]{1,0:T(8,128)(2,1)}, bf16[192,2048]{1,0:T(8,128)(2,1)S(1)}, u32[]{:S(2)}, u32[]{:S(2)}) collective-permute-start(bf16[192,2048]{1,0:T(8,128)(2,1)} %get-tuple-element.99), channel_id=1, source_target_pairs={{0,1},{1,0},{2,3},{3,2},{4,5},{5,4},{6,7},{7,6},{8,9},{9,8},{10,11... | collective-permute-start | bytes 2359304 | tf_op jit(solution)/shard_map/ppermute | solution.py:687
  391.2 25.8 %collective-permute-start.5 = (bf16[192,2048]{1,0:T(8,128)(2,1)}, bf16[192,2048]{1,0:T(8,128)(2,1)S(1)}, u32[]{:S(2)}, u32[]{:S(2)}) collective-permute-start(bf16[192,2048]{1,0:T(8,128)(2,1)} %get-tuple-element.106.refs_0_), channel_id=1, source_target_pairs={{0,1},{1,0},{2,3},{3,2},{4,5},{5,4},{6,7},{7,6},{8,9},{9,8},{10,11... | collective-permute-start | bytes 2359304 | tf_op jit(solution)/shard_map/ppermute | solution.py:687
  409.2 44.9 %collective-permute-start.6 = (bf16[192,2048]{1,0:T(8,128)(2,1)}, bf16[192,2048]{1,0:T(8,128)(2,1)S(1)}, u32[]{:S(2)}, u32[]{:S(2)}) collective-permute-start(bf16[192,2048]{1,0:T(8,128)(2,1)} %get-tuple-element.110.refs_0_), channel_id=1, source_target_pairs={{0,1},{1,0},{2,3},{3,2},{4,5},{5,4},{6,7},{7,6},{8,9},{9,8},{10,11... | collective-permute-start | bytes 2359304 | tf_op jit(solution)/shard_map/ppermute | solution.py:687
  453.0 26.3 %collective-permute-start.7 = (bf16[192,2048]{1,0:T(8,128)(2,1)}, bf16[192,2048]{1,0:T(8,128)(2,1)S(1)}, u32[]{:S(2)}, u32[]{:S(2)}) collective-permute-start(bf16[192,2048]{1,0:T(8,128)(2,1)} %get-tuple-element.109), channel_id=1, source_target_pairs={{0,1},{1,0},{2,3},{3,2},{4,5},{5,4},{6,7},{7,6},{8,9},{9,8},{10,11... | collective-permute-start | bytes 2359304 | tf_op jit(solution)/shard_map/ppermute | solution.py:687
  486.6 22.4 %collective-permute-start.9 = (bf16[192,2048]{1,0:T(8,128)(2,1)}, bf16[192,2048]{1,0:T(8,128)(2,1)}, u32[]{:S(2)}, u32[]{:S(2)}) collective-permute-start(bf16[192,2048]{1,0:T(8,128)(2,1)} %get-tuple-element.141.refs_0_), channel_id=1, source_target_pairs={{0,1},{1,0},{2,3},{3,2},{4,5},{5,4},{6,7},{7,6},{8,9},{9,8},{10,11... | collective-permute-start | bytes 2359304 | tf_op jit(solution)/shard_map/ppermute | solution.py:687
  509.0 125.1 %all-gather.16.cloned.1.call-start = ((), (), s32[]{:S(2)}) async-start(), calls=%async_computation.5 | async-start | bytes 1462272 | tf_op jit(solution)/shard_map/all_gather | solution.py:854
  512.4 17.4 %collective-permute-start.8 = (bf16[192,2048]{1,0:T(8,128)(2,1)}, bf16[192,2048]{1,0:T(8,128)(2,1)}, u32[]{:S(2)}, u32[]{:S(2)}) collective-permute-start(bf16[192,2048]{1,0:T(8,128)(2,1)} %get-tuple-element.123), channel_id=1, source_target_pairs={{0,1},{1,0},{2,3},{3,2},{4,5},{5,4},{6,7},{7,6},{8,9},{9,8},{10,11... | collective-permute-start | bytes 2359304 | tf_op jit(solution)/shard_map/ppermute | solution.py:687
  536.4 17.0 %collective-permute-start.10 = (bf16[192,2048]{1,0:T(8,128)(2,1)}, bf16[192,2048]{1,0:T(8,128)(2,1)}, u32[]{:S(2)}, u32[]{:S(2)}) collective-permute-start(bf16[192,2048]{1,0:T(8,128)(2,1)} %get-tuple-element.142.refs_1_), channel_id=1, source_target_pairs={{0,1},{1,0},{2,3},{3,2},{4,5},{5,4},{6,7},{7,6},{8,9},{9,8},{10,11... | collective-permute-start | bytes 2359304 | tf_op jit(solution)/shard_map/ppermute | solution.py:687
  583.8 38.2 %collective-permute-start.11 = (bf16[384,2048]{1,0:T(8,128)(2,1)}, bf16[384,2048]{1,0:T(8,128)(2,1)}, u32[]{:S(2)}, u32[]{:S(2)}) collective-permute-start(bf16[384,2048]{1,0:T(8,128)(2,1)} %add_convert_fusion), channel_id=1, source_target_pairs={{0,1},{1,0},{2,3},{3,2},{4,5},{5,4},{6,7},{7,6},{8,9},{9,8},{10,11... | collective-permute-start | bytes 4718600 | tf_op jit(solution)/shard_map/ppermute | solution.py:687
  595.6 34.1 %all-to-all-start = ((bf16[32,64,113]{2,1,0:T(8,128)(2,1)}), bf16[32,64,113]{2,1,0:T(8,128)(2,1)S(1)}, u32[]{:S(2)}, u32[]{:S(2)}) async-start(bf16[32,64,113]{2,1,0:T(8,128)(2,1)} %bitcast.32), calls=%async_computation | async-start | bytes 1048576 | tf_op jit(solution)/shard_map/all_to_all | solution.py:903
  (47 other events, 260.5 us)
Sparse Core Ops, SparseCore 0:
  10.6 94.2 all-gather.7
  107.0 138.4 all-gather.9
  247.1 98.9 all-gather.11
  509.1 62.5 all-gather.13
  592.0 40.1 all-gather.15

commit v3 on v2

v3 whole, which is shorter than its diff:
```python
import functools

import jax
import jax.numpy as jnp
from jax import lax
from jax.experimental import pallas as pl
from jax.experimental.pallas import tpu as pltpu
from jax.sharding import PartitionSpec as P

HEADS = 8
KV = 2
HD = 256
WIN = 512
BLK = 256
RANK = 16
UB = 512
GB = 2 * UB

NORM_EPSILON = 1e-06
RSQRT_TWO = 0.7071067811865476
ROPE_BASE = 10000.0
NEG_BIG = -1e30
GELU_A = 0.7978845608028654
GELU_B = 0.044715

F32 = jnp.float32
BF16 = jnp.bfloat16
VMEM_LIMIT = 58 * 1024 * 1024
DOWN_CHUNK = 512


def dot(a, b):
    return lax.dot_general(a, b, (((1,), (0,)), ((), ())), preferred_element_type=F32)


def dot_nt(a, b):
    return lax.dot_general(a, b, (((1,), (1,)), ((), ())), preferred_element_type=F32)


def dot_tn(a, b):
    return lax.dot_general(a, b, (((0,), (0,)), ((), ())), preferred_element_type=F32)


def inv_rms(v):
    return lax.rsqrt(jnp.mean(v * v, axis=-1, keepdims=True) + NORM_EPSILON)


def normed(v, gains):
    return v * inv_rms(v) * gains


def norm_back(v, gains, cotangent):
    r = inv_rms(v)
    gc = gains * cotangent
    return r * gc - v * (r * r * r * jnp.mean(v * gc, axis=-1, keepdims=True))


def gelu_tanh(v):
    return 0.5 * v * (1.0 + jnp.tanh(GELU_A * (v + GELU_B * v * v * v)))


def gelu_both(v):
    v2 = v * v
    th = jnp.tanh(GELU_A * v * (1.0 + GELU_B * v2))
    half = 0.5 * (1.0 + th)
    slope = half + 0.5 * v * (1.0 - th * th) * (GELU_A * (1.0 + 3.0 * GELU_B * v2))
    return v * half, slope


def const_spec(shape):
    return pl.BlockSpec(shape, lambda *_: (0,) * len(shape), pipeline_mode=pl.Buffered(1))


def any_spec():
    return pl.BlockSpec(memory_space=pl.ANY)


def params():
    return pltpu.CompilerParams(vmem_limit_bytes=VMEM_LIMIT)


def pack_shards(gate_up, first, count, rest, rows, name):
    width = count * GB + sum(n for _, n in rest)

    def body(*refs):
        out = refs[-1]
        for b in range(count):
            cs = slice(b * UB, (b + 1) * UB)
            out[:, b * GB : b * GB + UB] = refs[0][:, 0, cs]
            out[:, b * GB + UB : (b + 1) * GB] = refs[0][:, 1, cs]
        at = count * GB
        for ref, (value, n) in zip(refs[1 if count else 0 : -1], rest):
            out[:, at : at + n] = ref[...] if value.shape == (rows, n) else ref[...].T
            at += n

    block = (pl.Element(rows), pl.Element(2), pl.Element(count * UB))
    gate_spec = [pl.BlockSpec(block, lambda i: (0, 0, first * UB))] if count else []
    return pl.pallas_call(
        body,
        grid=(1,),
        in_specs=gate_spec + [const_spec(v.shape) for v, _ in rest],
        out_specs=const_spec((rows, width)),
        out_shape=jax.ShapeDtypeStruct((rows, width), BF16),
        compiler_params=params(),
        name=name,
    )(*([gate_up] if count else []), *[v for v, _ in rest])


def ffn_up(h2, packed, blocks, first, u_low, bgu, ad_t, prev):
    rows, width = h2.shape
    units = ad_t.shape[1]
    tile = rows // 2
    sub = 256

    def body(*refs):
        h_ref, w_ref, ul_ref, bgu_ref, ad_ref = refs[:5]
        g_out, u_out, hid_out, ud_out = refs[-4:]
        j = pl.program_id(0)

        @pl.when(j == 0)
        def _():
            if prev is None:
                ud_out[...] = jnp.zeros_like(ud_out)
            else:
                ud_out[...] = refs[5][...]

        for k in range(rows // tile):
            at_rows = slice(k * tile, (k + 1) * tile)
            h = h_ref[at_rows, :]
            ul = ul_ref[at_rows, :]
            for n in range(UB // sub):
                cs = slice(n * sub, (n + 1) * sub)
                us = slice(UB + n * sub, UB + (n + 1) * sub)
                g = dot(h, w_ref[:, cs]) + dot(ul, bgu_ref[:, cs])
                u = dot(h, w_ref[:, us]) + dot(ul, bgu_ref[:, us])
                g_out[at_rows, cs] = g.astype(BF16)
                u_out[at_rows, cs] = u.astype(BF16)
                hid_out[at_rows, cs] = (gelu_tanh(g) * u).astype(BF16)
            ud_out[at_rows, :] += dot_nt(hid_out[at_rows, :], ad_ref[...])

    in_specs = [
        const_spec((rows, width)),
        pl.BlockSpec((width, GB), lambda j: (0, j)),
        const_spec((rows, 2 * RANK)),
        pl.BlockSpec((2 * RANK, GB), lambda j: (0, first + j)),
        pl.BlockSpec((RANK, UB), lambda j: (0, first + j)),
    ]
    args = [h2, packed, u_low, bgu, ad_t]
    aliases = {}
    if prev is not None:
        in_specs += [const_spec((rows, RANK)), any_spec(), any_spec(), any_spec()]
        args += list(prev)
        aliases = {6: 0, 7: 1, 8: 2}
    unit_block = pl.BlockSpec((rows, UB), lambda j: (0, first + j))
    shape = jax.ShapeDtypeStruct
    g, u, hidden, ud = pl.pallas_call(
        body,
        grid=(blocks,),
        in_specs=in_specs,
        out_specs=[unit_block] * 3 + [const_spec((rows, RANK))],
        out_shape=[shape((rows, units), BF16)] * 3 + [shape((rows, RANK), F32)],
        input_output_aliases=aliases,
        compiler_params=params(),
        cost_estimate=pl.CostEstimate(
            flops=4 * rows * width * UB * blocks,
            bytes_accessed=2 * width * GB * blocks,
            transcendentals=rows * UB * blocks,
        ),
        name="ffn_up",
    )(*args)
    return ud, g, u, hidden


def ffn_down(hidden, packed, ud, bd, rb):
    rows, units = hidden.shape
    width = packed.shape[0]
    r = rows // 2
    half = r // 2
    chunk = DOWN_CHUNK

    def body(h_ref, w_ref, ud_ref, bd_ref, own_out, peer_out):
        total = dot_nt(h_ref[...], w_ref[...]) + dot(ud_ref[...].astype(BF16), bd_ref[...])
        own_out[...] = total[:half]
        peer_out[...] = total[half:].astype(BF16)

    row_const = lambda n: pl.BlockSpec((r, n), lambda j: (rb, 0), pipeline_mode=pl.Buffered(1))
    column = pl.BlockSpec((half, chunk), lambda j: (0, j))
    return pl.pallas_call(
        body,
        grid=(width // chunk,),
        in_specs=[
            row_const(units),
            pl.BlockSpec((chunk, units), lambda j: (j, 0)),
            row_const(RANK),
            pl.BlockSpec((RANK, chunk), lambda j: (0, j)),
        ],
        out_specs=[column, column],
        out_shape=[
            jax.ShapeDtypeStruct((half, width), F32),
            jax.ShapeDtypeStruct((half, width), BF16),
        ],
        compiler_params=params(),
        cost_estimate=pl.CostEstimate(
            flops=2 * r * width * units, bytes_accessed=2 * width * units, transcendentals=0
        ),
        name="ffn_down",
    )(hidden, packed, ud, bd)


def ffn_bwd(own, peer, packs, split, first, blocks, g_pre, u_pre, bgu, ad_t, bd, u_t, a_in_t, rb, base, prev, last):
    half, width = own.shape
    r = 2 * half
    units = ad_t.shape[1]
    sub = 256

    def body(*refs):
        own_ref, peer_ref, g_ref, u_ref, bgu_ref, ad_ref, bd_ref, ut_ref, ain_ref = refs[:9]
        pack_refs = refs[9 : 9 + len(packs)]
        at = 9 + len(packs)
        if base is not None:
            base_ref = refs[at]
            at += 1
        if prev is not None:
            acc_in, du_in = refs[at : at + 2]
            at += 3
        grad_out, du_out = refs[at : at + 2]
        if last:
            own_out, peer_out = refs[at + 2 : at + 4]
            at += 4
        else:
            acc_out = refs[at + 2]
            at += 3
        df, acc, wbuf, dd, du, dgu, hs, sem, acc_sem = refs[at:]
        j = pl.program_id(0)
        slot = lax.rem(j, 2)

        def copy(ref, column, where, part):
            lo, n = ((2 * UB, UB), (0, 2 * UB))[part]
            return pltpu.make_async_copy(
                ref.at[:, pl.ds(column, n)], wbuf.at[where, :, pl.ds(lo, n)], sem.at[where, part]
            )

        def fetch(step, where):
            block = first + step
            copy(pack_refs[2], pl.multiple_of(block * UB, UB), where, 0).start()

            @pl.when(block < split)
            def _():
                copy(pack_refs[0], pl.multiple_of(block * GB, GB), where, 1).start()

            @pl.when(block >= split)
            def _():
                copy(pack_refs[1], pl.multiple_of((block - split) * GB, GB), where, 1).start()

        @pl.when(j == 0)
        def _():
            fetch(j, 0)
            df[0:half, :] = own_ref[...]
            df[half:r, :] = peer_ref[...]
            if prev is None:
                acc[...] = jnp.zeros_like(acc)
                du[...] = jnp.zeros_like(du)
            else:
                pltpu.make_async_copy(acc_in, acc, acc_sem).start()
                du[...] = du_in[...]
            dd[...] = dot_nt(df[...], bd_ref[...]).astype(BF16)

        @pl.when(j + 1 < blocks)
        def _():
            fetch(j + 1, 1 - slot)

        copy(pack_refs[2], 0, slot, 0).wait()
        for n in range(UB // sub):
            cs = slice(n * sub, (n + 1) * sub)
            dh = dot(df[...], wbuf[slot, :, 2 * UB + n * sub : 2 * UB + (n + 1) * sub])
            dh += dot(dd[...], ad_ref[:, cs])
            g = g_ref[:, cs].astype(F32)
            u = u_ref[:, cs].astype(F32)
            act, slope = gelu_both(g)
            dgu[:, cs] = (dh * u * slope).astype(BF16)
            dgu[:, UB + n * sub : UB + (n + 1) * sub] = (dh * act).astype(BF16)
            hs[:, cs] = (act * u).astype(BF16)
        copy(pack_refs[0], 0, slot, 1).wait()
        if prev is not None:

            @pl.when(j == 0)
            def _():
                pltpu.make_async_copy(acc_in, acc, acc_sem).wait()

        d_both = dgu[...]
        for c in range(width // 512):
            cc = slice(c * 512, (c + 1) * 512)
            acc[:, cc] += dot_nt(d_both, wbuf[slot, cc, 0 : 2 * UB])
        du[...] += dot_nt(d_both, bgu_ref[...])
        both = dot(ut_ref[...], d_both)
        rows = (2.0 * both[:RANK, :UB], 2.0 * both[RANK:, UB:], dot_tn(dd[...], hs[...]))
        for m, row in enumerate(rows):
            ms = slice(m * RANK, (m + 1) * RANK)
            if base is not None:
                row = row + base_ref[ms, :]
            grad_out[ms, :] = row.astype(grad_out.dtype)

        @pl.when(j == blocks - 1)
        def _():
            du_out[...] = du[...]
            if last:
                total = acc[...] + dot(du[...].astype(BF16), ain_ref[...])
                own_out[...] = total[:half]
                peer_out[...] = total[half:].astype(BF16)
            else:
                acc_out[...] = acc[...]

    rows_block = lambda: pl.BlockSpec((r, UB), lambda j: (rb, first + j))
    unit_block = lambda: pl.BlockSpec((RANK, UB), lambda j: (0, first + j))
    shape = jax.ShapeDtypeStruct
    in_specs = [
        const_spec((half, width)),
        const_spec((half, width)),
        rows_block(),
        rows_block(),
        pl.BlockSpec((2 * RANK, 2 * UB), lambda j: (0, first + j)),
        unit_block(),
        const_spec((RANK, width)),
        pl.BlockSpec((2 * RANK, r), lambda j: (0, rb), pipeline_mode=pl.Buffered(1)),
        const_spec((2 * RANK, width)),
    ] + [any_spec() for _ in packs]
    args = [own, peer, g_pre, u_pre, bgu, ad_t, bd, u_t, a_in_t, *packs]
    aliases = {}
    grad_block = lambda: pl.BlockSpec((3 * RANK, UB), lambda j: (0, first + j))
    if base is not None:
        in_specs.append(grad_block())
        args.append(base)
    if prev is not None:
        aliases = {len(args) + 2: 0}
        in_specs += [any_spec(), const_spec((r, 2 * RANK)), any_spec()]
        args += list(prev)
    out_specs = [grad_block(), const_spec((r, 2 * RANK))]
    out_shape = [shape((3 * RANK, units), F32 if base is None else BF16), shape((r, 2 * RANK), F32)]
    if last:
        out_specs += [const_spec((half, width)), const_spec((half, width))]
        out_shape += [shape((half, width), F32), shape((half, width), BF16)]
    else:
        out_specs += [const_spec((r, width))]
        out_shape += [shape((r, width), F32)]
    return pl.pallas_call(
        body,
        grid=(blocks,),
        in_specs=in_specs,
        out_specs=out_specs,
        out_shape=out_shape,
        scratch_shapes=[
            pltpu.VMEM((r, width), BF16),
            pltpu.VMEM((r, width), F32),
            pltpu.VMEM((2, width, 3 * UB), BF16),
            pltpu.VMEM((r, RANK), BF16),
            pltpu.VMEM((r, 2 * RANK), F32),
            pltpu.VMEM((r, 2 * UB), BF16),
            pltpu.VMEM((r, UB), BF16),
            pltpu.SemaphoreType.DMA((2, 2)),
            pltpu.SemaphoreType.DMA,
        ],
        input_output_aliases=aliases,
        compiler_params=params(),
        cost_estimate=pl.CostEstimate(
            flops=6 * r * width * UB * blocks,
            bytes_accessed=6 * width * UB * blocks,
            transcendentals=r * UB * blocks,
        ),
        name="ffn_bwd",
    )(*args)


def ple_both(combined, ffn_own, ffn_recv, out_grad, ple_in, packed, column, gains, prev, rb):
    half, width = ffn_own.shape
    rows = combined.shape[0]
    pd = ple_in.shape[1]
    tile = half // 2

    def body(c_ref, fo_ref, fr_ref, og_ref, pi_ref, w_ref, gain_ref, *refs):
        out_ref, dffn_ref, dfirst_ref = refs[-3:]
        ffn = fo_ref[...] + fr_ref[...].astype(F32)
        y = c_ref[...] + normed(ffn, gain_ref[4:5, :])
        pre = dot(y.astype(BF16), w_ref[:, 0:pd])
        side = pi_ref[...].astype(F32)
        act, slope = gelu_both(pre)
        wide = dot_nt((act * side).astype(BF16), w_ref[:, pd : 2 * pd])
        out_ref[...] = (y + normed(wide, gain_ref[5:6, :])).astype(BF16)
        cot = og_ref[...].astype(F32)
        d_wide = norm_back(wide, gain_ref[5:6, :], cot).astype(BF16)
        d_pre = (dot(d_wide, w_ref[:, pd : 2 * pd]) * side * slope).astype(BF16)
        d_first = cot + dot_nt(d_pre, w_ref[:, 0:pd])
        dfirst_ref[...] = d_first
        dffn_ref[...] = norm_back(ffn, gain_ref[4:5, :], d_first).astype(BF16)

    n = half // tile
    here = lambda w: pl.BlockSpec((tile, w), lambda i: (i, 0))
    there = lambda w: pl.BlockSpec((tile, w), lambda i: (rb * n + i, 0))
    shape = jax.ShapeDtypeStruct
    return pl.pallas_call(
        body,
        grid=(n,),
        in_specs=[
            there(width),
            here(width),
            here(width),
            there(width),
            there(pd),
            pl.BlockSpec((width, 2 * pd), lambda i: (0, column), pipeline_mode=pl.Buffered(1)),
            const_spec(gains.shape),
        ]
        + [any_spec() for _ in prev],
        out_specs=[there(width), here(width), here(width)],
        out_shape=[
            shape((rows, width), BF16),
            shape((half, width), BF16),
            shape((half, width), F32),
        ],
        input_output_aliases={7: 0} if prev else {},
        compiler_params=params(),
        cost_estimate=pl.CostEstimate(
            flops=8 * half * width * pd, bytes_accessed=20 * half * width, transcendentals=0
        ),
        name="ple_both",
    )(combined, ffn_own, ffn_recv, out_grad, ple_in, packed, gains, *prev)


def between_bwd(d_first, combined, dh_own, dh_recv, attn_proj, low, packed, column, gains, prev, rb):
    half, width = d_first.shape
    rows = combined.shape[0]
    lr = low.shape[1]
    tile = half // 2

    def body(df_ref, c_ref, ho_ref, hr_ref, ap_ref, low_ref, w_ref, gain_ref, *refs):
        da_ref, db_ref, dn_ref = refs[-3:]
        d_h2 = ho_ref[...] + hr_ref[...].astype(F32)
        d_comb = df_ref[...] + norm_back(c_ref[...], gain_ref[3:4, :], d_h2)
        d_branch = d_comb * RSQRT_TWO
        db_ref[...] = d_branch
        da_ref[...] = norm_back(ap_ref[...], gain_ref[1:2, :], d_branch).astype(BF16)
        wide = dot_nt(low_ref[...], w_ref[:, lr : 2 * lr])
        d_wide = norm_back(wide, gain_ref[2:3, :], d_branch).astype(BF16)
        d_low = dot(d_wide, w_ref[:, lr : 2 * lr]).astype(BF16)
        dn_ref[...] = d_branch + dot_nt(d_low, w_ref[:, 0:lr])

    n = half // tile
    here = lambda w: pl.BlockSpec((tile, w), lambda i: (i, 0))
    there = lambda w: pl.BlockSpec((tile, w), lambda i: (rb * n + i, 0))
    shape = jax.ShapeDtypeStruct
    return pl.pallas_call(
        body,
        grid=(n,),
        in_specs=[
            here(width),
            there(width),
            here(width),
            here(width),
            there(width),
            there(lr),
            pl.BlockSpec((width, 2 * lr), lambda i: (0, column), pipeline_mode=pl.Buffered(1)),
            const_spec(gains.shape),
        ]
        + [any_spec() for _ in prev],
        out_specs=[here(width), there(width), there(width)],
        out_shape=[
            shape((half, width), BF16),
            shape((rows, width), F32),
            shape((rows, width), F32),
        ],
        input_output_aliases={8: 1, 9: 2} if prev else {},
        compiler_params=params(),
        cost_estimate=pl.CostEstimate(
            flops=6 * half * width * lr, bytes_accessed=26 * half * width, transcendentals=0
        ),
        name="between_bwd",
    )(d_first, combined, dh_own, dh_recv, attn_proj, low, packed, gains, *prev)


def attention_bwd(pieces, turn, packed, qkv_column, wo_column, bo, ao_t, q, k, v, probs, raw, gains, cos, sin,
                  context, u_t, b_qkv, a_in_t):
    length, q_width = q.shape
    width = packed.shape[0]
    heads = q_width // HD
    half_hd = HD // 2
    scale = HD ** (-0.5)
    n_blocks = length // BLK
    span = WIN // BLK
    quarter = pieces[0].shape[0]
    count = len(pieces)
    total = q_width + 2 * HD
    here = length // 2

    def unrotate(d, cos_v, sin_v):
        d1, d2 = d[:, :half_hd], d[:, half_hd:]
        return jnp.concatenate([d1 * cos_v + d2 * sin_v, d2 * cos_v - d1 * sin_v], axis=1)

    def body(turn_ref, *refs):
        piece_refs = refs[:count]
        (wo_ref, w_any, bo_ref, ao_ref, q_ref, k_ref, v_ref, p_ref, rq_ref, rk_ref, gain_ref, cos_ref,
         sin_ref, ctx_ref, ut_ref, b_ref, ain_ref, peer_0, peer_1, draw, du_out, heads_out,
         da, du, dk, dv, wq, sem) = refs[count:]
        hh = pl.program_id(0)
        weights = pltpu.make_async_copy(w_any.at[:, pl.ds(qkv_column, total)], wq, sem)

        @pl.when(hh == 0)
        def _():
            weights.start()
            shift = turn_ref[0] * here
            for i, ref in enumerate(piece_refs):
                place = lax.rem(shift + i * quarter, length)
                da[pl.ds(pl.multiple_of(place, quarter), quarter), :] = ref[...]
            du[...] = dot_nt(da[...], bo_ref[...]).astype(BF16)
            dk[...] = jnp.zeros_like(dk)
            dv[...] = jnp.zeros_like(dv)

        dctx = (dot(da[...], wo_ref[...]) + dot(du[...], ao_ref[...])).astype(BF16)
        cos_v, sin_v = cos_ref[...], sin_ref[...]
        column = pl.multiple_of(hh * HD, HD)
        for i in range(n_blocks):
            low, high = max(0, i - span + 1) * BLK, (i + 1) * BLK
            rows = slice(i * BLK, (i + 1) * BLK)
            d_i = dctx[rows]
            p_i = p_ref[0, rows, low:high]
            p_f = p_i.astype(F32)
            dp = dot_nt(d_i, v_ref[low:high, :])
            ds = p_f * (dp - jnp.sum(p_f * dp, axis=-1, keepdims=True))
            ds = ds.astype(BF16)
            dq = dot(ds, k_ref[low:high, :]) * scale
            dk[low:high, :] += dot_tn(ds, q_ref[rows, :])
            dv[low:high, :] += dot_tn(p_i, d_i)
            back = norm_back(rq_ref[rows, :], gain_ref[0:1, :], unrotate(dq, cos_v[rows], sin_v[rows]))
            draw[rows, pl.ds(column, HD)] = back.astype(BF16)
        heads_out[:, pl.ds(column, HD)] = (
            2.0 * dot(ut_ref[0:RANK, :], draw[:, pl.ds(column, HD)])
        ).astype(BF16)
        heads_out[:, pl.ds(pl.multiple_of(total + hh * HD, HD), HD)] = dot_tn(
            du[...], ctx_ref[...]
        ).astype(BF16)

        @pl.when(hh == heads - 1)
        def _():
            back = norm_back(rk_ref[...], gain_ref[1:2, :], unrotate(dk[...] * scale, cos_v, sin_v))
            at_k, at_v = slice(q_width, q_width + HD), slice(q_width + HD, total)
            draw[:, at_k] = back.astype(BF16)
            draw[:, at_v] = dv[...].astype(BF16)
            for m, where in ((1, at_k), (2, at_v)):
                got = dot(ut_ref[m * RANK : (m + 1) * RANK, :], draw[:, where])
                heads_out[:, where] = (2.0 * got).astype(BF16)
            du_out[...] = dot_nt(draw[...], b_ref[...]).astype(BF16)
            weights.wait()
            theirs = pl.multiple_of((1 - turn_ref[0]) * here, here)
            d_rows = draw[pl.ds(theirs, here), :]
            u_rows = du_out[pl.ds(theirs, here), :]
            for c in range(width // 512):
                cc = slice(c * 512, (c + 1) * 512)
                got = dot_nt(d_rows, wq[cc, :]) + dot(u_rows, ain_ref[:, cc])
                peer_0[:, cc] = got[: here // 2].astype(BF16)
                peer_1[:, cc] = got[here // 2 :].astype(BF16)

    shape = jax.ShapeDtypeStruct
    head_block = lambda: pl.BlockSpec((length, HD), lambda h: (0, h))
    return pl.pallas_call(
        body,
        grid=(heads,),
        in_specs=[pl.BlockSpec(memory_space=pltpu.SMEM)]
        + [const_spec(piece.shape) for piece in pieces]
        + [
            pl.BlockSpec((width, HD), lambda h: (0, wo_column + h)),
            any_spec(),
            const_spec(bo.shape),
            pl.BlockSpec((RANK, HD), lambda h: (0, h)),
            head_block(),
            const_spec(k.shape),
            const_spec(v.shape),
            pl.BlockSpec((1, length, length), lambda h: (h, 0, 0)),
            head_block(),
            pl.BlockSpec((length, HD), lambda h: (0, heads), pipeline_mode=pl.Buffered(1)),
            const_spec(gains.shape),
            const_spec(cos.shape),
            const_spec(sin.shape),
            head_block(),
            const_spec(u_t.shape),
            const_spec(b_qkv.shape),
            const_spec(a_in_t.shape),
        ],
        out_specs=[
            const_spec((here // 2, width)),
            const_spec((here // 2, width)),
            const_spec((length, total)),
            const_spec((length, 3 * RANK)),
            const_spec((RANK, total + q_width)),
        ],
        out_shape=[
            shape((here // 2, width), BF16),
            shape((here // 2, width), BF16),
            shape((length, total), BF16),
            shape((length, 3 * RANK), BF16),
            shape((RANK, total + q_width), BF16),
        ],
        scratch_shapes=[
            pltpu.VMEM((length, width), BF16),
            pltpu.VMEM((length, RANK), BF16),
            pltpu.VMEM((length, HD), F32),
            pltpu.VMEM((length, HD), F32),
            pltpu.VMEM((width, total), BF16),
            pltpu.SemaphoreType.DMA,
        ],
        compiler_params=params(),
        cost_estimate=pl.CostEstimate(flops=1024 * 1024, bytes_accessed=1024 * 1024, transcendentals=0),
        name="attention_bwd",
    )(turn, *pieces, packed, packed, bo, ao_t, q, k, v, probs, raw, raw, gains, cos, sin, context, u_t, b_qkv,
      a_in_t)


def final_bwd(x, d_norm, d_branch, dh_own, dh_recv, gains, prev, rb):
    rows, width = x.shape
    half = rows // 2
    tile = half // 2

    def body(x_ref, dn_ref, db_ref, ho_ref, hr_ref, gain_ref, *refs):
        out_ref = refs[-1]
        total = dn_ref[...] + ho_ref[...] + hr_ref[...].astype(F32)
        out_ref[...] = db_ref[...] + norm_back(x_ref[...].astype(F32), gain_ref[0:1, :], total)

    n = half // tile
    here = pl.BlockSpec((tile, width), lambda i: (i, 0))
    there = pl.BlockSpec((tile, width), lambda i: (rb * n + i, 0))
    return pl.pallas_call(
        body,
        grid=(n,),
        in_specs=[there] * 4 + [here, const_spec(gains.shape)] + [any_spec() for _ in prev],
        out_specs=there,
        out_shape=jax.ShapeDtypeStruct((rows, width), F32),
        input_output_aliases={6: 0} if prev else {},
        compiler_params=params(),
        cost_estimate=pl.CostEstimate(
            flops=20 * half * width, bytes_accessed=20 * half * width, transcendentals=0
        ),
        name="final_bwd",
    )(x, d_norm, d_branch, dh_own, dh_recv, gains, *prev)


def add_by_adapter(ids_ref, got_ref, total, seqs, share):
    total[...] = jnp.zeros_like(total)

    def step(i, carry):
        where = ids_ref[i // share]
        total[where] += got_ref[i].astype(F32)
        return carry

    lax.fori_loop(0, seqs, step, 0)


def ffn_adapter_sums(got, ids, adapters, units):
    seqs = got.shape[0]
    tile = 1024

    def body(ids_ref, got_ref, out_ref, down_ref, total):
        add_by_adapter(ids_ref, got_ref, total, seqs, 1)
        out_ref[:, :, 0, :] = total[:, :RANK, :]
        out_ref[:, :, 1, :] = total[:, RANK : 2 * RANK, :]
        down_ref[...] = total[:, 2 * RANK :, :]

    return pl.pallas_call(
        body,
        grid=(units // tile,),
        in_specs=[
            pl.BlockSpec(memory_space=pltpu.SMEM),
            pl.BlockSpec((seqs, 3 * RANK, tile), lambda i: (0, 0, i)),
        ],
        out_specs=[
            pl.BlockSpec((adapters, RANK, 2, tile), lambda i: (0, 0, 0, i)),
            pl.BlockSpec((adapters, RANK, tile), lambda i: (0, 0, i)),
        ],
        out_shape=[
            jax.ShapeDtypeStruct((adapters, RANK, 2, units), F32),
            jax.ShapeDtypeStruct((adapters, RANK, units), F32),
        ],
        scratch_shapes=[pltpu.VMEM((adapters, 3 * RANK, tile), F32)],
        compiler_params=params(),
        cost_estimate=pl.CostEstimate(
            flops=6 * seqs * RANK * units, bytes_accessed=6 * seqs * RANK * units, transcendentals=0
        ),
        name="adapter_sums",
    )(ids, got)


def shared_sums(got, ids, adapters):
    seqs, rows, columns = got.shape
    cuts = (2 * RANK, RANK, RANK, 3 * RANK)

    def body(ids_ref, got_ref, *refs):
        total = refs[-1]
        add_by_adapter(ids_ref, got_ref, total, seqs, 2)
        for n in range(adapters):
            flipped = total[n].T
            at = 0
            for ref, cut in zip(refs, cuts):
                ref[n] = flipped[at : at + cut, :]
                at += cut

    return pl.pallas_call(
        body,
        grid=(1,),
        in_specs=[pl.BlockSpec(memory_space=pltpu.SMEM), const_spec(got.shape)],
        out_specs=[const_spec((adapters, cut, rows)) for cut in cuts],
        out_shape=[jax.ShapeDtypeStruct((adapters, cut, rows), F32) for cut in cuts],
        scratch_shapes=[pltpu.VMEM((adapters, rows, columns), F32)],
        compiler_params=params(),
        name="shared_sums",
    )(ids, got)


def head_sums(got, ids, adapters, qkv_width):
    seqs, rank, columns = got.shape
    rest = columns - qkv_width

    def body(ids_ref, got_ref, qkv_ref, attn_ref, total):
        add_by_adapter(ids_ref, got_ref, total, seqs, 1)
        qkv_ref[:, :, 0, :] = total[:, :, :qkv_width]
        attn_ref[...] = total[:, :, qkv_width:]

    return pl.pallas_call(
        body,
        grid=(1,),
        in_specs=[pl.BlockSpec(memory_space=pltpu.SMEM), const_spec(got.shape)],
        out_specs=[const_spec((adapters, rank, 1, qkv_width)), const_spec((adapters, rank, rest))],
        out_shape=[
            jax.ShapeDtypeStruct((adapters, rank, 1, qkv_width), F32),
            jax.ShapeDtypeStruct((adapters, rank, rest), F32),
        ],
        scratch_shapes=[pltpu.VMEM((adapters, rank, columns), F32)],
        compiler_params=params(),
        name="head_sums",
    )(ids, got)


def rope_tables(length):
    half_dim = HD // 2
    inverse = ROPE_BASE ** (-jnp.arange(half_dim, dtype=F32) / half_dim)
    angles = jnp.arange(length, dtype=F32)[:, None] * inverse[None, :]
    return jnp.cos(angles), jnp.sin(angles)


def rotate(values, cos, sin):
    half_dim = HD // 2
    a, b = values[..., :half_dim], values[..., half_dim:]
    return jnp.concatenate([a * cos - b * sin, b * cos + a * sin], axis=-1)


def on_device(
    hidden_in,
    per_layer_input,
    out_grad,
    adapter_ids,
    weight_qkv,
    weight_attn_out,
    weight_gate_up,
    weight_down,
    laurel_left,
    laurel_right,
    per_layer_gate,
    per_layer_proj,
    norm_gains,
    head_gains,
    adapter_qkv_in,
    adapter_qkv_out,
    adapter_attn_in,
    adapter_attn_out,
    adapter_ffn_in,
    adapter_ffn_out,
    adapter_down_in,
    adapter_down_out,
):
    rows_here, width = hidden_in.shape
    dp = lax.axis_size("dp")
    length = rows_here * 2
    half = rows_here // 2
    per_group = HEADS // KV
    q_width = per_group * HD
    qkv_width = q_width + 2 * HD
    units = weight_down.shape[0]
    blocks = units // UB
    adapters = adapter_qkv_in.shape[0]
    a = adapter_ids[0]
    t = lax.axis_index("tensor")

    def swap(v):
        return lax.ppermute(v, "tensor", [(0, 1), (1, 0)])

    def in_order(own, other):
        first = jnp.where(t == 0, own, other)
        second = jnp.where(t == 0, other, own)
        return jnp.concatenate([first, second], axis=0)

    def mine(v):
        return lax.dynamic_slice_in_dim(v, t * rows_here, rows_here, axis=0)

    def theirs(v):
        return lax.dynamic_slice_in_dim(v, (1 - t) * rows_here, rows_here, axis=0)

    split = blocks // 4
    rows_packed = laurel_left.shape[0]
    lr = laurel_left.shape[1]
    pd = per_layer_gate.shape[1]
    pack_1 = pack_shards(
        weight_gate_up, 0, split,
        [(weight_qkv[:, 0, :], qkv_width), (weight_attn_out, q_width), (laurel_left.T, lr), (laurel_right, lr)],
        rows_packed, "pack_1",
    )
    gather = lambda v: lax.all_gather(v, "dp", axis=0, tiled=True)
    full_1 = gather(pack_1)
    x_peer = swap(hidden_in)
    pack_2 = pack_shards(weight_gate_up, split, blocks - split, [], rows_packed, "pack_2")
    pack_3 = pack_shards(
        None, 0, 0, [(weight_down, units), (per_layer_gate, pd), (per_layer_proj, pd)],
        rows_packed, "pack_3",
    )
    qkv_at = split * GB
    w_qkv = full_1[:, qkv_at : qkv_at + qkv_width]
    wo_at = qkv_at + qkv_width
    w_o_t = full_1[:, wo_at : wo_at + q_width]
    lau_at = wo_at + q_width
    left = full_1[:, lau_at : lau_at + lr]
    right_t = full_1[:, lau_at + lr : lau_at + 2 * lr]
    ple_column = units // (2 * pd)

    two = jnp.asarray(2.0, BF16)
    qkv_in = adapter_qkv_in[a]
    raw_out = adapter_qkv_out[a].reshape(RANK, qkv_width) * two
    column = jnp.arange(qkv_width)
    member = (column >= q_width).astype(jnp.int32) + (column >= q_width + HD).astype(jnp.int32)
    pick = (jnp.arange(3)[:, None] == member[None, :]).astype(BF16)
    b_qkv = (pick[:, None, :] * raw_out[None]).reshape(3 * RANK, qkv_width)
    a_o = adapter_attn_in[a]
    b_o = adapter_attn_out[a] * two
    a_ffn = adapter_ffn_in[a]
    b_ffn = adapter_ffn_out[a] * two
    b_unit = jnp.swapaxes(b_ffn.reshape(RANK, 2, blocks, UB), 1, 2)
    side = (jnp.arange(2)[:, None] == jnp.arange(2)[None, :]).astype(BF16)
    bgu = (side[:, None, None, :, None] * b_unit[None]).reshape(2 * RANK, 2 * units)
    ad_t = adapter_down_in[a].T
    b_d = adapter_down_out[a] * two

    cos, sin = rope_tables(length)
    x_float = hidden_in.astype(F32)
    x_norm = normed(x_float, norm_gains[0])
    h_own = x_norm.astype(BF16)
    x_all = in_order(hidden_in, x_peer)
    h_all = normed(x_all.astype(F32), norm_gains[0]).astype(BF16)
    u_qkv = dot(h_all, qkv_in).astype(BF16)
    ids = lax.all_gather(jnp.full((16, 128), a, BF16), "dp", axis=0, tiled=False)[:, 0, 0]
    ids = ids.astype(jnp.int32)
    pack_2, _, h_all, u_qkv, bgu, ids = lax.optimization_barrier(
        (pack_2, full_1, h_all, u_qkv, bgu, ids)
    )
    full_2 = gather(pack_2)
    raw = dot(h_all, w_qkv) + dot(u_qkv, b_qkv)
    q_raw = raw[:, :q_width].reshape(length, per_group, HD)
    k_raw = raw[:, q_width : q_width + HD]
    queries = rotate(normed(q_raw, head_gains[0]), cos[:, None], sin[:, None]).astype(BF16)
    keys = rotate(normed(k_raw, head_gains[1]), cos, sin).astype(BF16)
    values = raw[:, q_width + HD :].astype(BF16)
    index = jnp.arange(length) // BLK
    distance = index[:, None] - index[None, :]
    allowed = ((distance >= 0) & (distance < WIN // BLK))[None]
    scores = jnp.einsum("lqd,md->qlm", queries, keys, preferred_element_type=F32) * HD ** (-0.5)
    scores = jnp.where(allowed, scores, NEG_BIG)
    shifted = jnp.exp(scores - jnp.max(scores, axis=-1, keepdims=True))
    probs = (shifted / jnp.sum(shifted, axis=-1, keepdims=True)).astype(BF16)
    context = (
        jnp.einsum("qlm,md->lqd", probs, values, preferred_element_type=F32)
        .reshape(length, q_width)
        .astype(BF16)
    )
    queries = queries.reshape(length, q_width)
    u_attn_f = dot(context, a_o)
    u_attn = u_attn_f.astype(BF16)
    attn_part = dot_nt(context, w_o_t) + dot(u_attn, b_o)
    attn_recv = swap(theirs(attn_part).astype(BF16))
    attn_proj = mine(attn_part) + attn_recv.astype(F32)
    laurel_low = dot(h_own, left).astype(BF16)
    laurel_wide = dot_nt(laurel_low, right_t)
    combined = (
        x_float + normed(attn_proj, norm_gains[1]) + x_norm + normed(laurel_wide, norm_gains[2])
    ) * RSQRT_TWO
    h2_own = normed(combined, norm_gains[3]).astype(BF16)

    h2_peer = swap(h2_own)
    h2 = jnp.concatenate([h2_own[:half], h2_peer[:half], h2_own[half:], h2_peer[half:]], axis=0)
    u_ffn = dot(h2, a_ffn).astype(BF16)
    u_qkv_t, qkv_in_t, a_o_t, a_ffn_t, u_ffn_t = u_qkv.T, qkv_in.T, a_o.T, a_ffn.T, u_ffn.T
    pack_3, _, _ = lax.optimization_barrier((pack_3, full_2, h2_own))
    full_3 = gather(pack_3)
    partial = ffn_up(h2, full_1, split, 0, u_ffn, bgu, ad_t, None)
    ud, g_pre, u_pre, hidden = ffn_up(
        h2, full_2, blocks - split, split, u_ffn, bgu, ad_t, partial
    )
    (queries, keys, values, raw, context, u_qkv_t, qkv_in_t, a_o_t, a_ffn_t, u_ffn_t, b_qkv, b_o, cos, sin, hidden) = (
        lax.optimization_barrier(
            (queries, keys, values, raw, context, u_qkv_t, qkv_in_t, a_o_t, a_ffn_t, u_ffn_t, b_qkv, b_o, cos, sin, hidden)
        )
    )
    fwd_parts, ple_parts = [], []
    for s in range(2):
        own, peer = ffn_down(hidden, full_3, ud, b_d, s)
        if s == 0:
            hidden, peer = lax.optimization_barrier((hidden, peer))
        fwd_parts.append((own, swap(peer)))
    layer_out = []
    for s in range(2):
        own, recv = fwd_parts[s]
        whole, d_ffn_s, d_first_s = ple_both(
            combined, own, recv, out_grad, per_layer_input, full_3, ple_column, norm_gains,
            layer_out, s,
        )
        layer_out = [whole]
        ple_parts.append((d_ffn_s, swap(d_ffn_s), d_first_s))
    packs, early = (full_1, full_2, full_3), blocks * 5 // 8
    common = (g_pre, u_pre, bgu, ad_t, b_d, u_ffn_t, a_ffn_t)
    lau_column = lau_at // (2 * lr)
    (own_0, recv_0, first_0), (own_1, recv_1, first_1) = ple_parts
    d_ffn_parts = [own_0, recv_0, own_1, recv_1]
    grad_ffn, du_0, d_h2_own_0, d_h2_peer_0 = ffn_bwd(
        own_0, recv_0, packs, split, 0, blocks, *common, 0, None, None, True
    )
    d_h2_recv_0 = swap(d_h2_peer_0)
    own_1, _ = lax.optimization_barrier((own_1, d_h2_peer_0))
    send_ffn, du_1, acc_1 = ffn_bwd(
        own_1, recv_1, packs, split, 0, early, *common, 1, grad_ffn, None, False
    )
    d_h2_recv_0, acc_1 = lax.optimization_barrier((d_h2_recv_0, acc_1))
    d_attn_0, *branch = between_bwd(
        first_0, combined, d_h2_own_0, d_h2_recv_0, attn_proj, laurel_low, full_1, lau_column,
        norm_gains, [], 0,
    )
    d_attn_recv_0 = swap(d_attn_0)
    acc_1, _ = lax.optimization_barrier((acc_1, d_attn_0))
    send_ffn, du_1, d_h2_own_1, d_h2_peer_1 = ffn_bwd(
        own_1, recv_1, packs, split, early, blocks - early, *common, 1, grad_ffn,
        (acc_1, du_1, send_ffn), True,
    )
    send_ffn, d_attn_recv_0 = lax.optimization_barrier((send_ffn, d_attn_recv_0))
    got_ffn = lax.all_gather(send_ffn, "dp", axis=0, tiled=False)
    d_attn_1, *branch = between_bwd(
        first_1, combined, d_h2_own_1, swap(d_h2_peer_1), attn_proj, laurel_low, full_1,
        lau_column, norm_gains, branch, 1,
    )
    d_branch, d_norm = branch
    d_attn_recv_1 = swap(d_attn_1)

    d_ffn_all = jnp.concatenate(d_ffn_parts, axis=0)
    du_ffn = jnp.concatenate([du_0, du_1], axis=0).astype(BF16)
    ud_low = ud.astype(BF16)
    shared_ffn = jnp.concatenate(
        [dot_tn(h2, du_ffn).astype(BF16), (2.0 * dot_tn(d_ffn_all, ud_low)).astype(BF16)], axis=1
    )

    pieces = [d_attn_0, d_attn_1, d_attn_recv_0, d_attn_recv_1]
    pieces, shared_ffn = lax.optimization_barrier((pieces, shared_ffn))
    d_h_peer_0, d_h_peer_1, d_raw, d_u, send_heads = attention_bwd(
        pieces, t.astype(jnp.int32).reshape(1), full_1, qkv_at, wo_at // HD, b_o, a_o_t, queries, keys,
        values, probs, raw, head_gains, cos, sin, context, u_qkv_t, b_qkv, qkv_in_t,
    )
    d_h_recv_0 = swap(d_h_peer_0)
    d_raw, d_u, got_ffn = lax.optimization_barrier((d_raw, d_u, got_ffn))
    got_heads = lax.all_gather(send_heads, "dp", axis=0, tiled=False)
    d_attn_all = in_order(
        jnp.concatenate([d_attn_0, d_attn_1], axis=0),
        jnp.concatenate([d_attn_recv_0, d_attn_recv_1], axis=0),
    )
    send = jnp.concatenate(
        [
            shared_ffn,
            (2.0 * dot_tn(d_attn_all, u_attn)).astype(BF16),
            dot_tn(h_all, d_u).astype(BF16),
        ],
        axis=1,
    )
    send, d_h_peer_1 = lax.optimization_barrier((send, d_h_peer_1))
    d_h_recv_1 = swap(d_h_peer_1)
    got = lax.all_to_all(send, ("dp", "tensor"), 0, 0, tiled=True).reshape(2 * dp, -1, send.shape[1])
    out_ffn_out, out_down_in = ffn_adapter_sums(got_ffn, ids, adapters, units)
    d_h_own = dot_nt(mine(d_raw), w_qkv) + dot_nt(mine(d_u), qkv_in)
    got, out_ffn_out, out_down_in, d_h_own = lax.optimization_barrier(
        (got, out_ffn_out, out_down_in, d_h_own)
    )
    out_ffn_in, out_down_out, out_attn_out, out_qkv_in = shared_sums(got, ids, adapters)
    d_h_own, out_qkv_in = lax.optimization_barrier((d_h_own, out_qkv_in))
    final_args = (hidden_in, d_norm, d_branch, d_h_own)
    input_grad = final_bwd(*final_args, d_h_recv_0, norm_gains, [], 0)
    input_grad = final_bwd(*final_args, d_h_recv_1, norm_gains, [input_grad], 1)
    got_heads, input_grad = lax.optimization_barrier((got_heads, input_grad))
    out_qkv_out, out_attn_in = head_sums(got_heads, ids, adapters, qkv_width)
    return (
        layer_out[0],
        input_grad,
        jnp.swapaxes(out_qkv_in, 1, 2),
        out_qkv_out,
        jnp.swapaxes(out_attn_in, 1, 2),
        out_attn_out,
        jnp.swapaxes(out_ffn_in, 1, 2),
        out_ffn_out,
        jnp.swapaxes(out_down_in, 1, 2),
        out_down_out,
    )


def solution(mesh):
    in_specs = (
        P(("dp", "tensor"), None),
        P(("dp", "tensor"), None),
        P(("dp", "tensor"), None),
        P("dp"),
        P("dp", "tensor", None),
        P("tensor", "dp"),
        P("dp", None, "tensor"),
        P("tensor", "dp"),
        P("dp", None),
        P(None, "dp"),
        P("dp", None),
        P(None, "dp"),
        P(),
        P(),
        P(),
        P(None, None, "tensor", None),
        P(None, "tensor", None),
        P(),
        P(),
        P(None, None, None, "tensor"),
        P(None, "tensor", None),
        P(),
    )
    out_specs = (
        P(("dp", "tensor"), None),
        P(("dp", "tensor"), None),
        P(None, ("dp", "tensor"), None),
        P(None, None, "tensor", None),
        P(None, "tensor", None),
        P(None, None, ("dp", "tensor")),
        P(None, ("dp", "tensor"), None),
        P(None, None, None, "tensor"),
        P(None, "tensor", None),
        P(None, None, ("dp", "tensor")),
    )
    return jax.shard_map(
        on_device, mesh=mesh, in_specs=in_specs, out_specs=out_specs, check_vma=False
    )
```

time: 655 us -> 633 us (0.966)
  waiting for transfers between devices: 204 us -> 154 us
  blocking collectives: 0 us -> 34.1 us
    unnamed x0 -> x1, blocking collectives: none -> 34.1 us
    all_gather x3, waiting for transfers between devices: 87.5 us -> 59.1 us  [on_device(): gather = lambda v: lax.all_gather(v, 'dp', axis=0, tiled=True)]
    ppermute x12 -> x13, waiting for transfers between devices: 116 us -> 94.2 us  [swap(): return lax.ppermute(v, 'tensor', [(0, 1), (1, 0)])]
    pallas_call x8 -> x11, Pallas kernels: 97.2 us -> 93.1 us  [the longest x2 42.9 us: ffn_up(): pl.pallas_call(body, grid=(blocks,), in_specs=in_specs, out_specs=[unit_b...]
    dot_general x7 -> x4, matrix products: 23.9 us -> 26.3 us  [dot_nt(): lax.dot_general(a, b, (((1,), (1,)), ((), ())), preferred_element_type=F32)]
    unnamed x115 -> x103, local copies, waits for them, and re-layouts: 22.4 us -> 20.7 us
    ppermute x12 -> x13, starting transfers between devices: 17.9 us -> 19.5 us  [swap(): return lax.ppermute(v, 'tensor', [(0, 1), (1, 0)])]
  transfers between devices with their start and end apart: 18 -> 19, of which waited for: 12 -> 12; matrix products, arithmetic and copies ran while one was open for 23% -> 24% of each run, Pallas kernels for 33% -> 33%
where the time goes in v3:
time: 633 us; the launch traced here: 624 us
  Pallas kernels  233 us (37%)
  waiting for transfers between devices  154 us (24%)
  matrix products  58.8 us (9%)
  local copies, waits for them, and re-layouts  53.8 us (8%)
  other arithmetic  51.5 us (8%)
  blocking collectives  34.1 us (5%)
  starting transfers between devices  23.8 us (4%)
  between operations  15.4 us (2%)
    ppermute x13, waiting for transfers between devices, swap(): return lax.ppermute(v, 'tensor', [(0, 1), (1, 0)])  94.2 us
    pallas_call x3, Pallas kernels, ffn_bwd(): pl.pallas_call(body, grid=(blocks,), in_specs=in_specs, out_specs=out_spe...  76.8 us
    all_gather x3, waiting for transfers between devices, on_device(): gather = lambda v: lax.all_gather(v, 'dp', axis=0, tiled=True)  59.1 us
    pallas_call x2, Pallas kernels, ffn_up(): pl.pallas_call(body, grid=(blocks,), in_specs=in_specs, out_specs=[unit_b...  42.9 us
    unnamed x1, blocking collectives  34.1 us
    pallas_call x1, Pallas kernels, attention_bwd(): pl.pallas_call(body, grid=(heads,), in_specs=[pl.BlockSpec(memory_space=p...  26.5 us
    dot_general x4, matrix products, dot_nt(): lax.dot_general(a, b, (((1,), (1,)), ((), ())), preferred_element_type=F32)  26.3 us
    pallas_call x2, Pallas kernels, ffn_down(): pl.pallas_call(body, grid=(width // chunk,), in_specs=[row_const(units),...  24.1 us
  transfers between devices with their start and end apart: 19, of which 12 were waited for; matrix products, arithmetic and copies ran while one was open for 24% of the time, Pallas kernels for 33%

profile of v3, /device:TPU:0, one launch (start us, length us, event | category | flops | bytes accessed | tf_op | source)
XLA Modules:
  0.0 624.1 jit_solution(1973226003153251319)
XLA Ops:
  16.2 34.1 %all-reduce = bf16[16]{0:T(256)(128)(2,1)S(1)} all-reduce(bf16[16]{0:T(256)(128)(2,1)S(1)} %dynamic-update-slice), channel_id=2, replica_groups=mesh['dp'=16,'tensor'=2] {'dp'}, use_global_device_ids=true, to_apply=%add | all-reduce | flops 16 | bytes 64
  69.9 45.9 %all-gather.8.cloned.1.call-done.refs_1_.refs_9_.w_ref.refs_4_.refs_5_ = bf16[2048,4736]{1,0:T(8,128)(2,1)} async-done(((bf16[128,4736]{1,0:T(8,128)(2,1)}), bf16[2048,4736]{1,0:T(8,128)(2,1)}) %all-gather.8.cloned.1.call-update) | async-done | bytes 19398672 | tf_op jit(solution)/shard_map/all_gather | solution.py:810
  120.9 8.1 %fusion.7 = f32[768,1536]{1,0:T(8,128)S(1)} fusion(bf16[768,2048]{1,0:T(8,128)(2,1)} %copy-done.3, bf16[2048,4736]{1,0:T(8,128)(2,1)} %all-gather.8.cloned.1.call-done.refs_1_.refs_9_.w_ref.refs_4_.refs_5_), kind=kOutput, calls=%fused_computation.12 | convolution fusion | flops 4831838208 | bytes 14155776 | tf_op jit(solution)/shard_map/dot_general | solution.py:33
  156.2 14.6 %fusion.95 = (f32[4,768]{1,0:T(4,128)S(1)}, f32[4,768,768]{2,1,0:T(8,128)}) fusion(f32[768,768,4]{0,1,2:T(8,128)} %fusion.56, pred[768,768]{1,0:T(8,128)(4,1)S(1)} %copy-done.36), kind=kOutput, calls=%fused_computation.160 | output fusion | flops 14156543 | bytes 19476480 | tf_op jit(solution)/shard_map/sub | solution.py:868
  179.4 17.2 %fusion.12 = f32[768,2048]{1,0:T(8,128)S(1)} fusion(bf16[768,1024]{0,1:T(8,128)(2,1)S(1)} %bitcast.103, bf16[2048,4736]{1,0:T(8,128)(2,1)} %all-gather.8.cloned.1.call-done.refs_1_.refs_9_.w_ref.refs_4_.refs_5_), kind=kOutput, calls=%fused_computation.20 | convolution fusion | flops 3221225472 | bytes 12058624 | tf_op jit(solution)/shard_map/dot_general | solution.py:37
  210.2 28.4 %collective-permute-done.1 = bf16[384,2048]{1,0:T(8,128)(2,1)} collective-permute-done((bf16[384,2048]{1,0:T(8,128)(2,1)}, bf16[384,2048]{1,0:T(8,128)(2,1)}, u32[]{:S(2)}, u32[]{:S(2)}) %collective-permute-start.1) | collective-permute-done | bytes 1572896 | tf_op jit(solution)/shard_map/ppermute | solution.py:788
  262.0 24.7 %collective-permute-done.2 = bf16[384,2048]{1,0:T(8,128)(2,1)} collective-permute-done((bf16[384,2048]{1,0:T(8,128)(2,1)}, bf16[384,2048]{1,0:T(8,128)(2,1)}, u32[]{:S(2)}, u32[]{:S(2)}) %collective-permute-start.2) | collective-permute-done | bytes 1572896 | tf_op jit(solution)/shard_map/ppermute | solution.py:788
  293.2 13.0 %ffn_up.2 = (bf16[768,4096]{1,0:T(8,128)(2,1)}, bf16[768,4096]{1,0:T(8,128)(2,1)}, bf16[768,4096]{1,0:T(8,128)(2,1)}, f32[768,16]{1,0:T(8,128)}) custom-call(bf16[768,2048]{1,0:T(8,128)(2,1)} %copy-done.5, bf16[2048,4736]{1,0:T(8,128)(2,1)} %all-gather.8.cloned.1.call-done.refs_1_.refs_9_.w_ref.refs_4_.refs_5_, bf16[768,32]{1,0:T(8,128)(2,1)} %copy.72.refs_2_, ...), custom_call_target="tpu_custom_call" | custom-call | flops 6442450944 | bytes 8388608 | tf_op jit(solution)/shard_map/ffn_up/pallas_call | solution.py:156
  306.1 29.9 %ffn_up.3 = (bf16[768,4096]{1,0:T(8,128)(2,1)}, bf16[768,4096]{1,0:T(8,128)(2,1)}, bf16[768,4096]{1,0:T(8,128)(2,1)}, f32[768,16]{1,0:T(8,128)}) custom-call(bf16[768,2048]{1,0:T(8,128)(2,1)} %copy-done.5, bf16[2048,6144]{1,0:T(8,128)(2,1)} %all-gather.10.cloned.1.call-done.refs_1_.refs_10_, ...), custom_call_target="tpu_custom_call", output_to_operand_aliasing={{0}: (6, {}), {1}: (7, {}), {2}: (8, {})} | custom-call | flops 19327352832 | bytes 25165824 | tf_op jit(solution)/shard_map/ffn_up/pallas_call | solution.py:156
  336.1 11.2 %all-gather.12.cloned.1.call-done.w_ref.refs_11_ = bf16[2048,4608]{1,0:T(8,128)(2,1)} async-done(((bf16[128,4608]{1,0:T(8,128)(2,1)}), bf16[2048,4608]{1,0:T(8,128)(2,1)}) %all-gather.12.cloned.1.call-update) | async-done | bytes 18874384 | tf_op jit(solution)/shard_map/all_gather | solution.py:810
  347.3 12.0 %ffn_down.2 = (f32[192,2048]{1,0:T(8,128)}, bf16[192,2048]{1,0:T(8,128)(2,1)}) custom-call(bf16[768,4096]{1,0:T(8,128)(2,1)} %get-tuple-element.118.h_ref, bf16[2048,4608]{1,0:T(8,128)(2,1)} %all-gather.12.cloned.1.call-done.w_ref.refs_11_, f32[768,16]{1,0:T(8,128)} %get-tuple-element.116.ud_ref, bf16[16,2048]{1,0:T(8,128)(2,1)} %multiply_bitcast_fusion.bd_ref.refs_6_), custom_call_target="tpu_custom_call" | custom-call | flops 6442450944 | bytes 16777216 | tf_op jit(solution)/shard_map/ffn_down/pallas_call | solution.py:188
  360.8 12.0 %ffn_down.3 = (f32[192,2048]{1,0:T(8,128)}, bf16[192,2048]{1,0:T(8,128)(2,1)}) custom-call(bf16[768,4096]{1,0:T(8,128)(2,1)} %get-tuple-element.118.h_ref, bf16[2048,4608]{1,0:T(8,128)(2,1)} %all-gather.12.cloned.1.call-done.w_ref.refs_11_, f32[768,16]{1,0:T(8,128)} %get-tuple-element.116.ud_ref, bf16[16,2048]{1,0:T(8,128)(2,1)} %multiply_bitcast_fusion.bd_ref.refs_6_), custom_call_target="tpu_custom_call" | custom-call | flops 6442450944 | bytes 16777216 | tf_op jit(solution)/shard_map/ffn_down/pallas_call | solution.py:188
  373.4 6.5 %collective-permute-done.4.fr_ref = bf16[192,2048]{1,0:T(8,128)(2,1)S(1)} collective-permute-done((bf16[192,2048]{1,0:T(8,128)(2,1)}, bf16[192,2048]{1,0:T(8,128)(2,1)S(1)}, u32[]{:S(2)}, u32[]{:S(2)}) %collective-permute-start.4) | collective-permute-done | bytes 786464 | tf_op jit(solution)/shard_map/ppermute | solution.py:788
  380.8 8.4 %ple_both.2 = (bf16[384,2048]{1,0:T(8,128)(2,1)}, bf16[192,2048]{1,0:T(8,128)(2,1)}, f32[192,2048]{1,0:T(8,128)}) custom-call(f32[384,2048]{1,0:T(8,128)} %get-tuple-element.209.c_ref, f32[192,2048]{1,0:T(8,128)} %get-tuple-element.121.fo_ref, bf16[192,2048]{1,0:T(8,128)(2,1)} %copy-done.33, bf16[384,2048]{1,0:T(8,128)(2,1)} %og_ref.3, ...), custom_call_target="tpu_custom_call" | custom-call | flops 805306368 | bytes 7864320 | tf_op jit(solution)/shard_map/ple_both/pallas_call | solution.py:399
  397.6 8.2 %ple_both.3 = (bf16[384,2048]{1,0:T(8,128)(2,1)}, bf16[192,2048]{1,0:T(8,128)(2,1)}, f32[192,2048]{1,0:T(8,128)}) custom-call(f32[384,2048]{1,0:T(8,128)} %get-tuple-element.209.c_ref, f32[192,2048]{1,0:T(8,128)} %get-tuple-element.119.fo_ref, bf16[192,2048]{1,0:T(8,128)(2,1)} %copy-done.34, ...), custom_call_target="tpu_custom_call", output_to_operand_aliasing={{0}: (7, {})} | custom-call | flops 805306368 | bytes 7864320 | tf_op jit(solution)/shard_map/ple_both/pallas_call | solution.py:399
  414.5 35.1 %ffn_bwd.3 = (f32[48,4096]{1,0:T(8,128)}, f32[384,32]{1,0:T(8,128)}, f32[192,2048]{1,0:T(8,128)}, bf16[192,2048]{1,0:T(8,128)(2,1)}) custom-call(bf16[192,2048]{1,0:T(8,128)(2,1)} %get-tuple-element.126.refs_0_, bf16[192,2048]{1,0:T(8,128)(2,1)} %copy-done.31, bf16[768,4096]{1,0:T(8,128)(2,1)} %get-tuple-element.127.refs_2_, ...), custom_call_target="tpu_custom_call" | custom-call | flops 19327352832 | bytes 50331648 | tf_op jit(solution)/shard_map/ffn_bwd/pallas_call | solution.py:345
  452.1 24.0 %ffn_bwd.4 = (bf16[48,4096]{1,0:T(8,128)(2,1)}, f32[384,32]{1,0:T(8,128)}, f32[384,2048]{1,0:T(8,128)}) custom-call(bf16[192,2048]{1,0:T(8,128)(2,1)} %get-tuple-element.134.refs_0_, bf16[192,2048]{1,0:T(8,128)(2,1)} %copy-done.19, bf16[768,4096]{1,0:T(8,128)(2,1)} %get-tuple-element.127.refs_2_, bf16[768,4096]{1,0:T(8,128)(2,1)} %get-tuple-element.128.refs_3_, ...), custom_call_target="tpu_custom_call" | custom-call | flops 12079595520 | bytes 31457280 | tf_op jit(solution)/shard_map/ffn_bwd/pallas_call | solution.py:345
  477.0 6.6 %between_bwd.2 = (bf16[192,2048]{1,0:T(8,128)(2,1)}, f32[384,2048]{1,0:T(8,128)}, f32[384,2048]{1,0:T(8,128)}) custom-call(f32[192,2048]{1,0:T(8,128)} %get-tuple-element.125.df_ref, f32[384,2048]{1,0:T(8,128)} %get-tuple-element.209.c_ref, f32[192,2048]{1,0:T(8,128)} %get-tuple-element.131.ho_ref, bf16[192,2048]{1,0:T(8,128)(2,1)} %copy-done.35, ...), custom_call_target="tpu_custom_call" | custom-call | flops 150994944 | bytes 10223616 | tf_op jit(solution)/shard_map/between_bwd/pallas_call | solution.py:449
  484.2 17.6 %ffn_bwd.5 = (bf16[48,4096]{1,0:T(8,128)(2,1)}, f32[384,32]{1,0:T(8,128)}, f32[192,2048]{1,0:T(8,128)}, bf16[192,2048]{1,0:T(8,128)(2,1)}) custom-call(bf16[192,2048]{1,0:T(8,128)(2,1)} %get-tuple-element.134.refs_0_, bf16[192,2048]{1,0:T(8,128)(2,1)} %copy-done.19, bf16[768,4096]{1,0:T(8,128)(2,1)} %get-tuple-element.127.refs_2_, ...), custom_call_target="tpu_custom_call", output_to_operand_aliasing={{0}: (15, {})} | custom-call | flops 7247757312 | bytes 18874368 | tf_op jit(solution)/shard_map/ffn_bwd/pallas_call | solution.py:345
  512.0 7.9 %collective-permute-done.8.hr_ref = bf16[192,2048]{1,0:T(8,128)(2,1)} collective-permute-done((bf16[192,2048]{1,0:T(8,128)(2,1)}, bf16[192,2048]{1,0:T(8,128)(2,1)}, u32[]{:S(2)}, u32[]{:S(2)}) %collective-permute-start.8) | collective-permute-done | bytes 786464 | tf_op jit(solution)/shard_map/ppermute | solution.py:788
  519.9 6.6 %between_bwd.3 = (bf16[192,2048]{1,0:T(8,128)(2,1)}, f32[384,2048]{1,0:T(8,128)}, f32[384,2048]{1,0:T(8,128)}) custom-call(f32[192,2048]{1,0:T(8,128)} %get-tuple-element.139.df_ref, f32[384,2048]{1,0:T(8,128)} %get-tuple-element.209.c_ref, f32[192,2048]{1,0:T(8,128)} %get-tuple-element.144.ho_ref, ...), custom_call_target="tpu_custom_call", output_to_operand_aliasing={{1}: (8, {}), {2}: (9, {})} | custom-call | flops 150994944 | bytes 10223616 | tf_op jit(solution)/shard_map/between_bwd/pallas_call | solution.py:449
  531.2 12.3 %collective-permute-done.10.refs_3_ = bf16[192,2048]{1,0:T(8,128)(2,1)S(1)} collective-permute-done((bf16[192,2048]{1,0:T(8,128)(2,1)}, bf16[192,2048]{1,0:T(8,128)(2,1)S(1)}, u32[]{:S(2)}, u32[]{:S(2)}) %collective-permute-start.10) | collective-permute-done | bytes 786464 | tf_op jit(solution)/shard_map/ppermute | solution.py:788
  544.3 26.5 %attention_bwd.1 = (bf16[192,2048]{1,0:T(8,128)(2,1)}, bf16[192,2048]{1,0:T(8,128)(2,1)}, bf16[768,1536]{1,0:T(8,128)(2,1)}, bf16[768,48]{1,0:T(8,128)(2,1)}, bf16[16,2560]{1,0:T(8,128)(2,1)}) custom-call(s32[1]{0:T(128)} %bitcast.33.turn_ref, bf16[192,2048]{1,0:T(8,128)(2,1)} %get-tuple-element.153.refs_0_, bf16[192,2048]{1,0:T(8,128)(2,1)} %get-tuple-element.154.refs_1_, ...), custom_call_target="tpu_custom_call" | custom-call | flops 1048576 | bytes 1048576 | tf_op jit(solution)/shard_map/attention_bwd/pallas_call | solution.py:561
  585.7 6.9 %adapter_sums.1 = (f32[8,16,2,4096]{3,2,1,0:T(2,128)}, f32[8,16,4096]{2,1,0:T(8,128)}) custom-call(s32[16]{0:T(128)} %convert_element_type.142.ids_ref, bf16[16,48,4096]{2,1,0:T(8,128)(2,1)} %bitcast.101), custom_call_target="tpu_custom_call" | custom-call | flops 6291456 | bytes 6291456 | tf_op jit(solution)/shard_map/adapter_sums/pallas_call | solution.py:663
  (227 shorter events, 191.0 us)
Async XLA Ops:
  7.2 61.6 %copy-start = (bf16[8,2048,48]{1,2,0:T(8,128)(2,1)S(1)}, bf16[8,2048,48]{1,2,0:T(8,128)(2,1)}, u32[]{:S(2)}) copy-start(bf16[8,2048,48]{1,2,0:T(8,128)(2,1)} %param.36) | copy-start | bytes 4718596
  7.2 108.5 %all-gather.8.cloned.1.call-start = ((), (), s32[]{:S(2)}) async-start(), calls=%async_computation.1 | async-start | bytes 20611072 | tf_op jit(solution)/shard_map/all_gather | solution.py:810
  11.1 235.6 %all-gather.10.cloned.1.call-start = ((), (), s32[]{:S(2)}) async-start(), calls=%async_computation.2 | async-start | bytes 26738688 | tf_op jit(solution)/shard_map/all_gather | solution.py:810
  11.1 52.9 %collective-permute-start = (bf16[384,2048]{1,0:T(8,128)(2,1)S(1)}, bf16[384,2048]{1,0:T(8,128)(2,1)}, u32[]{:S(2)}, u32[]{:S(2)}) collective-permute-start(bf16[384,2048]{1,0:T(8,128)(2,1)S(1)} %copy-done.4), channel_id=1, source_target_pairs={{0,1},{1,0},{2,3},{3,2},{4,5},{5,4},{6,7},{7,6},{8,9},{9,8},{10,11... | collective-permute-start | bytes 4718600 | tf_op jit(solution)/shard_map/ppermute | solution.py:788
  68.8 47.8 %copy-start.45 = (f32[2,256]{1,0:T(2,128)S(1)}, f32[2,256]{1,0:T(2,128)}, u32[]{:S(2)}) copy-start(f32[2,256]{1,0:T(2,128)} %refs_14_.1) | copy-start | bytes 6148
  69.8 59.2 %copy-start.30 = (bf16[768,48]{0,1:T(8,128)(2,1)}, bf16[768,48]{0,1:T(8,128)(2,1)S(1)}, u32[]{:S(2)}) copy-start(bf16[768,48]{0,1:T(8,128)(2,1)S(1)} %convolution_convert_fusion.3) | copy-start | bytes 221188
  115.8 231.5 %all-gather.12.cloned.1.call-start = ((), (), s32[]{:S(2)}) async-start(), calls=%async_computation.3 | async-start | bytes 20054016 | tf_op jit(solution)/shard_map/all_gather | solution.py:810
  201.6 37.0 %collective-permute-start.1 = (bf16[384,2048]{1,0:T(8,128)(2,1)}, bf16[384,2048]{1,0:T(8,128)(2,1)}, u32[]{:S(2)}, u32[]{:S(2)}) collective-permute-start(bf16[384,2048]{1,0:T(8,128)(2,1)} %dynamic-slice_convert_fusion), channel_id=1, source_target_pairs={{0,1},{1,0},{2,3},{3,2},{4,5},{5,4},{6,7},{7,6},{8,9},{9,8},{10,11... | collective-permute-start | bytes 4718600 | tf_op jit(solution)/shard_map/ppermute | solution.py:788
  206.1 32.5 %copy-start.8 = (f32[768,2048]{1,0:T(8,128)S(1)}, f32[768,2048]{1,0:T(8,128)}, u32[]{:S(2)}) copy-start(f32[768,2048]{1,0:T(8,128)} %copy-done.7) | copy-start | bytes 18874372
  210.1 30.4 %copy-start.43 = (f32[1,2048]{1,0:T(1,128)S(1)}, f32[1,2048]{1,0:T(1,128)}, u32[]{:S(2)}) copy-start(f32[1,2048]{1,0:T(1,128)} %get-tuple-element.219) | copy-start | bytes 24580
  246.7 329.1 %all-gather.16.cloned.1.call-start = ((), (), s32[]{:S(2)}) async-start(), calls=%async_computation.5 | async-start | bytes 6684672 | tf_op jit(solution)/shard_map/all_gather | solution.py:943
  249.8 36.9 %collective-permute-start.2 = (bf16[384,2048]{1,0:T(8,128)(2,1)}, bf16[384,2048]{1,0:T(8,128)(2,1)}, u32[]{:S(2)}, u32[]{:S(2)}) collective-permute-start(bf16[384,2048]{1,0:T(8,128)(2,1)} %get-tuple-element.208), channel_id=1, source_target_pairs={{0,1},{1,0},{2,3},{3,2},{4,5},{5,4},{6,7},{7,6},{8,9},{9,8},{10,11... | collective-permute-start | bytes 4718600 | tf_op jit(solution)/shard_map/ppermute | solution.py:788
  359.3 20.6 %collective-permute-start.4 = (bf16[192,2048]{1,0:T(8,128)(2,1)}, bf16[192,2048]{1,0:T(8,128)(2,1)S(1)}, u32[]{:S(2)}, u32[]{:S(2)}) collective-permute-start(bf16[192,2048]{1,0:T(8,128)(2,1)} %get-tuple-element.122), channel_id=1, source_target_pairs={{0,1},{1,0},{2,3},{3,2},{4,5},{5,4},{6,7},{7,6},{8,9},{9,8},{10,11... | collective-permute-start | bytes 2359304 | tf_op jit(solution)/shard_map/ppermute | solution.py:788
  372.8 23.9 %collective-permute-start.3 = (bf16[192,2048]{1,0:T(8,128)(2,1)}, bf16[192,2048]{1,0:T(8,128)(2,1)S(1)}, u32[]{:S(2)}, u32[]{:S(2)}) collective-permute-start(bf16[192,2048]{1,0:T(8,128)(2,1)} %get-tuple-element.120), channel_id=1, source_target_pairs={{0,1},{1,0},{2,3},{3,2},{4,5},{5,4},{6,7},{7,6},{8,9},{9,8},{10,11... | collective-permute-start | bytes 2359304 | tf_op jit(solution)/shard_map/ppermute | solution.py:788
  389.2 24.4 %collective-permute-start.5 = (bf16[192,2048]{1,0:T(8,128)(2,1)}, bf16[192,2048]{1,0:T(8,128)(2,1)S(1)}, u32[]{:S(2)}, u32[]{:S(2)}) collective-permute-start(bf16[192,2048]{1,0:T(8,128)(2,1)} %get-tuple-element.126.refs_0_), channel_id=1, source_target_pairs={{0,1},{1,0},{2,3},{3,2},{4,5},{5,4},{6,7},{7,6},{8,9},{9,8},{10,11... | collective-permute-start | bytes 2359304 | tf_op jit(solution)/shard_map/ppermute | solution.py:788
  405.9 45.3 %collective-permute-start.7 = (bf16[192,2048]{1,0:T(8,128)(2,1)}, bf16[192,2048]{1,0:T(8,128)(2,1)S(1)}, u32[]{:S(2)}, u32[]{:S(2)}) collective-permute-start(bf16[192,2048]{1,0:T(8,128)(2,1)} %get-tuple-element.134.refs_0_), channel_id=1, source_target_pairs={{0,1},{1,0},{2,3},{3,2},{4,5},{5,4},{6,7},{7,6},{8,9},{9,8},{10,11... | collective-permute-start | bytes 2359304 | tf_op jit(solution)/shard_map/ppermute | solution.py:788
  449.7 26.4 %collective-permute-start.6 = (bf16[192,2048]{1,0:T(8,128)(2,1)}, bf16[192,2048]{1,0:T(8,128)(2,1)S(1)}, u32[]{:S(2)}, u32[]{:S(2)}) collective-permute-start(bf16[192,2048]{1,0:T(8,128)(2,1)} %get-tuple-element.132), channel_id=1, source_target_pairs={{0,1},{1,0},{2,3},{3,2},{4,5},{5,4},{6,7},{7,6},{8,9},{9,8},{10,11... | collective-permute-start | bytes 2359304 | tf_op jit(solution)/shard_map/ppermute | solution.py:788
  483.6 18.3 %collective-permute-start.9 = (bf16[192,2048]{1,0:T(8,128)(2,1)}, bf16[192,2048]{1,0:T(8,128)(2,1)}, u32[]{:S(2)}, u32[]{:S(2)}) collective-permute-start(bf16[192,2048]{1,0:T(8,128)(2,1)} %get-tuple-element.153.refs_0_), channel_id=1, source_target_pairs={{0,1},{1,0},{2,3},{3,2},{4,5},{5,4},{6,7},{7,6},{8,9},{9,8},{10,11... | collective-permute-start | bytes 2359304 | tf_op jit(solution)/shard_map/ppermute | solution.py:788
  501.9 112.7 %all-gather.14.cloned.1.call-start = ((), (), s32[]{:S(2)}) async-start(), calls=%async_computation.4 | async-start | bytes 1392640 | tf_op jit(solution)/shard_map/all_gather | solution.py:966
  501.9 18.0 %collective-permute-start.8 = (bf16[192,2048]{1,0:T(8,128)(2,1)}, bf16[192,2048]{1,0:T(8,128)(2,1)}, u32[]{:S(2)}, u32[]{:S(2)}) collective-permute-start(bf16[192,2048]{1,0:T(8,128)(2,1)} %get-tuple-element.145), channel_id=1, source_target_pairs={{0,1},{1,0},{2,3},{3,2},{4,5},{5,4},{6,7},{7,6},{8,9},{9,8},{10,11... | collective-permute-start | bytes 2359304 | tf_op jit(solution)/shard_map/ppermute | solution.py:788
  526.5 17.0 %collective-permute-start.10 = (bf16[192,2048]{1,0:T(8,128)(2,1)}, bf16[192,2048]{1,0:T(8,128)(2,1)S(1)}, u32[]{:S(2)}, u32[]{:S(2)}) collective-permute-start(bf16[192,2048]{1,0:T(8,128)(2,1)} %get-tuple-element.154.refs_1_), channel_id=1, source_target_pairs={{0,1},{1,0},{2,3},{3,2},{4,5},{5,4},{6,7},{7,6},{8,9},{9,8},{10,11... | collective-permute-start | bytes 2359304 | tf_op jit(solution)/shard_map/ppermute | solution.py:788
  570.9 32.4 %collective-permute-start.12 = (bf16[192,2048]{1,0:T(8,128)(2,1)}, bf16[192,2048]{1,0:T(8,128)(2,1)}, u32[]{:S(2)}, u32[]{:S(2)}) collective-permute-start(bf16[192,2048]{1,0:T(8,128)(2,1)} %get-tuple-element.189), channel_id=1, source_target_pairs={{0,1},{1,0},{2,3},{3,2},{4,5},{5,4},{6,7},{7,6},{8,9},{9,8},{10,11... | collective-permute-start | bytes 2359304 | tf_op jit(solution)/shard_map/ppermute | solution.py:788
  579.8 20.1 %all-to-all-start = ((bf16[32,64,112]{2,1,0:T(8,128)(2,1)}), bf16[32,64,112]{2,1,0:T(8,128)(2,1)S(1)}, u32[]{:S(2)}, u32[]{:S(2)}) async-start(bf16[32,64,112]{2,1,0:T(8,128)(2,1)} %bitcast.36), calls=%async_computation | async-start | bytes 1048576 | tf_op jit(solution)/shard_map/all_to_all | solution.py:981
  583.8 25.7 %collective-permute-start.11 = (bf16[192,2048]{1,0:T(8,128)(2,1)}, bf16[192,2048]{1,0:T(8,128)(2,1)S(1)}, u32[]{:S(2)}, u32[]{:S(2)}) collective-permute-start(bf16[192,2048]{1,0:T(8,128)(2,1)} %get-tuple-element.188), channel_id=1, source_target_pairs={{0,1},{1,0},{2,3},{3,2},{4,5},{5,4},{6,7},{7,6},{8,9},{9,8},{10,11... | collective-permute-start | bytes 2359304 | tf_op jit(solution)/shard_map/ppermute | solution.py:788
  (44 other events, 306.1 us)
Sparse Core Ops, SparseCore 0:
  11.2 104.5 all-gather.7
  117.9 128.7 all-gather.9
  248.3 98.9 all-gather.11
  502.0 61.7 all-gather.15
  572.6 39.9 all-gather.13

commit v4 on v3

--- a/solution.py
+++ b/solution.py
@@ -25,8 +25,9 @@
 
 F32 = jnp.float32
 BF16 = jnp.bfloat16
-VMEM_LIMIT = 58 * 1024 * 1024
+VMEM_LIMIT = 63 * 1024 * 1024
 DOWN_CHUNK = 512
+STREAMS = 3
 
 
 def dot(a, b):
@@ -171,20 +172,21 @@
     return ud, g, u, hidden
 
 
-def ffn_down(hidden, packed, ud, bd, rb):
+def ffn_down(hidden, packed, ud, bd, rb, streams):
     rows, units = hidden.shape
     width = packed.shape[0]
-    r = rows // 2
-    half = r // 2
+    part = rows // (2 * STREAMS)
+    r = 2 * part * streams
     chunk = DOWN_CHUNK
 
-    def body(h_ref, w_ref, ud_ref, bd_ref, own_out, peer_out):
+    def body(h_ref, w_ref, ud_ref, bd_ref, *outs):
         total = dot_nt(h_ref[...], w_ref[...]) + dot(ud_ref[...].astype(BF16), bd_ref[...])
-        own_out[...] = total[:half]
-        peer_out[...] = total[half:].astype(BF16)
+        for n, out in enumerate(outs):
+            out[...] = total[n * part : (n + 1) * part].astype(out.dtype)
 
     row_const = lambda n: pl.BlockSpec((r, n), lambda j: (rb, 0), pipeline_mode=pl.Buffered(1))
-    column = pl.BlockSpec((half, chunk), lambda j: (0, j))
+    column = pl.BlockSpec((part, chunk), lambda j: (0, j))
+    shape = jax.ShapeDtypeStruct
     return pl.pallas_call(
         body,
         grid=(width // chunk,),
@@ -194,11 +196,8 @@
             row_const(RANK),
             pl.BlockSpec((RANK, chunk), lambda j: (0, j)),
         ],
-        out_specs=[column, column],
-        out_shape=[
-            jax.ShapeDtypeStruct((half, width), F32),
-            jax.ShapeDtypeStruct((half, width), BF16),
-        ],
+        out_specs=[column] * (2 * streams),
+        out_shape=[shape((part, width), F32), shape((part, width), BF16)] * streams,
         compiler_params=params(),
         cost_estimate=pl.CostEstimate(
             flops=2 * r * width * units, bytes_accessed=2 * width * units, transcendentals=0
@@ -207,30 +206,25 @@
     )(hidden, packed, ud, bd)
 
 
-def ffn_bwd(own, peer, packs, split, first, blocks, g_pre, u_pre, bgu, ad_t, bd, u_t, a_in_t, rb, base, prev, last):
+def ffn_bwd(own, peer, packs, split, g_pre, u_pre, bgu, ad_t, bd, u_t, a_in_t, h2, ud_t, rb, base, grad_type):
     half, width = own.shape
     r = 2 * half
     units = ad_t.shape[1]
+    first, blocks = 0, units // UB
     sub = 256
 
     def body(*refs):
         own_ref, peer_ref, g_ref, u_ref, bgu_ref, ad_ref, bd_ref, ut_ref, ain_ref = refs[:9]
         pack_refs = refs[9 : 9 + len(packs)]
         at = 9 + len(packs)
+        h2_any, udt_ref = refs[at : at + 2]
+        at += 2
         if base is not None:
-            base_ref = refs[at]
-            at += 1
-        if prev is not None:
-            acc_in, du_in = refs[at : at + 2]
-            at += 3
-        grad_out, du_out = refs[at : at + 2]
-        if last:
-            own_out, peer_out = refs[at + 2 : at + 4]
-            at += 4
-        else:
-            acc_out = refs[at + 2]
-            at += 3
-        df, acc, wbuf, dd, du, dgu, hs, sem, acc_sem = refs[at:]
+            base_ref, base_in = refs[at : at + 2]
+            at += 2
+        grad_out, in_out, own_out, peer_out = refs[at : at + 4]
+        at += 4
+        df, acc, wbuf, dd, du, dgu, hs, sem, h2_sem = refs[at:]
         j = pl.program_id(0)
         slot = lax.rem(j, 2)
 
@@ -257,12 +251,8 @@
             fetch(j, 0)
             df[0:half, :] = own_ref[...]
             df[half:r, :] = peer_ref[...]
-            if prev is None:
-                acc[...] = jnp.zeros_like(acc)
-                du[...] = jnp.zeros_like(du)
-            else:
-                pltpu.make_async_copy(acc_in, acc, acc_sem).start()
-                du[...] = du_in[...]
+            acc[...] = jnp.zeros_like(acc)
+            du[...] = jnp.zeros_like(du)
             dd[...] = dot_nt(df[...], bd_ref[...]).astype(BF16)
 
         @pl.when(j + 1 < blocks)
@@ -281,12 +271,6 @@
             dgu[:, UB + n * sub : UB + (n + 1) * sub] = (dh * act).astype(BF16)
             hs[:, cs] = (act * u).astype(BF16)
         copy(pack_refs[0], 0, slot, 1).wait()
-        if prev is not None:
-
-            @pl.when(j == 0)
-            def _():
-                pltpu.make_async_copy(acc_in, acc, acc_sem).wait()
-
         d_both = dgu[...]
         for c in range(width // 512):
             cc = slice(c * 512, (c + 1) * 512)
@@ -302,13 +286,21 @@
 
         @pl.when(j == blocks - 1)
         def _():
-            du_out[...] = du[...]
-            if last:
-                total = acc[...] + dot(du[...].astype(BF16), ain_ref[...])
-                own_out[...] = total[:half]
-                peer_out[...] = total[half:].astype(BF16)
-            else:
-                acc_out[...] = acc[...]
+            down = dot(udt_ref[...], df[...])
+            rows_copy = pltpu.make_async_copy(h2_any.at[pl.ds(rb * r, r), :], df, h2_sem)
+            rows_copy.start()
+            du_low = du[...].astype(BF16)
+            total = acc[...] + dot(du_low, ain_ref[...])
+            own_out[...] = total[:half]
+            peer_out[...] = total[half:].astype(BF16)
+            rows_copy.wait()
+            up = dot_tn(du_low, df[...])
+            down = 2.0 * down
+            if base is not None:
+                up = up + base_in[0 : 2 * RANK, :]
+                down = down + base_in[2 * RANK : 3 * RANK, :]
+            in_out[0 : 2 * RANK, :] = up
+            in_out[2 * RANK : 3 * RANK, :] = down
 
     rows_block = lambda: pl.BlockSpec((r, UB), lambda j: (rb, first + j))
     unit_block = lambda: pl.BlockSpec((RANK, UB), lambda j: (0, first + j))
@@ -325,23 +317,27 @@
         const_spec((2 * RANK, width)),
     ] + [any_spec() for _ in packs]
     args = [own, peer, g_pre, u_pre, bgu, ad_t, bd, u_t, a_in_t, *packs]
-    aliases = {}
     grad_block = lambda: pl.BlockSpec((3 * RANK, UB), lambda j: (0, first + j))
+    in_specs += [
+        any_spec(),
+        pl.BlockSpec((RANK, r), lambda j: (0, rb), pipeline_mode=pl.Buffered(1)),
+    ]
+    args += [h2, ud_t]
     if base is not None:
-        in_specs.append(grad_block())
-        args.append(base)
-    if prev is not None:
-        aliases = {len(args) + 2: 0}
-        in_specs += [any_spec(), const_spec((r, 2 * RANK)), any_spec()]
-        args += list(prev)
-    out_specs = [grad_block(), const_spec((r, 2 * RANK))]
-    out_shape = [shape((3 * RANK, units), F32 if base is None else BF16), shape((r, 2 * RANK), F32)]
-    if last:
-        out_specs += [const_spec((half, width)), const_spec((half, width))]
-        out_shape += [shape((half, width), F32), shape((half, width), BF16)]
-    else:
-        out_specs += [const_spec((r, width))]
-        out_shape += [shape((r, width), F32)]
+        in_specs += [grad_block(), const_spec((3 * RANK, width))]
+        args += list(base)
+    out_specs = [
+        grad_block(),
+        const_spec((3 * RANK, width)),
+        const_spec((half, width)),
+        const_spec((half, width)),
+    ]
+    out_shape = [
+        shape((3 * RANK, units), grad_type),
+        shape((3 * RANK, width), F32),
+        shape((half, width), F32),
+        shape((half, width), BF16),
+    ]
     return pl.pallas_call(
         body,
         grid=(blocks,),
@@ -359,7 +355,6 @@
             pltpu.SemaphoreType.DMA((2, 2)),
             pltpu.SemaphoreType.DMA,
         ],
-        input_output_aliases=aliases,
         compiler_params=params(),
         cost_estimate=pl.CostEstimate(
             flops=6 * r * width * UB * blocks,
@@ -374,7 +369,7 @@
     half, width = ffn_own.shape
     rows = combined.shape[0]
     pd = ple_in.shape[1]
-    tile = half // 2
+    tile = half
 
     def body(c_ref, fo_ref, fr_ref, og_ref, pi_ref, w_ref, gain_ref, *refs):
         out_ref, dffn_ref, dfirst_ref = refs[-3:]
@@ -428,7 +423,7 @@
     half, width = d_first.shape
     rows = combined.shape[0]
     lr = low.shape[1]
-    tile = half // 2
+    tile = half
 
     def body(df_ref, c_ref, ho_ref, hr_ref, ap_ref, low_ref, w_ref, gain_ref, *refs):
         da_ref, db_ref, dn_ref = refs[-3:]
@@ -476,7 +471,7 @@
 
 
 def attention_bwd(pieces, turn, packed, qkv_column, wo_column, bo, ao_t, q, k, v, probs, raw, gains, cos, sin,
-                  context, u_t, b_qkv, a_in_t):
+                  context, u_t, b_qkv, a_in_t, u_attn_t):
     length, q_width = q.shape
     width = packed.shape[0]
     heads = q_width // HD
@@ -496,7 +491,7 @@
     def body(turn_ref, *refs):
         piece_refs = refs[:count]
         (wo_ref, w_any, bo_ref, ao_ref, q_ref, k_ref, v_ref, p_ref, rq_ref, rk_ref, gain_ref, cos_ref,
-         sin_ref, ctx_ref, ut_ref, b_ref, ain_ref, peer_0, peer_1, draw, du_out, heads_out,
+         sin_ref, ctx_ref, ut_ref, b_ref, ain_ref, uat_ref, peer_0, peer_1, draw, du_out, heads_out, out_rows,
          da, du, dk, dv, wq, sem) = refs[count:]
         hh = pl.program_id(0)
         weights = pltpu.make_async_copy(w_any.at[:, pl.ds(qkv_column, total)], wq, sem)
@@ -546,6 +541,7 @@
                 got = dot(ut_ref[m * RANK : (m + 1) * RANK, :], draw[:, where])
                 heads_out[:, where] = (2.0 * got).astype(BF16)
             du_out[...] = dot_nt(draw[...], b_ref[...]).astype(BF16)
+            out_rows[...] = (2.0 * dot(uat_ref[...], da[...])).astype(BF16)
             weights.wait()
             theirs = pl.multiple_of((1 - turn_ref[0]) * here, here)
             d_rows = draw[pl.ds(theirs, here), :]
@@ -581,6 +577,7 @@
             const_spec(u_t.shape),
             const_spec(b_qkv.shape),
             const_spec(a_in_t.shape),
+            const_spec(u_attn_t.shape),
         ],
         out_specs=[
             const_spec((here // 2, width)),
@@ -588,6 +585,7 @@
             const_spec((length, total)),
             const_spec((length, 3 * RANK)),
             const_spec((RANK, total + q_width)),
+            const_spec((RANK, width)),
         ],
         out_shape=[
             shape((here // 2, width), BF16),
@@ -595,6 +593,7 @@
             shape((length, total), BF16),
             shape((length, 3 * RANK), BF16),
             shape((RANK, total + q_width), BF16),
+            shape((RANK, width), BF16),
         ],
         scratch_shapes=[
             pltpu.VMEM((length, width), BF16),
@@ -608,7 +607,7 @@
         cost_estimate=pl.CostEstimate(flops=1024 * 1024, bytes_accessed=1024 * 1024, transcendentals=0),
         name="attention_bwd",
     )(turn, *pieces, packed, packed, bo, ao_t, q, k, v, probs, raw, raw, gains, cos, sin, context, u_t, b_qkv,
-      a_in_t)
+      a_in_t, u_attn_t)
 
 
 def final_bwd(x, d_norm, d_branch, dh_own, dh_recv, gains, prev, rb):
@@ -774,7 +773,7 @@
     rows_here, width = hidden_in.shape
     dp = lax.axis_size("dp")
     length = rows_here * 2
-    half = rows_here // 2
+    part = rows_here // STREAMS
     per_group = HEADS // KV
     q_width = per_group * HD
     qkv_width = q_width + 2 * HD
@@ -886,96 +885,94 @@
     h2_own = normed(combined, norm_gains[3]).astype(BF16)
 
     h2_peer = swap(h2_own)
-    h2 = jnp.concatenate([h2_own[:half], h2_peer[:half], h2_own[half:], h2_peer[half:]], axis=0)
+    h2 = jnp.concatenate(
+        [v[s * part : (s + 1) * part] for s in range(STREAMS) for v in (h2_own, h2_peer)], axis=0
+    )
     u_ffn = dot(h2, a_ffn).astype(BF16)
     u_qkv_t, qkv_in_t, a_o_t, a_ffn_t, u_ffn_t = u_qkv.T, qkv_in.T, a_o.T, a_ffn.T, u_ffn.T
+    u_attn_t = u_attn.T
     pack_3, _, _ = lax.optimization_barrier((pack_3, full_2, h2_own))
     full_3 = gather(pack_3)
     partial = ffn_up(h2, full_1, split, 0, u_ffn, bgu, ad_t, None)
     ud, g_pre, u_pre, hidden = ffn_up(
         h2, full_2, blocks - split, split, u_ffn, bgu, ad_t, partial
     )
-    (queries, keys, values, raw, context, u_qkv_t, qkv_in_t, a_o_t, a_ffn_t, u_ffn_t, b_qkv, b_o, cos, sin, hidden) = (
+    ud_t = ud.astype(BF16).T
+    (queries, keys, values, raw, context, u_qkv_t, qkv_in_t, a_o_t, a_ffn_t, u_ffn_t, b_qkv, b_o, cos, sin, u_attn_t, ud_t, hidden) = (
         lax.optimization_barrier(
-            (queries, keys, values, raw, context, u_qkv_t, qkv_in_t, a_o_t, a_ffn_t, u_ffn_t, b_qkv, b_o, cos, sin, hidden)
+            (queries, keys, values, raw, context, u_qkv_t, qkv_in_t, a_o_t, a_ffn_t, u_ffn_t, b_qkv, b_o, cos, sin, u_attn_t, ud_t, hidden)
         )
     )
-    fwd_parts, ple_parts = [], []
-    for s in range(2):
-        own, peer = ffn_down(hidden, full_3, ud, b_d, s)
+    ple_parts, layer_out = [], []
+    own_0, peer_0, own_1, peer_1 = ffn_down(hidden, full_3, ud, b_d, 0, 2)
+    hidden, peer_0, peer_1 = lax.optimization_barrier((hidden, peer_0, peer_1))
+    own_2, peer_2 = ffn_down(hidden, full_3, ud, b_d, 2, 1)
+    recv_0 = swap(peer_0)
+    recv_1 = swap(peer_1)
+    for s, (own, recv) in enumerate(((own_0, recv_0), (own_1, recv_1), (own_2, None))):
         if s == 0:
-            hidden, peer = lax.optimization_barrier((hidden, peer))
-        fwd_parts.append((own, swap(peer)))
-    layer_out = []
-    for s in range(2):
-        own, recv = fwd_parts[s]
+            recv, own_2 = lax.optimization_barrier((recv, own_2))
+        if s == 2:
+            peer_2, _ = lax.optimization_barrier((peer_2, ple_parts[0][1]))
+            recv = swap(peer_2)
         whole, d_ffn_s, d_first_s = ple_both(
             combined, own, recv, out_grad, per_layer_input, full_3, ple_column, norm_gains,
             layer_out, s,
         )
         layer_out = [whole]
-        ple_parts.append((d_ffn_s, swap(d_ffn_s), d_first_s))
-    packs, early = (full_1, full_2, full_3), blocks * 5 // 8
-    common = (g_pre, u_pre, bgu, ad_t, b_d, u_ffn_t, a_ffn_t)
+        ple_parts.append([d_ffn_s, swap(d_ffn_s), d_first_s])
+    packs = (full_1, full_2, full_3)
+    common = (g_pre, u_pre, bgu, ad_t, b_d, u_ffn_t, a_ffn_t, h2, ud_t)
     lau_column = lau_at // (2 * lr)
-    (own_0, recv_0, first_0), (own_1, recv_1, first_1) = ple_parts
-    d_ffn_parts = [own_0, recv_0, own_1, recv_1]
-    grad_ffn, du_0, d_h2_own_0, d_h2_peer_0 = ffn_bwd(
-        own_0, recv_0, packs, split, 0, blocks, *common, 0, None, None, True
-    )
-    d_h2_recv_0 = swap(d_h2_peer_0)
-    own_1, _ = lax.optimization_barrier((own_1, d_h2_peer_0))
-    send_ffn, du_1, acc_1 = ffn_bwd(
-        own_1, recv_1, packs, split, 0, early, *common, 1, grad_ffn, None, False
-    )
-    d_h2_recv_0, acc_1 = lax.optimization_barrier((d_h2_recv_0, acc_1))
-    d_attn_0, *branch = between_bwd(
-        first_0, combined, d_h2_own_0, d_h2_recv_0, attn_proj, laurel_low, full_1, lau_column,
-        norm_gains, [], 0,
-    )
-    d_attn_recv_0 = swap(d_attn_0)
-    acc_1, _ = lax.optimization_barrier((acc_1, d_attn_0))
-    send_ffn, du_1, d_h2_own_1, d_h2_peer_1 = ffn_bwd(
-        own_1, recv_1, packs, split, early, blocks - early, *common, 1, grad_ffn,
-        (acc_1, du_1, send_ffn), True,
-    )
-    send_ffn, d_attn_recv_0 = lax.optimization_barrier((send_ffn, d_attn_recv_0))
+    d_attn_own, d_attn_recv, branch, waiting, sums = [], [], [], [], None
+
+    def between(branch):
+        d_first_s, d_h2_own, d_h2_recv, s = waiting.pop(0)
+        d_attn_s, *branch = between_bwd(
+            d_first_s, combined, d_h2_own, d_h2_recv, attn_proj, laurel_low, full_1, lau_column,
+            norm_gains, branch, s,
+        )
+        d_attn_own.append(d_attn_s)
+        d_attn_recv.append(swap(d_attn_s))
+        return branch
+
+    for s in range(STREAMS):
+        own, recv, first = ple_parts[s]
+        if s >= 2:
+            own, _ = lax.optimization_barrier((own, d_attn_own[s - 2]))
+        elif s == 1:
+            own, _ = lax.optimization_barrier((own, d_h2_peer))
+        *sums, d_h2_own, d_h2_peer = ffn_bwd(
+            own, recv, packs, split, *common, s, sums, BF16 if s == STREAMS - 1 else F32
+        )
+        send_ffn = sums[0]
+        if waiting:
+            first_w, own_w, recv_w, s_w = waiting[0]
+            if s == STREAMS - 1:
+                send_ffn, recv_w = lax.optimization_barrier((send_ffn, recv_w))
+            else:
+                recv_w, _ = lax.optimization_barrier((recv_w, d_h2_peer))
+            waiting[0] = (first_w, own_w, recv_w, s_w)
+            waiting.append((first, d_h2_own, swap(d_h2_peer), s))
+            branch = between(branch)
+        else:
+            waiting.append((first, d_h2_own, swap(d_h2_peer), s))
+    send_ffn, d_attn_recv[0] = lax.optimization_barrier((send_ffn, d_attn_recv[0]))
     got_ffn = lax.all_gather(send_ffn, "dp", axis=0, tiled=False)
-    d_attn_1, *branch = between_bwd(
-        first_1, combined, d_h2_own_1, swap(d_h2_peer_1), attn_proj, laurel_low, full_1,
-        lau_column, norm_gains, branch, 1,
-    )
-    d_branch, d_norm = branch
-    d_attn_recv_1 = swap(d_attn_1)
-
-    d_ffn_all = jnp.concatenate(d_ffn_parts, axis=0)
-    du_ffn = jnp.concatenate([du_0, du_1], axis=0).astype(BF16)
-    ud_low = ud.astype(BF16)
-    shared_ffn = jnp.concatenate(
-        [dot_tn(h2, du_ffn).astype(BF16), (2.0 * dot_tn(d_ffn_all, ud_low)).astype(BF16)], axis=1
-    )
-
-    pieces = [d_attn_0, d_attn_1, d_attn_recv_0, d_attn_recv_1]
-    pieces, shared_ffn = lax.optimization_barrier((pieces, shared_ffn))
-    d_h_peer_0, d_h_peer_1, d_raw, d_u, send_heads = attention_bwd(
+    d_branch, d_norm = between(branch)
+
+    pieces = d_attn_own + d_attn_recv
+    d_h_peer_0, d_h_peer_1, d_raw, d_u, send_heads, grad_attn_out = attention_bwd(
         pieces, t.astype(jnp.int32).reshape(1), full_1, qkv_at, wo_at // HD, b_o, a_o_t, queries, keys,
         values, probs, raw, head_gains, cos, sin, context, u_qkv_t, b_qkv, qkv_in_t,
+        u_attn_t,
     )
     d_h_recv_0 = swap(d_h_peer_0)
     d_raw, d_u, got_ffn = lax.optimization_barrier((d_raw, d_u, got_ffn))
     got_heads = lax.all_gather(send_heads, "dp", axis=0, tiled=False)
-    d_attn_all = in_order(
-        jnp.concatenate([d_attn_0, d_attn_1], axis=0),
-        jnp.concatenate([d_attn_recv_0, d_attn_recv_1], axis=0),
-    )
     send = jnp.concatenate(
-        [
-            shared_ffn,
-            (2.0 * dot_tn(d_attn_all, u_attn)).astype(BF16),
-            dot_tn(h_all, d_u).astype(BF16),
-        ],
-        axis=1,
-    )
+        [sums[1].astype(BF16), grad_attn_out, dot_tn(d_u, h_all).astype(BF16)], axis=0
+    ).T
     send, d_h_peer_1 = lax.optimization_barrier((send, d_h_peer_1))
     d_h_recv_1 = swap(d_h_peer_1)
     got = lax.all_to_all(send, ("dp", "tensor"), 0, 0, tiled=True).reshape(2 * dp, -1, send.shape[1])

time: 633 us -> 622 us (0.983)
  waiting for transfers between devices: 154 us -> 177 us
  matrix products: 58.8 us -> 39.4 us
  local copies, waits for them, and re-layouts: 53.8 us -> 38.1 us
  other arithmetic: 51.5 us -> 39.9 us
  Pallas kernels: 233 us -> 242 us
    all_gather x3, waiting for transfers between devices: 59.1 us -> 91.4 us  [on_device(): gather = lambda v: lax.all_gather(v, 'dp', axis=0, tiled=True)]
    dot_general x4, matrix products: 26.3 us -> 16 us  [dot_nt(): lax.dot_general(a, b, (((1,), (1,)), ((), ())), preferred_element_type=F32)]
    ppermute x13 -> x17, waiting for transfers between devices: 94.2 us -> 85.8 us  [swap(): return lax.ppermute(v, 'tensor', [(0, 1), (1, 0)])]
    sub x1, other arithmetic: 14.6 us -> 6.53 us  [on_device(): shifted = jnp.exp(scores - jnp.max(scores, axis=-1, keepdims=True))]
    unnamed x103 -> x102, local copies, waits for them, and re-layouts: 20.7 us -> 14.2 us
    pallas_call x2 -> x3, Pallas kernels: 13.2 us -> 15.4 us  [between_bwd(): pl.pallas_call(body, grid=(n,), in_specs=[here(width), there(width), here...]
    ppermute x13 -> x17, starting transfers between devices: 19.5 us -> 21.6 us  [swap(): return lax.ppermute(v, 'tensor', [(0, 1), (1, 0)])]
    pallas_call x2 -> x3, Pallas kernels: 16.6 us -> 18 us  [ple_both(): pl.pallas_call(body, grid=(n,), in_specs=[there(width), here(width), here...]
  transfers between devices with their start and end apart: 19 -> 23, of which waited for: 12 -> 12; matrix products, arithmetic and copies ran while one was open for 24% -> 17% of each run, Pallas kernels for 33% -> 36%
where the time goes in v4:
time: 622 us; the launch traced here: 613 us
  Pallas kernels  242 us (39%)
  waiting for transfers between devices  177 us (28%)
  other arithmetic  39.9 us (6%)
  matrix products  39.4 us (6%)
  local copies, waits for them, and re-layouts  38.1 us (6%)
  blocking collectives  34.1 us (5%)
  starting transfers between devices  26.4 us (4%)
  between operations  15.7 us (3%)
    all_gather x3, waiting for transfers between devices, on_device(): gather = lambda v: lax.all_gather(v, 'dp', axis=0, tiled=True)  91.4 us
    ppermute x17, waiting for transfers between devices, swap(): return lax.ppermute(v, 'tensor', [(0, 1), (1, 0)])  85.8 us
    pallas_call x3, Pallas kernels, ffn_bwd(): pl.pallas_call(body, grid=(blocks,), in_specs=in_specs, out_specs=out_spe...  81.5 us
    pallas_call x2, Pallas kernels, ffn_up(): pl.pallas_call(body, grid=(blocks,), in_specs=in_specs, out_specs=[unit_b...  42.8 us
    unnamed x1, blocking collectives  34.1 us
    pallas_call x1, Pallas kernels, attention_bwd(): pl.pallas_call(body, grid=(heads,), in_specs=[pl.BlockSpec(memory_space=p...  27.1 us
    pallas_call x2, Pallas kernels, ffn_down(): pl.pallas_call(body, grid=(width // chunk,), in_specs=[row_const(units),...  24.5 us
    ppermute x17, starting transfers between devices, swap(): return lax.ppermute(v, 'tensor', [(0, 1), (1, 0)])  21.6 us
  transfers between devices with their start and end apart: 23, of which 12 were waited for; matrix products, arithmetic and copies ran while one was open for 17% of the time, Pallas kernels for 36%

profile of v4, /device:TPU:0, one launch (start us, length us, event | category | flops | bytes accessed | tf_op | source)
XLA Modules:
  0.0 613.0 jit_solution(8987888165802666743)
XLA Ops:
  16.0 34.1 %all-reduce = bf16[16]{0:T(256)(128)(2,1)S(1)} all-reduce(bf16[16]{0:T(256)(128)(2,1)S(1)} %dynamic-update-slice), channel_id=2, replica_groups=mesh['dp'=16,'tensor'=2] {'dp'}, use_global_device_ids=true, to_apply=%add | all-reduce | flops 16 | bytes 64
  50.1 5.9 pack_2.1
  65.9 49.7 %all-gather.8.cloned.1.call-done.refs_1_.refs_9_.w_ref.refs_6_.refs_7_ = bf16[2048,4736]{1,0:T(8,128)(2,1)} async-done(((bf16[128,4736]{1,0:T(8,128)(2,1)}), bf16[2048,4736]{1,0:T(8,128)(2,1)}) %all-gather.8.cloned.1.call-update) | async-done | bytes 19398672 | tf_op jit(solution)/shard_map/all_gather | solution.py:809
  119.9 7.3 %fusion.7 = f32[768,1536]{1,0:T(8,128)S(1)} fusion(bf16[768,2048]{1,0:T(8,128)(2,1)S(1)} %fusion.4, bf16[2048,4736]{1,0:T(8,128)(2,1)} %all-gather.8.cloned.1.call-done.refs_1_.refs_9_.w_ref.refs_6_.refs_7_), kind=kOutput, calls=%fused_computation.12 | convolution fusion | flops 4831838208 | bytes 14155776 | tf_op jit(solution)/shard_map/dot_general | solution.py:34
  146.3 6.5 %fusion.62 = (f32[4,768]{1,0:T(4,128)S(1)}, f32[4,768,768]{2,1,0:T(8,128)}) fusion(f32[768,768,4]{0,1,2:T(8,128)S(1)} %fusion.32, pred[768,768]{1,0:T(8,128)(4,1)S(1)} %copy-done.31), kind=kOutput, calls=%fused_computation.133 | output fusion | flops 14156543 | bytes 19476480 | tf_op jit(solution)/shard_map/sub | solution.py:867
  160.7 5.7 fusion.12
  181.9 26.4 %collective-permute-done.1 = bf16[384,2048]{1,0:T(8,128)(2,1)} collective-permute-done((bf16[384,2048]{1,0:T(8,128)(2,1)}, bf16[384,2048]{1,0:T(8,128)(2,1)}, u32[]{:S(2)}, u32[]{:S(2)}) %collective-permute-start.1) | collective-permute-done | bytes 1572896 | tf_op jit(solution)/shard_map/ppermute | solution.py:787
  214.5 32.0 %all-gather.10.cloned.1.call-done.refs_1_.refs_10_ = bf16[2048,6144]{1,0:T(8,128)(2,1)} async-done(((bf16[128,6144]{1,0:T(8,128)(2,1)}), bf16[2048,6144]{1,0:T(8,128)(2,1)}) %all-gather.10.cloned.1.call-update) | async-done | bytes 25165840 | tf_op jit(solution)/shard_map/all_gather | solution.py:809
  261.4 23.7 %collective-permute-done.2 = bf16[384,2048]{1,0:T(8,128)(2,1)} collective-permute-done((bf16[384,2048]{1,0:T(8,128)(2,1)}, bf16[384,2048]{1,0:T(8,128)(2,1)}, u32[]{:S(2)}, u32[]{:S(2)}) %collective-permute-start.2) | collective-permute-done | bytes 1572896 | tf_op jit(solution)/shard_map/ppermute | solution.py:787
  292.9 13.0 %ffn_up.2 = (bf16[768,4096]{1,0:T(8,128)(2,1)}, bf16[768,4096]{1,0:T(8,128)(2,1)}, bf16[768,4096]{1,0:T(8,128)(2,1)}, f32[768,16]{1,0:T(8,128)}) custom-call(bf16[768,2048]{1,0:T(8,128)(2,1)} %copy-done.4, bf16[2048,4736]{1,0:T(8,128)(2,1)} %all-gather.8.cloned.1.call-done.refs_1_.refs_9_.w_ref.refs_6_.refs_7_, bf16[768,32]{1,0:T(8,128)(2,1)} %copy.74.refs_2_, ...), custom_call_target="tpu_custom_call" | custom-call | flops 6442450944 | bytes 8388608 | tf_op jit(solution)/shard_map/ffn_up/pallas_call | solution.py:157
  305.8 29.8 %ffn_up.3 = (bf16[768,4096]{1,0:T(8,128)(2,1)}, bf16[768,4096]{1,0:T(8,128)(2,1)}, bf16[768,4096]{1,0:T(8,128)(2,1)}, f32[768,16]{1,0:T(8,128)}) custom-call(bf16[768,2048]{1,0:T(8,128)(2,1)} %copy-done.4, bf16[2048,6144]{1,0:T(8,128)(2,1)} %all-gather.10.cloned.1.call-done.refs_1_.refs_10_, ...), custom_call_target="tpu_custom_call", output_to_operand_aliasing={{0}: (6, {}), {1}: (7, {}), {2}: (8, {})} | custom-call | flops 19327352832 | bytes 25165824 | tf_op jit(solution)/shard_map/ffn_up/pallas_call | solution.py:157
  337.4 9.7 %all-gather.12.cloned.1.call-done.w_ref.refs_11_ = bf16[2048,4608]{1,0:T(8,128)(2,1)} async-done(((bf16[128,4608]{1,0:T(8,128)(2,1)}), bf16[2048,4608]{1,0:T(8,128)(2,1)}) %all-gather.12.cloned.1.call-update) | async-done | bytes 18874384 | tf_op jit(solution)/shard_map/all_gather | solution.py:809
  347.1 14.2 %ffn_down.2 = (f32[128,2048]{1,0:T(8,128)}, bf16[128,2048]{1,0:T(8,128)(2,1)}, f32[128,2048]{1,0:T(8,128)}, bf16[128,2048]{1,0:T(8,128)(2,1)}) custom-call(bf16[768,4096]{1,0:T(8,128)(2,1)} %get-tuple-element.130.h_ref, bf16[2048,4608]{1,0:T(8,128)(2,1)} %all-gather.12.cloned.1.call-done.w_ref.refs_11_, f32[768,16]{1,0:T(8,128)} %get-tuple-element.124.ud_ref, ...), custom_call_target="tpu_custom_call" | custom-call | flops 8589934592 | bytes 16777216 | tf_op jit(solution)/shard_map/ffn_down/pallas_call | solution.py:190
  363.3 10.4 %ffn_down.3 = (f32[128,2048]{1,0:T(8,128)}, bf16[128,2048]{1,0:T(8,128)(2,1)}) custom-call(bf16[768,4096]{1,0:T(8,128)(2,1)} %get-tuple-element.130.h_ref, bf16[2048,4608]{1,0:T(8,128)(2,1)} %all-gather.12.cloned.1.call-done.w_ref.refs_11_, f32[768,16]{1,0:T(8,128)} %get-tuple-element.124.ud_ref, bf16[16,2048]{1,0:T(8,128)(2,1)} %multiply_bitcast_fusion.bd_ref.refs_6_), custom_call_target="tpu_custom_call" | custom-call | flops 4294967296 | bytes 16777216 | tf_op jit(solution)/shard_map/ffn_down/pallas_call | solution.py:190
  376.3 6.0 ple_both.3
  388.3 6.0 ple_both.4
  400.3 26.9 %ffn_bwd.3 = (f32[48,4096]{1,0:T(8,128)}, f32[48,2048]{1,0:T(8,128)}, f32[128,2048]{1,0:T(8,128)}, bf16[128,2048]{1,0:T(8,128)(2,1)}) custom-call(bf16[128,2048]{1,0:T(8,128)(2,1)} %get-tuple-element.136.refs_0_, bf16[128,2048]{1,0:T(8,128)(2,1)} %collective-permute-done.4.refs_1_, bf16[768,4096]{1,0:T(8,128)(2,1)} %get-tuple-element.144.refs_2_, ...), custom_call_target="tpu_custom_call" | custom-call | flops 12884901888 | bytes 50331648 | tf_op jit(solution)/shard_map/ffn_bwd/pallas_call | solution.py:341
  427.8 6.0 ple_both.5
  436.1 27.4 %ffn_bwd.4 = (f32[48,4096]{1,0:T(8,128)}, f32[48,2048]{1,0:T(8,128)}, f32[128,2048]{1,0:T(8,128)}, bf16[128,2048]{1,0:T(8,128)(2,1)}) custom-call(bf16[128,2048]{1,0:T(8,128)(2,1)} %get-tuple-element.152.refs_0_, bf16[128,2048]{1,0:T(8,128)(2,1)} %copy-done.34, bf16[768,4096]{1,0:T(8,128)(2,1)} %get-tuple-element.144.refs_2_, ...), custom_call_target="tpu_custom_call" | custom-call | flops 12884901888 | bytes 50331648 | tf_op jit(solution)/shard_map/ffn_bwd/pallas_call | solution.py:341
  470.7 27.2 %ffn_bwd.5 = (bf16[48,4096]{1,0:T(8,128)(2,1)}, f32[48,2048]{1,0:T(8,128)}, f32[128,2048]{1,0:T(8,128)}, bf16[128,2048]{1,0:T(8,128)(2,1)}) custom-call(bf16[128,2048]{1,0:T(8,128)(2,1)} %get-tuple-element.161.refs_0_, bf16[128,2048]{1,0:T(8,128)(2,1)} %collective-permute-done.9.refs_1_, bf16[768,4096]{1,0:T(8,128)(2,1)} %get-tuple-element.144.refs_2_, ...), custom_call_target="tpu_custom_call" | custom-call | flops 12884901888 | bytes 50331648 | tf_op jit(solution)/shard_map/ffn_bwd/pallas_call | solution.py:341
  505.3 8.0 %collective-permute-done.11.hr_ref = bf16[128,2048]{1,0:T(8,128)(2,1)} collective-permute-done((bf16[128,2048]{1,0:T(8,128)(2,1)}, bf16[128,2048]{1,0:T(8,128)(2,1)}, u32[]{:S(2)}, u32[]{:S(2)}) %collective-permute-start.11) | collective-permute-done | bytes 524320 | tf_op jit(solution)/shard_map/ppermute | solution.py:787
  524.4 7.7 %collective-permute-done.14.refs_5_ = bf16[128,2048]{1,0:T(8,128)(2,1)} collective-permute-done((bf16[128,2048]{1,0:T(8,128)(2,1)}, bf16[128,2048]{1,0:T(8,128)(2,1)}, u32[]{:S(2)}, u32[]{:S(2)}) %collective-permute-start.14) | collective-permute-done | bytes 524320 | tf_op jit(solution)/shard_map/ppermute | solution.py:787
  532.1 27.1 %attention_bwd.1 = (bf16[192,2048]{1,0:T(8,128)(2,1)}, bf16[192,2048]{1,0:T(8,128)(2,1)}, bf16[768,1536]{1,0:T(8,128)(2,1)}, bf16[768,48]{1,0:T(8,128)(2,1)}, bf...) custom-call(s32[1]{0:T(128)} %bitcast.35.turn_ref, bf16[128,2048]{1,0:T(8,128)(2,1)} %get-tuple-element.157.refs_0_, ...), custom_call_target="tpu_custom_call" | custom-call | flops 1048576 | bytes 1048576 | tf_op jit(solution)/shard_map/attention_bwd/pallas_call | solution.py:557
  571.1 6.9 %adapter_sums.1 = (f32[8,16,2,4096]{3,2,1,0:T(2,128)}, f32[8,16,4096]{2,1,0:T(8,128)}) custom-call(s32[16]{0:T(128)} %convert_element_type.138.ids_ref, bf16[16,48,4096]{2,1,0:T(8,128)(2,1)} %bitcast.105), custom_call_target="tpu_custom_call" | custom-call | flops 6291456 | bytes 6291456 | tf_op jit(solution)/shard_map/adapter_sums/pallas_call | solution.py:662
  (225 shorter events, 179.8 us)
Async XLA Ops:
  7.2 153.2 %copy-start = (bf16[8,1024,16]{1,2,0:T(8,128)(2,1)S(1)}, bf16[8,1024,16]{1,2,0:T(8,128)(2,1)}, u32[]{:S(2)}) copy-start(bf16[8,1024,16]{1,2,0:T(8,128)(2,1)} %param.38) | copy-start | bytes 786436
  7.2 108.4 %all-gather.8.cloned.1.call-start = ((), (), s32[]{:S(2)}) async-start(), calls=%async_computation.1 | async-start | bytes 20611072 | tf_op jit(solution)/shard_map/all_gather | solution.py:809
  10.9 235.6 %all-gather.10.cloned.1.call-start = ((), (), s32[]{:S(2)}) async-start(), calls=%async_computation.2 | async-start | bytes 26738688 | tf_op jit(solution)/shard_map/all_gather | solution.py:809
  10.9 49.5 %collective-permute-start = (bf16[384,2048]{1,0:T(8,128)(2,1)}, bf16[384,2048]{1,0:T(8,128)(2,1)}, u32[]{:S(2)}, u32[]{:S(2)}) collective-permute-start(bf16[384,2048]{1,0:T(8,128)(2,1)} %x_ref.3), channel_id=1, source_target_pairs={{0,1},{1,0},{2,3},{3,2},{4,5},{5,4},{6,7},{7,6},{8,9},{9,8},{10,11... | collective-permute-start | bytes 4718600 | tf_op jit(solution)/shard_map/ppermute | solution.py:787
  115.6 231.5 %all-gather.12.cloned.1.call-start = ((), (), s32[]{:S(2)}) async-start(), calls=%async_computation.3 | async-start | bytes 20054016 | tf_op jit(solution)/shard_map/all_gather | solution.py:809
  171.4 36.8 %collective-permute-start.1 = (bf16[384,2048]{1,0:T(8,128)(2,1)}, bf16[384,2048]{1,0:T(8,128)(2,1)}, u32[]{:S(2)}, u32[]{:S(2)}) collective-permute-start(bf16[384,2048]{1,0:T(8,128)(2,1)} %dynamic-slice_convert_fusion), channel_id=1, source_target_pairs={{0,1},{1,0},{2,3},{3,2},{4,5},{5,4},{6,7},{7,6},{8,9},{9,8},{10,11... | collective-permute-start | bytes 4718600 | tf_op jit(solution)/shard_map/ppermute | solution.py:787
  246.6 314.4 %all-gather.16.cloned.1.call-start = ((), (), s32[]{:S(2)}) async-start(), calls=%async_computation.5 | async-start | bytes 6684672 | tf_op jit(solution)/shard_map/all_gather | solution.py:961
  248.2 36.9 %collective-permute-start.2 = (bf16[384,2048]{1,0:T(8,128)(2,1)}, bf16[384,2048]{1,0:T(8,128)(2,1)}, u32[]{:S(2)}, u32[]{:S(2)}) collective-permute-start(bf16[384,2048]{1,0:T(8,128)(2,1)} %get-tuple-element.228), channel_id=1, source_target_pairs={{0,1},{1,0},{2,3},{3,2},{4,5},{5,4},{6,7},{7,6},{8,9},{9,8},{10,11... | collective-permute-start | bytes 4718600 | tf_op jit(solution)/shard_map/ppermute | solution.py:787
  361.3 15.1 %collective-permute-start.3 = (bf16[128,2048]{1,0:T(8,128)(2,1)}, bf16[128,2048]{1,0:T(8,128)(2,1)}, u32[]{:S(2)}, u32[]{:S(2)}) collective-permute-start(bf16[128,2048]{1,0:T(8,128)(2,1)} %get-tuple-element.134), channel_id=1, source_target_pairs={{0,1},{1,0},{2,3},{3,2},{4,5},{5,4},{6,7},{7,6},{8,9},{9,8},{10,11... | collective-permute-start | bytes 1572872 | tf_op jit(solution)/shard_map/ppermute | solution.py:787
  362.7 24.7 %collective-permute-start.6 = (bf16[128,2048]{1,0:T(8,128)(2,1)}, bf16[128,2048]{1,0:T(8,128)(2,1)S(1)}, u32[]{:S(2)}, u32[]{:S(2)}) collective-permute-start(bf16[128,2048]{1,0:T(8,128)(2,1)} %get-tuple-element.139), channel_id=1, source_target_pairs={{0,1},{1,0},{2,3},{3,2},{4,5},{5,4},{6,7},{7,6},{8,9},{9,8},{10,11... | collective-permute-start | bytes 1572872 | tf_op jit(solution)/shard_map/ppermute | solution.py:787
  382.4 16.4 %collective-permute-start.4 = (bf16[128,2048]{1,0:T(8,128)(2,1)}, bf16[128,2048]{1,0:T(8,128)(2,1)}, u32[]{:S(2)}, u32[]{:S(2)}) collective-permute-start(bf16[128,2048]{1,0:T(8,128)(2,1)} %get-tuple-element.136.refs_0_), channel_id=1, source_target_pairs={{0,1},{1,0},{2,3},{3,2},{4,5},{5,4},{6,7},{7,6},{8,9},{9,8},{10,11... | collective-permute-start | bytes 1572872 | tf_op jit(solution)/shard_map/ppermute | solution.py:787
  394.2 41.0 %collective-permute-start.8 = (bf16[128,2048]{1,0:T(8,128)(2,1)}, bf16[128,2048]{1,0:T(8,128)(2,1)S(1)}, u32[]{:S(2)}, u32[]{:S(2)}) collective-permute-start(bf16[128,2048]{1,0:T(8,128)(2,1)} %get-tuple-element.152.refs_0_), channel_id=1, source_target_pairs={{0,1},{1,0},{2,3},{3,2},{4,5},{5,4},{6,7},{7,6},{8,9},{9,8},{10,11... | collective-permute-start | bytes 1572872 | tf_op jit(solution)/shard_map/ppermute | solution.py:787
  398.8 29.0 %collective-permute-start.5 = (bf16[128,2048]{1,0:T(8,128)(2,1)}, bf16[128,2048]{1,0:T(8,128)(2,1)}, u32[]{:S(2)}, u32[]{:S(2)}) collective-permute-start(bf16[128,2048]{1,0:T(8,128)(2,1)} %get-tuple-element.137), channel_id=1, source_target_pairs={{0,1},{1,0},{2,3},{3,2},{4,5},{5,4},{6,7},{7,6},{8,9},{9,8},{10,11... | collective-permute-start | bytes 1572872 | tf_op jit(solution)/shard_map/ppermute | solution.py:787
  427.2 36.9 %collective-permute-start.7 = (bf16[128,2048]{1,0:T(8,128)(2,1)}, bf16[128,2048]{1,0:T(8,128)(2,1)}, u32[]{:S(2)}, u32[]{:S(2)}) collective-permute-start(bf16[128,2048]{1,0:T(8,128)(2,1)} %get-tuple-element.150), channel_id=1, source_target_pairs={{0,1},{1,0},{2,3},{3,2},{4,5},{5,4},{6,7},{7,6},{8,9},{9,8},{10,11... | collective-permute-start | bytes 1572872 | tf_op jit(solution)/shard_map/ppermute | solution.py:787
  433.8 36.9 %collective-permute-start.9 = (bf16[128,2048]{1,0:T(8,128)(2,1)}, bf16[128,2048]{1,0:T(8,128)(2,1)}, u32[]{:S(2)}, u32[]{:S(2)}) collective-permute-start(bf16[128,2048]{1,0:T(8,128)(2,1)} %get-tuple-element.161.refs_0_), channel_id=1, source_target_pairs={{0,1},{1,0},{2,3},{3,2},{4,5},{5,4},{6,7},{7,6},{8,9},{9,8},{10,11... | collective-permute-start | bytes 1572872 | tf_op jit(solution)/shard_map/ppermute | solution.py:787
  463.5 34.5 %collective-permute-start.10 = (bf16[128,2048]{1,0:T(8,128)(2,1)}, bf16[128,2048]{1,0:T(8,128)(2,1)}, u32[]{:S(2)}, u32[]{:S(2)}) collective-permute-start(bf16[128,2048]{1,0:T(8,128)(2,1)} %get-tuple-element.155), channel_id=1, source_target_pairs={{0,1},{1,0},{2,3},{3,2},{4,5},{5,4},{6,7},{7,6},{8,9},{9,8},{10,11... | collective-permute-start | bytes 1572872 | tf_op jit(solution)/shard_map/ppermute | solution.py:787
  469.2 28.7 %collective-permute-start.12 = (bf16[128,2048]{1,0:T(8,128)(2,1)}, bf16[128,2048]{1,0:T(8,128)(2,1)S(1)}, u32[]{:S(2)}, u32[]{:S(2)}) collective-permute-start(bf16[128,2048]{1,0:T(8,128)(2,1)} %get-tuple-element.157.refs_0_), channel_id=1, source_target_pairs={{0,1},{1,0},{2,3},{3,2},{4,5},{5,4},{6,7},{7,6},{8,9},{9,8},{10,11... | collective-permute-start | bytes 1572872 | tf_op jit(solution)/shard_map/ppermute | solution.py:787
  498.0 105.2 %all-gather.14.cloned.1.call-start = ((), (), s32[]{:S(2)}) async-start(), calls=%async_computation.4 | async-start | bytes 1392640 | tf_op jit(solution)/shard_map/all_gather | solution.py:972
  498.0 15.2 %collective-permute-start.11 = (bf16[128,2048]{1,0:T(8,128)(2,1)}, bf16[128,2048]{1,0:T(8,128)(2,1)}, u32[]{:S(2)}, u32[]{:S(2)}) collective-permute-start(bf16[128,2048]{1,0:T(8,128)(2,1)} %get-tuple-element.171), channel_id=1, source_target_pairs={{0,1},{1,0},{2,3},{3,2},{4,5},{5,4},{6,7},{7,6},{8,9},{9,8},{10,11... | collective-permute-start | bytes 1572872 | tf_op jit(solution)/shard_map/ppermute | solution.py:787
  503.8 20.6 %collective-permute-start.13 = (bf16[128,2048]{1,0:T(8,128)(2,1)}, bf16[128,2048]{1,0:T(8,128)(2,1)S(1)}, u32[]{:S(2)}, u32[]{:S(2)}) collective-permute-start(bf16[128,2048]{1,0:T(8,128)(2,1)} %get-tuple-element.168.refs_1_), channel_id=1, source_target_pairs={{0,1},{1,0},{2,3},{3,2},{4,5},{5,4},{6,7},{7,6},{8,9},{9,8},{10,11... | collective-permute-start | bytes 1572872 | tf_op jit(solution)/shard_map/ppermute | solution.py:787
  518.4 13.7 %collective-permute-start.14 = (bf16[128,2048]{1,0:T(8,128)(2,1)}, bf16[128,2048]{1,0:T(8,128)(2,1)}, u32[]{:S(2)}, u32[]{:S(2)}) collective-permute-start(bf16[128,2048]{1,0:T(8,128)(2,1)} %get-tuple-element.174.refs_2_), channel_id=1, source_target_pairs={{0,1},{1,0},{2,3},{3,2},{4,5},{5,4},{6,7},{7,6},{8,9},{9,8},{10,11... | collective-permute-start | bytes 1572872 | tf_op jit(solution)/shard_map/ppermute | solution.py:787
  560.3 29.3 %collective-permute-start.16 = (bf16[192,2048]{1,0:T(8,128)(2,1)}, bf16[192,2048]{1,0:T(8,128)(2,1)}, u32[]{:S(2)}, u32[]{:S(2)}) collective-permute-start(bf16[192,2048]{1,0:T(8,128)(2,1)} %get-tuple-element.211), channel_id=1, source_target_pairs={{0,1},{1,0},{2,3},{3,2},{4,5},{5,4},{6,7},{7,6},{8,9},{9,8},{10,11... | collective-permute-start | bytes 2359304 | tf_op jit(solution)/shard_map/ppermute | solution.py:787
  564.7 21.6 %all-to-all-start = ((bf16[32,64,112]{2,1,0:T(8,128)(2,1)}), bf16[32,64,112]{2,1,0:T(8,128)(2,1)S(1)}, u32[]{:S(2)}, u32[]{:S(2)}) async-start(bf16[32,64,112]{2,1,0:T(8,128)(2,1)} %bitcast.39), calls=%async_computation | async-start | bytes 1048576 | tf_op jit(solution)/shard_map/all_to_all | solution.py:978
  569.3 29.8 %collective-permute-start.15 = (bf16[192,2048]{1,0:T(8,128)(2,1)}, bf16[192,2048]{1,0:T(8,128)(2,1)}, u32[]{:S(2)}, u32[]{:S(2)}) collective-permute-start(bf16[192,2048]{1,0:T(8,128)(2,1)} %get-tuple-element.210), channel_id=1, source_target_pairs={{0,1},{1,0},{2,3},{3,2},{4,5},{5,4},{6,7},{7,6},{8,9},{9,8},{10,11... | collective-permute-start | bytes 2359304 | tf_op jit(solution)/shard_map/ppermute | solution.py:787
  (46 other events, 631.1 us)
Sparse Core Ops, SparseCore 0:
  11.0 104.5 all-gather.7
  117.7 128.7 all-gather.9
  248.1 98.9 all-gather.11
  498.1 60.9 all-gather.15
  561.2 38.4 all-gather.13

commit v5 on v4

--- a/solution.py
+++ b/solution.py
@@ -299,8 +299,8 @@
             if base is not None:
                 up = up + base_in[0 : 2 * RANK, :]
                 down = down + base_in[2 * RANK : 3 * RANK, :]
-            in_out[0 : 2 * RANK, :] = up
-            in_out[2 * RANK : 3 * RANK, :] = down
+            in_out[0 : 2 * RANK, :] = up.astype(grad_type)
+            in_out[2 * RANK : 3 * RANK, :] = down.astype(grad_type)
 
     rows_block = lambda: pl.BlockSpec((r, UB), lambda j: (rb, first + j))
     unit_block = lambda: pl.BlockSpec((RANK, UB), lambda j: (0, first + j))
@@ -334,7 +334,7 @@
     ]
     out_shape = [
         shape((3 * RANK, units), grad_type),
-        shape((3 * RANK, width), F32),
+        shape((3 * RANK, width), grad_type),
         shape((half, width), F32),
         shape((half, width), BF16),
     ]
@@ -971,7 +971,7 @@
     d_raw, d_u, got_ffn = lax.optimization_barrier((d_raw, d_u, got_ffn))
     got_heads = lax.all_gather(send_heads, "dp", axis=0, tiled=False)
     send = jnp.concatenate(
-        [sums[1].astype(BF16), grad_attn_out, dot_tn(d_u, h_all).astype(BF16)], axis=0
+        [sums[1], grad_attn_out, dot_tn(d_u, h_all).astype(BF16)], axis=0
     ).T
     send, d_h_peer_1 = lax.optimization_barrier((send, d_h_peer_1))
     d_h_recv_1 = swap(d_h_peer_1)

time: 622 us -> 621 us (level)
    unnamed x102 -> x104, local copies, waits for them, and re-layouts: 14.2 us -> 14.2 us
  transfers between devices with their start and end apart: 23 -> 23, of which waited for: 12 -> 13; matrix products, arithmetic and copies ran while one was open for 17% -> 17% of each run, Pallas kernels for 36% -> 36%
where the time goes in v5:
time: 621 us; the launch traced here: 612 us
  Pallas kernels  242 us (39%)
  waiting for transfers between devices  177 us (29%)
  matrix products  39.4 us (6%)
  other arithmetic  39 us (6%)
  local copies, waits for them, and re-layouts  38.1 us (6%)
  blocking collectives  34.1 us (5%)
  starting transfers between devices  26.5 us (4%)
  between operations  15.7 us (3%)
    all_gather x3, waiting for transfers between devices, on_device(): gather = lambda v: lax.all_gather(v, 'dp', axis=0, tiled=True)  91.3 us
    ppermute x17, waiting for transfers between devices, swap(): return lax.ppermute(v, 'tensor', [(0, 1), (1, 0)])  85.4 us
    pallas_call x3, Pallas kernels, ffn_bwd(): pl.pallas_call(body, grid=(blocks,), in_specs=in_specs, out_specs=out_spe...  81.5 us
    pallas_call x2, Pallas kernels, ffn_up(): pl.pallas_call(body, grid=(blocks,), in_specs=in_specs, out_specs=[unit_b...  42.8 us
    unnamed x1, blocking collectives  34.1 us
    pallas_call x1, Pallas kernels, attention_bwd(): pl.pallas_call(body, grid=(heads,), in_specs=[pl.BlockSpec(memory_space=p...  27.2 us
    pallas_call x2, Pallas kernels, ffn_down(): pl.pallas_call(body, grid=(width // chunk,), in_specs=[row_const(units),...  24.5 us
    ppermute x17, starting transfers between devices, swap(): return lax.ppermute(v, 'tensor', [(0, 1), (1, 0)])  21.8 us
  transfers between devices with their start and end apart: 23, of which 13 were waited for; matrix products, arithmetic and copies ran while one was open for 17% of the time, Pallas kernels for 36%

profile of v5, /device:TPU:0, one launch (start us, length us, event | category | flops | bytes accessed | tf_op | source)
XLA Modules:
  0.0 611.9 jit_solution(5154935313575050846)
XLA Ops:
  16.0 34.1 %all-reduce = bf16[16]{0:T(256)(128)(2,1)S(1)} all-reduce(bf16[16]{0:T(256)(128)(2,1)S(1)} %dynamic-update-slice), channel_id=2, replica_groups=mesh['dp'=16,'tensor'=2] {'dp'}, use_global_device_ids=true, to_apply=%add | all-reduce | flops 16 | bytes 64
  50.1 5.9 pack_2.1
  65.9 49.7 %all-gather.8.cloned.1.call-done.refs_1_.refs_9_.w_ref.refs_6_.refs_7_ = bf16[2048,4736]{1,0:T(8,128)(2,1)} async-done(((bf16[128,4736]{1,0:T(8,128)(2,1)}), bf16[2048,4736]{1,0:T(8,128)(2,1)}) %all-gather.8.cloned.1.call-update) | async-done | bytes 19398672 | tf_op jit(solution)/shard_map/all_gather | solution.py:809
  120.0 7.3 %fusion.7 = f32[768,1536]{1,0:T(8,128)S(1)} fusion(bf16[768,2048]{1,0:T(8,128)(2,1)S(1)} %fusion.4, bf16[2048,4736]{1,0:T(8,128)(2,1)} %all-gather.8.cloned.1.call-done.refs_1_.refs_9_.w_ref.refs_6_.refs_7_), kind=kOutput, calls=%fused_computation.12 | convolution fusion | flops 4831838208 | bytes 14155776 | tf_op jit(solution)/shard_map/dot_general | solution.py:34
  146.3 6.5 %fusion.62 = (f32[4,768]{1,0:T(4,128)S(1)}, f32[4,768,768]{2,1,0:T(8,128)}) fusion(f32[768,768,4]{0,1,2:T(8,128)S(1)} %fusion.32, pred[768,768]{1,0:T(8,128)(4,1)S(1)} %copy-done.31), kind=kOutput, calls=%fused_computation.133 | output fusion | flops 14156543 | bytes 19476480 | tf_op jit(solution)/shard_map/sub | solution.py:867
  160.7 5.7 fusion.12
  182.0 26.3 %collective-permute-done.1 = bf16[384,2048]{1,0:T(8,128)(2,1)} collective-permute-done((bf16[384,2048]{1,0:T(8,128)(2,1)}, bf16[384,2048]{1,0:T(8,128)(2,1)}, u32[]{:S(2)}, u32[]{:S(2)}) %collective-permute-start.1) | collective-permute-done | bytes 1572896 | tf_op jit(solution)/shard_map/ppermute | solution.py:787
  214.6 32.0 %all-gather.10.cloned.1.call-done.refs_1_.refs_10_ = bf16[2048,6144]{1,0:T(8,128)(2,1)} async-done(((bf16[128,6144]{1,0:T(8,128)(2,1)}), bf16[2048,6144]{1,0:T(8,128)(2,1)}) %all-gather.10.cloned.1.call-update) | async-done | bytes 25165840 | tf_op jit(solution)/shard_map/all_gather | solution.py:809
  261.4 23.6 %collective-permute-done.2 = bf16[384,2048]{1,0:T(8,128)(2,1)} collective-permute-done((bf16[384,2048]{1,0:T(8,128)(2,1)}, bf16[384,2048]{1,0:T(8,128)(2,1)}, u32[]{:S(2)}, u32[]{:S(2)}) %collective-permute-start.2) | collective-permute-done | bytes 1572896 | tf_op jit(solution)/shard_map/ppermute | solution.py:787
  292.9 13.0 %ffn_up.2 = (bf16[768,4096]{1,0:T(8,128)(2,1)}, bf16[768,4096]{1,0:T(8,128)(2,1)}, bf16[768,4096]{1,0:T(8,128)(2,1)}, f32[768,16]{1,0:T(8,128)}) custom-call(bf16[768,2048]{1,0:T(8,128)(2,1)} %copy-done.4, bf16[2048,4736]{1,0:T(8,128)(2,1)} %all-gather.8.cloned.1.call-done.refs_1_.refs_9_.w_ref.refs_6_.refs_7_, bf16[768,32]{1,0:T(8,128)(2,1)} %copy.74.refs_2_, ...), custom_call_target="tpu_custom_call" | custom-call | flops 6442450944 | bytes 8388608 | tf_op jit(solution)/shard_map/ffn_up/pallas_call | solution.py:157
  305.8 29.8 %ffn_up.3 = (bf16[768,4096]{1,0:T(8,128)(2,1)}, bf16[768,4096]{1,0:T(8,128)(2,1)}, bf16[768,4096]{1,0:T(8,128)(2,1)}, f32[768,16]{1,0:T(8,128)}) custom-call(bf16[768,2048]{1,0:T(8,128)(2,1)} %copy-done.4, bf16[2048,6144]{1,0:T(8,128)(2,1)} %all-gather.10.cloned.1.call-done.refs_1_.refs_10_, ...), custom_call_target="tpu_custom_call", output_to_operand_aliasing={{0}: (6, {}), {1}: (7, {}), {2}: (8, {})} | custom-call | flops 19327352832 | bytes 25165824 | tf_op jit(solution)/shard_map/ffn_up/pallas_call | solution.py:157
  337.4 9.7 %all-gather.12.cloned.1.call-done.w_ref.refs_11_ = bf16[2048,4608]{1,0:T(8,128)(2,1)} async-done(((bf16[128,4608]{1,0:T(8,128)(2,1)}), bf16[2048,4608]{1,0:T(8,128)(2,1)}) %all-gather.12.cloned.1.call-update) | async-done | bytes 18874384 | tf_op jit(solution)/shard_map/all_gather | solution.py:809
  347.1 14.2 %ffn_down.2 = (f32[128,2048]{1,0:T(8,128)}, bf16[128,2048]{1,0:T(8,128)(2,1)}, f32[128,2048]{1,0:T(8,128)}, bf16[128,2048]{1,0:T(8,128)(2,1)}) custom-call(bf16[768,4096]{1,0:T(8,128)(2,1)} %get-tuple-element.130.h_ref, bf16[2048,4608]{1,0:T(8,128)(2,1)} %all-gather.12.cloned.1.call-done.w_ref.refs_11_, f32[768,16]{1,0:T(8,128)} %get-tuple-element.124.ud_ref, ...), custom_call_target="tpu_custom_call" | custom-call | flops 8589934592 | bytes 16777216 | tf_op jit(solution)/shard_map/ffn_down/pallas_call | solution.py:190
  363.3 10.3 %ffn_down.3 = (f32[128,2048]{1,0:T(8,128)}, bf16[128,2048]{1,0:T(8,128)(2,1)}) custom-call(bf16[768,4096]{1,0:T(8,128)(2,1)} %get-tuple-element.130.h_ref, bf16[2048,4608]{1,0:T(8,128)(2,1)} %all-gather.12.cloned.1.call-done.w_ref.refs_11_, f32[768,16]{1,0:T(8,128)} %get-tuple-element.124.ud_ref, bf16[16,2048]{1,0:T(8,128)(2,1)} %multiply_bitcast_fusion.bd_ref.refs_6_), custom_call_target="tpu_custom_call" | custom-call | flops 4294967296 | bytes 16777216 | tf_op jit(solution)/shard_map/ffn_down/pallas_call | solution.py:190
  376.3 6.0 ple_both.3
  388.3 6.0 ple_both.4
  400.3 26.9 %ffn_bwd.3 = (f32[48,4096]{1,0:T(8,128)}, f32[48,2048]{1,0:T(8,128)}, f32[128,2048]{1,0:T(8,128)}, bf16[128,2048]{1,0:T(8,128)(2,1)}) custom-call(bf16[128,2048]{1,0:T(8,128)(2,1)} %get-tuple-element.136.refs_0_, bf16[128,2048]{1,0:T(8,128)(2,1)} %collective-permute-done.4.refs_1_, bf16[768,4096]{1,0:T(8,128)(2,1)} %get-tuple-element.144.refs_2_, ...), custom_call_target="tpu_custom_call" | custom-call | flops 12884901888 | bytes 50331648 | tf_op jit(solution)/shard_map/ffn_bwd/pallas_call | solution.py:341
  427.8 5.9 ple_both.5
  436.0 27.4 %ffn_bwd.4 = (f32[48,4096]{1,0:T(8,128)}, f32[48,2048]{1,0:T(8,128)}, f32[128,2048]{1,0:T(8,128)}, bf16[128,2048]{1,0:T(8,128)(2,1)}) custom-call(bf16[128,2048]{1,0:T(8,128)(2,1)} %get-tuple-element.152.refs_0_, bf16[128,2048]{1,0:T(8,128)(2,1)} %copy-done.34, bf16[768,4096]{1,0:T(8,128)(2,1)} %get-tuple-element.144.refs_2_, ...), custom_call_target="tpu_custom_call" | custom-call | flops 12884901888 | bytes 50331648 | tf_op jit(solution)/shard_map/ffn_bwd/pallas_call | solution.py:341
  470.7 27.2 %ffn_bwd.5 = (bf16[48,4096]{1,0:T(8,128)(2,1)}, bf16[48,2048]{1,0:T(8,128)(2,1)}, f32[128,2048]{1,0:T(8,128)}, bf16[128,2048]{1,0:T(8,128)(2,1)}) custom-call(bf16[128,2048]{1,0:T(8,128)(2,1)} %get-tuple-element.161.refs_0_, bf16[128,2048]{1,0:T(8,128)(2,1)} %collective-permute-done.9.refs_1_, bf16[768,4096]{1,0:T(8,128)(2,1)} %get-tuple-element.144.refs_2_, ...), custom_call_target="tpu_custom_call" | custom-call | flops 12884901888 | bytes 50331648 | tf_op jit(solution)/shard_map/ffn_bwd/pallas_call | solution.py:341
  505.2 8.0 %collective-permute-done.11.hr_ref = bf16[128,2048]{1,0:T(8,128)(2,1)} collective-permute-done((bf16[128,2048]{1,0:T(8,128)(2,1)}, bf16[128,2048]{1,0:T(8,128)(2,1)}, u32[]{:S(2)}, u32[]{:S(2)}) %collective-permute-start.11) | collective-permute-done | bytes 524320 | tf_op jit(solution)/shard_map/ppermute | solution.py:787
  524.3 7.7 %collective-permute-done.14.refs_5_ = bf16[128,2048]{1,0:T(8,128)(2,1)} collective-permute-done((bf16[128,2048]{1,0:T(8,128)(2,1)}, bf16[128,2048]{1,0:T(8,128)(2,1)}, u32[]{:S(2)}, u32[]{:S(2)}) %collective-permute-start.14) | collective-permute-done | bytes 524320 | tf_op jit(solution)/shard_map/ppermute | solution.py:787
  532.0 27.2 %attention_bwd.1 = (bf16[192,2048]{1,0:T(8,128)(2,1)}, bf16[192,2048]{1,0:T(8,128)(2,1)}, bf16[768,1536]{1,0:T(8,128)(2,1)}, bf16[768,48]{1,0:T(8,128)(2,1)}, bf...) custom-call(s32[1]{0:T(128)} %bitcast.35.turn_ref, bf16[128,2048]{1,0:T(8,128)(2,1)} %get-tuple-element.157.refs_0_, ...), custom_call_target="tpu_custom_call" | custom-call | flops 1048576 | bytes 1048576 | tf_op jit(solution)/shard_map/attention_bwd/pallas_call | solution.py:557
  570.0 6.9 %adapter_sums.1 = (f32[8,16,2,4096]{3,2,1,0:T(2,128)}, f32[8,16,4096]{2,1,0:T(8,128)}) custom-call(s32[16]{0:T(128)} %convert_element_type.134.ids_ref, bf16[16,48,4096]{2,1,0:T(8,128)(2,1)} %bitcast.105), custom_call_target="tpu_custom_call" | custom-call | flops 6291456 | bytes 6291456 | tf_op jit(solution)/shard_map/adapter_sums/pallas_call | solution.py:662
  (226 shorter events, 179.1 us)
Async XLA Ops:
  7.2 153.2 %copy-start = (bf16[8,1024,16]{1,2,0:T(8,128)(2,1)S(1)}, bf16[8,1024,16]{1,2,0:T(8,128)(2,1)}, u32[]{:S(2)}) copy-start(bf16[8,1024,16]{1,2,0:T(8,128)(2,1)} %param.38) | copy-start | bytes 786436
  7.2 108.4 %all-gather.8.cloned.1.call-start = ((), (), s32[]{:S(2)}) async-start(), calls=%async_computation.1 | async-start | bytes 20611072 | tf_op jit(solution)/shard_map/all_gather | solution.py:809
  10.9 235.6 %all-gather.10.cloned.1.call-start = ((), (), s32[]{:S(2)}) async-start(), calls=%async_computation.2 | async-start | bytes 26738688 | tf_op jit(solution)/shard_map/all_gather | solution.py:809
  10.9 49.5 %collective-permute-start = (bf16[384,2048]{1,0:T(8,128)(2,1)}, bf16[384,2048]{1,0:T(8,128)(2,1)}, u32[]{:S(2)}, u32[]{:S(2)}) collective-permute-start(bf16[384,2048]{1,0:T(8,128)(2,1)} %x_ref.3), channel_id=1, source_target_pairs={{0,1},{1,0},{2,3},{3,2},{4,5},{5,4},{6,7},{7,6},{8,9},{9,8},{10,11... | collective-permute-start | bytes 4718600 | tf_op jit(solution)/shard_map/ppermute | solution.py:787
  115.6 231.5 %all-gather.12.cloned.1.call-start = ((), (), s32[]{:S(2)}) async-start(), calls=%async_computation.3 | async-start | bytes 20054016 | tf_op jit(solution)/shard_map/all_gather | solution.py:809
  171.4 36.8 %collective-permute-start.1 = (bf16[384,2048]{1,0:T(8,128)(2,1)}, bf16[384,2048]{1,0:T(8,128)(2,1)}, u32[]{:S(2)}, u32[]{:S(2)}) collective-permute-start(bf16[384,2048]{1,0:T(8,128)(2,1)} %dynamic-slice_convert_fusion), channel_id=1, source_target_pairs={{0,1},{1,0},{2,3},{3,2},{4,5},{5,4},{6,7},{7,6},{8,9},{9,8},{10,11... | collective-permute-start | bytes 4718600 | tf_op jit(solution)/shard_map/ppermute | solution.py:787
  246.6 313.3 %all-gather.16.cloned.1.call-start = ((), (), s32[]{:S(2)}) async-start(), calls=%async_computation.5 | async-start | bytes 6684672 | tf_op jit(solution)/shard_map/all_gather | solution.py:961
  248.2 36.9 %collective-permute-start.2 = (bf16[384,2048]{1,0:T(8,128)(2,1)}, bf16[384,2048]{1,0:T(8,128)(2,1)}, u32[]{:S(2)}, u32[]{:S(2)}) collective-permute-start(bf16[384,2048]{1,0:T(8,128)(2,1)} %get-tuple-element.228), channel_id=1, source_target_pairs={{0,1},{1,0},{2,3},{3,2},{4,5},{5,4},{6,7},{7,6},{8,9},{9,8},{10,11... | collective-permute-start | bytes 4718600 | tf_op jit(solution)/shard_map/ppermute | solution.py:787
  361.3 15.1 %collective-permute-start.3 = (bf16[128,2048]{1,0:T(8,128)(2,1)}, bf16[128,2048]{1,0:T(8,128)(2,1)}, u32[]{:S(2)}, u32[]{:S(2)}) collective-permute-start(bf16[128,2048]{1,0:T(8,128)(2,1)} %get-tuple-element.134), channel_id=1, source_target_pairs={{0,1},{1,0},{2,3},{3,2},{4,5},{5,4},{6,7},{7,6},{8,9},{9,8},{10,11... | collective-permute-start | bytes 1572872 | tf_op jit(solution)/shard_map/ppermute | solution.py:787
  362.8 24.7 %collective-permute-start.6 = (bf16[128,2048]{1,0:T(8,128)(2,1)}, bf16[128,2048]{1,0:T(8,128)(2,1)S(1)}, u32[]{:S(2)}, u32[]{:S(2)}) collective-permute-start(bf16[128,2048]{1,0:T(8,128)(2,1)} %get-tuple-element.139), channel_id=1, source_target_pairs={{0,1},{1,0},{2,3},{3,2},{4,5},{5,4},{6,7},{7,6},{8,9},{9,8},{10,11... | collective-permute-start | bytes 1572872 | tf_op jit(solution)/shard_map/ppermute | solution.py:787
  382.4 16.5 %collective-permute-start.4 = (bf16[128,2048]{1,0:T(8,128)(2,1)}, bf16[128,2048]{1,0:T(8,128)(2,1)}, u32[]{:S(2)}, u32[]{:S(2)}) collective-permute-start(bf16[128,2048]{1,0:T(8,128)(2,1)} %get-tuple-element.136.refs_0_), channel_id=1, source_target_pairs={{0,1},{1,0},{2,3},{3,2},{4,5},{5,4},{6,7},{7,6},{8,9},{9,8},{10,11... | collective-permute-start | bytes 1572872 | tf_op jit(solution)/shard_map/ppermute | solution.py:787
  394.2 41.0 %collective-permute-start.8 = (bf16[128,2048]{1,0:T(8,128)(2,1)}, bf16[128,2048]{1,0:T(8,128)(2,1)S(1)}, u32[]{:S(2)}, u32[]{:S(2)}) collective-permute-start(bf16[128,2048]{1,0:T(8,128)(2,1)} %get-tuple-element.152.refs_0_), channel_id=1, source_target_pairs={{0,1},{1,0},{2,3},{3,2},{4,5},{5,4},{6,7},{7,6},{8,9},{9,8},{10,11... | collective-permute-start | bytes 1572872 | tf_op jit(solution)/shard_map/ppermute | solution.py:787
  398.8 29.0 %collective-permute-start.5 = (bf16[128,2048]{1,0:T(8,128)(2,1)}, bf16[128,2048]{1,0:T(8,128)(2,1)}, u32[]{:S(2)}, u32[]{:S(2)}) collective-permute-start(bf16[128,2048]{1,0:T(8,128)(2,1)} %get-tuple-element.137), channel_id=1, source_target_pairs={{0,1},{1,0},{2,3},{3,2},{4,5},{5,4},{6,7},{7,6},{8,9},{9,8},{10,11... | collective-permute-start | bytes 1572872 | tf_op jit(solution)/shard_map/ppermute | solution.py:787
  427.2 36.9 %collective-permute-start.7 = (bf16[128,2048]{1,0:T(8,128)(2,1)}, bf16[128,2048]{1,0:T(8,128)(2,1)}, u32[]{:S(2)}, u32[]{:S(2)}) collective-permute-start(bf16[128,2048]{1,0:T(8,128)(2,1)} %get-tuple-element.150), channel_id=1, source_target_pairs={{0,1},{1,0},{2,3},{3,2},{4,5},{5,4},{6,7},{7,6},{8,9},{9,8},{10,11... | collective-permute-start | bytes 1572872 | tf_op jit(solution)/shard_map/ppermute | solution.py:787
  433.8 36.9 %collective-permute-start.9 = (bf16[128,2048]{1,0:T(8,128)(2,1)}, bf16[128,2048]{1,0:T(8,128)(2,1)}, u32[]{:S(2)}, u32[]{:S(2)}) collective-permute-start(bf16[128,2048]{1,0:T(8,128)(2,1)} %get-tuple-element.161.refs_0_), channel_id=1, source_target_pairs={{0,1},{1,0},{2,3},{3,2},{4,5},{5,4},{6,7},{7,6},{8,9},{9,8},{10,11... | collective-permute-start | bytes 1572872 | tf_op jit(solution)/shard_map/ppermute | solution.py:787
  463.4 34.4 %collective-permute-start.10 = (bf16[128,2048]{1,0:T(8,128)(2,1)}, bf16[128,2048]{1,0:T(8,128)(2,1)}, u32[]{:S(2)}, u32[]{:S(2)}) collective-permute-start(bf16[128,2048]{1,0:T(8,128)(2,1)} %get-tuple-element.155), channel_id=1, source_target_pairs={{0,1},{1,0},{2,3},{3,2},{4,5},{5,4},{6,7},{7,6},{8,9},{9,8},{10,11... | collective-permute-start | bytes 1572872 | tf_op jit(solution)/shard_map/ppermute | solution.py:787
  469.2 28.7 %collective-permute-start.12 = (bf16[128,2048]{1,0:T(8,128)(2,1)}, bf16[128,2048]{1,0:T(8,128)(2,1)S(1)}, u32[]{:S(2)}, u32[]{:S(2)}) collective-permute-start(bf16[128,2048]{1,0:T(8,128)(2,1)} %get-tuple-element.157.refs_0_), channel_id=1, source_target_pairs={{0,1},{1,0},{2,3},{3,2},{4,5},{5,4},{6,7},{7,6},{8,9},{9,8},{10,11... | collective-permute-start | bytes 1572872 | tf_op jit(solution)/shard_map/ppermute | solution.py:787
  497.9 104.2 %all-gather.14.cloned.1.call-start = ((), (), s32[]{:S(2)}) async-start(), calls=%async_computation.4 | async-start | bytes 1392640 | tf_op jit(solution)/shard_map/all_gather | solution.py:972
  497.9 15.2 %collective-permute-start.11 = (bf16[128,2048]{1,0:T(8,128)(2,1)}, bf16[128,2048]{1,0:T(8,128)(2,1)}, u32[]{:S(2)}, u32[]{:S(2)}) collective-permute-start(bf16[128,2048]{1,0:T(8,128)(2,1)} %get-tuple-element.171), channel_id=1, source_target_pairs={{0,1},{1,0},{2,3},{3,2},{4,5},{5,4},{6,7},{7,6},{8,9},{9,8},{10,11... | collective-permute-start | bytes 1572872 | tf_op jit(solution)/shard_map/ppermute | solution.py:787
  503.7 20.6 %collective-permute-start.13 = (bf16[128,2048]{1,0:T(8,128)(2,1)}, bf16[128,2048]{1,0:T(8,128)(2,1)S(1)}, u32[]{:S(2)}, u32[]{:S(2)}) collective-permute-start(bf16[128,2048]{1,0:T(8,128)(2,1)} %get-tuple-element.168.refs_1_), channel_id=1, source_target_pairs={{0,1},{1,0},{2,3},{3,2},{4,5},{5,4},{6,7},{7,6},{8,9},{9,8},{10,11... | collective-permute-start | bytes 1572872 | tf_op jit(solution)/shard_map/ppermute | solution.py:787
  518.3 13.6 %collective-permute-start.14 = (bf16[128,2048]{1,0:T(8,128)(2,1)}, bf16[128,2048]{1,0:T(8,128)(2,1)}, u32[]{:S(2)}, u32[]{:S(2)}) collective-permute-start(bf16[128,2048]{1,0:T(8,128)(2,1)} %get-tuple-element.174.refs_2_), channel_id=1, source_target_pairs={{0,1},{1,0},{2,3},{3,2},{4,5},{5,4},{6,7},{7,6},{8,9},{9,8},{10,11... | collective-permute-start | bytes 1572872 | tf_op jit(solution)/shard_map/ppermute | solution.py:787
  559.2 29.5 %collective-permute-start.16 = (bf16[192,2048]{1,0:T(8,128)(2,1)}, bf16[192,2048]{1,0:T(8,128)(2,1)}, u32[]{:S(2)}, u32[]{:S(2)}) collective-permute-start(bf16[192,2048]{1,0:T(8,128)(2,1)} %get-tuple-element.211), channel_id=1, source_target_pairs={{0,1},{1,0},{2,3},{3,2},{4,5},{5,4},{6,7},{7,6},{8,9},{9,8},{10,11... | collective-permute-start | bytes 2359304 | tf_op jit(solution)/shard_map/ppermute | solution.py:787
  563.6 21.8 %all-to-all-start = ((bf16[32,64,112]{2,1,0:T(8,128)(2,1)}), bf16[32,64,112]{2,1,0:T(8,128)(2,1)S(1)}, u32[]{:S(2)}, u32[]{:S(2)}) async-start(bf16[32,64,112]{2,1,0:T(8,128)(2,1)} %bitcast.39), calls=%async_computation | async-start | bytes 1048576 | tf_op jit(solution)/shard_map/all_to_all | solution.py:978
  568.1 29.8 %collective-permute-start.15 = (bf16[192,2048]{1,0:T(8,128)(2,1)}, bf16[192,2048]{1,0:T(8,128)(2,1)}, u32[]{:S(2)}, u32[]{:S(2)}) collective-permute-start(bf16[192,2048]{1,0:T(8,128)(2,1)} %get-tuple-element.210), channel_id=1, source_target_pairs={{0,1},{1,0},{2,3},{3,2},{4,5},{5,4},{6,7},{7,6},{8,9},{9,8},{10,11... | collective-permute-start | bytes 2359304 | tf_op jit(solution)/shard_map/ppermute | solution.py:787
  (47 other events, 633.3 us)
Sparse Core Ops, SparseCore 0:
  11.0 104.5 all-gather.7
  117.7 128.7 all-gather.9
  248.1 98.9 all-gather.11
  498.0 60.9 all-gather.15
  561.1 39.7 all-gather.13
